TPU v7x, 32 devices: a whole 2x2x4 slice. The times are simulated.
32 devices in a mesh: row: 4 (over y, x), col: 8 (over z, core).
Axes of the slice: x: 2, y: 2, z: 4, core: 2. Of those that a mesh axis runs over, the one named last changes fastest.
Arguments:
- student_hidden: bfloat16 [4096, 1920], P(('row', 'col')), may hold values from -6 to 6
- projection: bfloat16 [1920, 768], replicated, may hold values from -0.125 to 0.125
- teacher: bfloat16 [2560, 768], P(('row', 'col')), may hold values from -6 to 6
- block_map: int32 [32, 3, 1024], P(('row', 'col')), may hold values from 0 to 127, as said below
- block_counts: int32 [32, 32], P(('row', 'col')), may hold values from 16 to 32, as said below
- interp_weights: float32 [64], replicated, may hold values from 0.1 to 1
Outputs:
- grad_hidden: bfloat16 [4096, 1920], P(('row', 'col'))
Inputs may be any that keep to these rules, and one draw needn't show every extreme that they name: `block_map`: field 0 is a tubelet of the sending device below 80, field 1 a cell of the receiving device below 128, field 2 a level below 64. Slots to the sending device itself name cells near the tubelet's proportional position; slots to other devices name any of their cells. Dead slots hold values in range. `block_counts`: entry [s, d] counts the live slots from device s to device d, at the start of d's 32 slots; it is at least 16. In every draw some device receives 32 blocks from every device.
All inputs are finite; a program needn't handle non-finite values.
Results may differ from a plain program's by a relative error of at most 0.025.
Values may be sent and summed in bfloat16 or wider, within the bound.
No kernel may reach another device: no remote copies, remote signals or barrier semaphores. Data moves between devices by JAX's collectives and lax.ppermute only.
A program may use at most 64 MiB of HBM per device.

v0:
```python
import jax
import jax.numpy as jnp
from jax import lax
from jax.sharding import PartitionSpec as P

huber_delta = 0.05
norm_eps = 1e-06


def local(student_hidden, projection, teacher, block_map, block_counts, interp_weights):
    slots = block_map.shape[2]
    peers = block_counts.shape[1]
    per_peer = slots // peers
    tokens_dev = student_hidden.shape[0]
    levels = interp_weights.shape[0]
    fields = block_map[0]
    tube_index = fields[0]
    cell_index = fields[1]
    level_index = fields[2]
    matches = level_index[:, None] == jnp.arange(levels, dtype=jnp.int32)[None, :]
    weights = jnp.sum(jnp.where(matches, interp_weights[None, :], 0.0), axis=1)
    live = (jnp.arange(per_peer, dtype=jnp.int32)[None, :] < block_counts[0][:, None]).reshape(
        slots
    )
    scale = weights * live.astype(jnp.float32)
    rows = teacher[tube_index]
    contrib = (rows.astype(jnp.float32) * scale[:, None]).astype(jnp.bfloat16)
    arrived, cells = (
        lax.all_to_all(contrib, ("row", "col"), split_axis=0, concat_axis=0, tiled=True),
        lax.all_to_all(cell_index, ("row", "col"), split_axis=0, concat_axis=0, tiled=True),
    )
    onehot = (cells[None, :] == jnp.arange(tokens_dev, dtype=jnp.int32)[:, None]).astype(
        jnp.bfloat16
    )
    target = jnp.dot(onehot, arrived, preferred_element_type=jnp.float32)
    teacher_unit = (
        target * lax.rsqrt(jnp.sum(target * target, axis=1, keepdims=True) + norm_eps)
    ).astype(jnp.bfloat16)
    proj = jnp.dot(student_hidden, projection, preferred_element_type=jnp.float32)
    inverse = lax.rsqrt(jnp.sum(proj * proj, axis=1, keepdims=True) + norm_eps)
    unit = proj * inverse
    student_unit = unit.astype(jnp.bfloat16)
    row_student, row_teacher = (
        lax.all_gather(student_unit, "col", axis=0, tiled=True),
        lax.all_gather(teacher_unit, "col", axis=0, tiled=True),
    )
    column_student, column_teacher = (
        lax.all_gather(student_unit, "row", axis=0, tiled=True),
        lax.all_gather(teacher_unit, "row", axis=0, tiled=True),
    )
    contract = (((1,), (1,)), ((), ()))
    gram_s = lax.dot_general(
        row_student, column_student, contract, preferred_element_type=jnp.float32
    )
    gram_t = lax.dot_general(
        row_teacher, column_teacher, contract, preferred_element_type=jnp.float32
    )
    slope = jnp.clip((gram_s - gram_t) / huber_delta, -1.0, 1.0).astype(jnp.bfloat16)
    grad_unit = 2.0 * lax.psum_scatter(
        lax.dot_general(
            slope, row_student, (((0,), (0,)), ((), ())), preferred_element_type=jnp.float32
        ).astype(jnp.bfloat16),
        "row",
        scatter_dimension=0,
        tiled=True,
    ).astype(jnp.float32)
    along = jnp.sum(unit * grad_unit, axis=1, keepdims=True)
    grad_proj = ((grad_unit - unit * along) * inverse).astype(jnp.bfloat16)
    grad_hidden = lax.dot_general(
        grad_proj, projection, contract, preferred_element_type=jnp.float32
    )
    return grad_hidden.astype(jnp.bfloat16)


def solution(mesh):
    in_specs = (
        P(("row", "col"), None),
        P(),
        P(("row", "col"), None),
        P(("row", "col"), None, None),
        P(("row", "col"), None),
        P(),
    )
    out_specs = P(("row", "col"), None)
    return jax.shard_map(local, mesh=mesh, in_specs=in_specs, out_specs=out_specs, check_vma=False)
```

profile of v0, /device:TPU:0, one launch (start us, length us, event | category | flops | bytes accessed | tf_op | source)
XLA Modules:
  0.0 154.5 jit_solution(6741319789277700004)
XLA Ops:
  6.5 0.0 copy-start
  6.5 0.0 copy-start.1
  6.5 0.9 slice_reduce_fusion
  7.4 0.7 all_to_all.12
  8.1 7.3 %all-to-all-start = ((s32[32,32,1]{1,2,0:T(1,128)}), s32[32,32,1]{1,2,0:T(1,128)S(1)}, u32[]{:S(2)}, u32[]{:S(2)}) async-start(s32[32,32,1]{1,2,0:T(1,128)} %all_to_all.12), calls=%async_computation | async-start | bytes 32768 | tf_op jit(solution)/shard_map/all_to_all | solution.py:30
  15.4 0.7 compare_select_fusion
  16.1 0.8 select_reduce_fusion
  16.9 0.1 reduce_sum.40
  17.0 0.7 fusion.6
  17.7 0.0 copy-done.1
  17.7 5.2 %gather_fusion = bf16[1024,768]{1,0:T(8,128)(2,1)} fusion(bf16[80,768]{1,0:T(8,128)(2,1)S(1)} %copy-done.1, s32[1024]{0:T(1024)S(1)} %broadcast_clamp_fusion), kind=kCustom, calls=%fused_computation | custom fusion | bytes 3149824 | tf_op jit(solution)/shard_map/gather | solution.py:26
  23.0 2.9 %fusion = bf16[32,32,768]{2,1,0:T(8,128)(2,1)} fusion(bf16[32,32,768]{2,1,0:T(8,128)(2,1)} %bitcast.18, f32[32,32]{1,0:T(8,128)S(1)} %fusion.6), kind=kLoop, calls=%fused_computation.2 | loop fusion | flops 2359296 | bytes 3149824 | tf_op jit(solution)/shard_map/convert_element_type | solution.py:27
  25.9 0.0 all-to-all-done
  25.9 0.0 copy-start.4
  25.9 0.6 copy-done.4
  26.5 5.9 %all-to-all-start.1 = ((bf16[32,32,768]{2,1,0:T(8,128)(2,1)}), bf16[32,32,768]{2,1,0:T(8,128)(2,1)}, u32[]{:S(2)}, u32[]{:S(2)}) async-start(bf16[32,32,768]{2,1,0:T(8,128)(2,1)} %fusion), calls=%async_computation.1 | async-start | bytes 3145728 | tf_op jit(solution)/shard_map/all_to_all | solution.py:29
  32.4 0.0 all-gather.3.cloned.1.call-start
  32.5 0.0 copy-done
  32.5 1.7 %multiply_reduce_fusion.2 = (f32[128]{0:T(128)S(1)}, f32[128,768]{1,0:T(8,128)S(1)}) fusion(bf16[128,1920]{1,0:T(8,128)(2,1)} %param.6, bf16[1920,768]{1,0:T(8,128)(2,1)S(1)} %copy-done), kind=kOutput, calls=%fused_computation.13 | convolution fusion | flops 377683840 | bytes 3834368 | tf_op jit(solution)/shard_map/dot_general | solution.py:39
  34.2 0.0 copy-start.5
  34.2 0.5 copy-done.5
  34.7 0.8 multiply_convert_fusion.2
  35.5 0.0 copy-start.2
  35.5 0.0 all-gather.3.cloned.1.call-update
  35.5 0.0 all-gather.5.cloned.1.call-start
  35.6 0.5 broadcast.56
  36.0 1.3 reduce.7
  37.3 0.7 eq.30
  38.0 45.8 %all-to-all-done.1 = bf16[32,32,768]{2,1,0:T(8,128)(2,1)} async-done(((bf16[32,32,768]{2,1,0:T(8,128)(2,1)}), bf16[32,32,768]{2,1,0:T(8,128)(2,1)}, u32[]{:S(2)}, u32[]{:S(2)}) %all-to-all-start.1) | async-done | bytes 1572896 | tf_op jit(solution)/shard_map/all_to_all | solution.py:29
  83.8 1.9 %multiply_reduce_fusion.1 = (f32[128]{0:T(128)S(1)}, f32[128,768]{1,0:T(8,128)S(1)}) fusion(bf16[1024,768]{1,0:T(8,128)(2,1)} %bitcast.5, s32[1024]{0:T(1024)} %eq.30), kind=kOutput, calls=%fused_computation.12 | convolution fusion | flops 201654144 | bytes 1970688 | tf_op jit(solution)/shard_map/dot_general | solution.py:35
  85.7 0.8 multiply_convert_fusion.1
  86.5 0.0 all-gather.5.cloned.1.call-update
  86.5 0.0 reduce-scatter.2.cloned.1.call-start
  86.6 0.0 copy-done.2
  86.6 12.2 %all_gather.13 = bf16[512,768]{1,0:T(8,128)(2,1)} all-gather(bf16[128,768]{1,0:T(8,128)(2,1)S(1)} %copy-done.2), channel_id=1, replica_groups=mesh['row'=4,'col'=8] {'row'}, dimensions={0}, use_global_device_ids=true | all-gather | bytes 983040 | tf_op jit(solution)/shard_map/all_gather | solution.py:48
  98.8 0.0 copy-start.3
  98.8 0.0 all-gather.3.cloned.1.call-done
  98.8 4.0 %fusion.11 = f32[1024,512]{1,0:T(8,128)} fusion(bf16[1024,768]{1,0:T(8,128)(2,1)} %all-gather.3.cloned.1.call-done, bf16[512,768]{1,0:T(8,128)(2,1)} %all_gather.13), kind=kOutput, calls=%fused_computation.32 | convolution fusion | flops 805306368 | bytes 4456448 | tf_op jit(solution)/shard_map/dot_general | solution.py:52
  102.8 0.0 copy-done.3
  102.8 10.9 %all_gather.15 = bf16[512,768]{1,0:T(8,128)(2,1)} all-gather(bf16[128,768]{1,0:T(8,128)(2,1)S(1)} %copy-done.3), channel_id=1, replica_groups=mesh['row'=4,'col'=8] {'row'}, dimensions={0}, use_global_device_ids=true | all-gather | bytes 983040 | tf_op jit(solution)/shard_map/all_gather | solution.py:49
  113.7 0.0 copy-start.6
  113.7 0.0 all-gather.5.cloned.1.call-done
  113.7 5.9 %convolution_convert_fusion.1 = bf16[512,768]{1,0:T(8,128)(2,1)} fusion(bf16[1024,768]{1,0:T(8,128)(2,1)} %all-gather.3.cloned.1.call-done, f32[1024,512]{1,0:T(8,128)} %fusion.11, bf16[1024,768]{1,0:T(8,128)(2,1)} %all-gather.5.cloned.1.call-done, bf16[512,768]{1,0:T(8,128)(2,1)} %all_gather.15), kind=kOutput, calls=%fused_computation.5 | convolution fusion | flops 1613103104 | bytes 6815744 | tf_op jit(solution)/shard_map/dot_general | solution.py:60
  119.7 0.0 reduce-scatter.2.cloned.1.call-update
  119.7 24.3 %reduce-scatter.2.cloned.1.call-done = bf16[128,768]{1,0:T(8,128)(2,1)} async-done(((bf16[512,768]{1,0:T(8,128)(2,1)}), bf16[128,768]{1,0:T(8,128)(2,1)}) %reduce-scatter.2.cloned.1.call-update) | async-done | bytes 196624 | tf_op jit(solution)/shard_map/reduce_scatter | solution.py:59
  144.0 0.0 copy-done.6
  144.0 1.1 multiply_reduce_fusion
  145.2 2.8 %convolution_convert_fusion = bf16[128,1920]{1,0:T(8,128)(2,1)} fusion(bf16[1920,768]{1,0:T(8,128)(2,1)S(1)} %copy-done, bf16[128,768]{1,0:T(8,128)(2,1)} %reduce-scatter.2.cloned.1.call-done, f32[128,768]{1,0:T(8,128)S(1)} %get-tuple-element.8, f32[128]{0:T(128)S(1)} %multiply_reduce_fusion, f32[128]{0:T(128)S(1)} %copy-done.6), kind=kOutput, calls=%fused_computation.3 | convolution fusion | flops 378421248 | bytes 4031488 | tf_op jit(solution)/shard_map/dot_general | solution.py:69
  (3 shorter events, 0.0 us)
Async XLA Ops:
  6.5 25.9 %copy-start = (bf16[1920,768]{1,0:T(8,128)(2,1)S(1)}, bf16[1920,768]{1,0:T(8,128)(2,1)}, u32[]{:S(2)}) copy-start(bf16[1920,768]{1,0:T(8,128)(2,1)} %param.7) | copy-start | bytes 8847364
  6.5 11.2 %copy-start.1 = (bf16[80,768]{1,0:T(8,128)(2,1)S(1)}, bf16[80,768]{1,0:T(8,128)(2,1)}, u32[]{:S(2)}) copy-start(bf16[80,768]{1,0:T(8,128)(2,1)} %param.8) | copy-start | bytes 368644
  8.1 17.8 %all-to-all-start = ((s32[32,32,1]{1,2,0:T(1,128)}), s32[32,32,1]{1,2,0:T(1,128)S(1)}, u32[]{:S(2)}, u32[]{:S(2)}) async-start(s32[32,32,1]{1,2,0:T(1,128)} %all_to_all.12), calls=%async_computation | async-start | bytes 32768 | tf_op jit(solution)/shard_map/all_to_all | solution.py:30
  25.9 0.6 copy-start.4
  26.5 57.3 %all-to-all-start.1 = ((bf16[32,32,768]{2,1,0:T(8,128)(2,1)}), bf16[32,32,768]{2,1,0:T(8,128)(2,1)}, u32[]{:S(2)}, u32[]{:S(2)}) async-start(bf16[32,32,768]{2,1,0:T(8,128)(2,1)} %fusion), calls=%async_computation.1 | async-start | bytes 3145728 | tf_op jit(solution)/shard_map/all_to_all | solution.py:29
  32.4 66.4 %all-gather.3.cloned.1.call-start = ((), (), s32[]{:S(2)}) async-start(), calls=%async_computation.3 | async-start | bytes 1769472 | tf_op jit(solution)/shard_map/all_gather | solution.py:44
  34.2 0.5 copy-start.5
  35.5 51.1 %copy-start.2 = (bf16[128,768]{1,0:T(8,128)(2,1)S(1)}, bf16[128,768]{1,0:T(8,128)(2,1)}, u32[]{:S(2)}) copy-start(bf16[128,768]{1,0:T(8,128)(2,1)} %multiply_convert_fusion.2) | copy-start | bytes 589828
  35.5 78.2 %all-gather.5.cloned.1.call-start = ((), (), s32[]{:S(2)}) async-start(), calls=%async_computation.4 | async-start | bytes 1769472 | tf_op jit(solution)/shard_map/all_gather | solution.py:45
  86.5 57.5 %reduce-scatter.2.cloned.1.call-start = ((), (), s32[]{:S(2)}) async-start(), calls=%async_computation.5 | async-start | bytes 983040 | tf_op jit(solution)/shard_map/reduce_scatter | solution.py:59
  98.8 4.1 %copy-start.3 = (bf16[128,768]{1,0:T(8,128)(2,1)S(1)}, bf16[128,768]{1,0:T(8,128)(2,1)}, u32[]{:S(2)}) copy-start(bf16[128,768]{1,0:T(8,128)(2,1)} %multiply_convert_fusion.1) | copy-start | bytes 589828
  113.7 30.3 %copy-start.6 = (f32[128]{0:T(128)S(1)}, f32[128]{0:T(128)}, u32[]{:S(2)}) copy-start(f32[128]{0:T(128)} %copy-done.5) | copy-start | bytes 1540
Sparse Core Ops, SparseCore 0:
  35.6 42.9 all-gather.2
  86.6 22.9 all-gather.4
  119.8 24.1 reduce-scatter.1
where the time goes:
time: 155 us; the launch traced here: 154 us
  waiting for transfers between devices  70.2 us (45%)
  blocking collectives  23.1 us (15%)
  matrix products  16.3 us (11%)
  starting transfers between devices  13.4 us (9%)
  between operations  13.2 us (9%)
  local copies, waits for them, and re-layouts  9.16 us (6%)
  other arithmetic  9.1 us (6%)
    all_to_all x1, waiting for transfers between devices, local(): lax.all_to_all(contrib, ('row', 'col'), split_axis=0, concat_axis=0, tile...  45.8 us
    reduce_scatter x1, waiting for transfers between devices, local(): lax.psum_scatter(lax.dot_general(slope, row_student, (((0,), (0,)), ((),...  24.3 us
    all_gather x1, blocking collectives, local(): lax.all_gather(student_unit, 'row', axis=0, tiled=True)  12.2 us
    all_gather x1, blocking collectives, local(): lax.all_gather(teacher_unit, 'row', axis=0, tiled=True)  10.9 us
    all_to_all x1, starting transfers between devices, local(): lax.all_to_all(cell_index, ('row', 'col'), split_axis=0, concat_axis=0, t...  7.33 us
    all_to_all x1, starting transfers between devices, local(): lax.all_to_all(contrib, ('row', 'col'), split_axis=0, concat_axis=0, tile...  5.95 us
    dot_general x1, matrix products, local(): lax.dot_general(slope, row_student, (((0,), (0,)), ((), ())), preferred_e...  5.93 us
    gather x1, local copies, waits for them, and re-layouts, local(): rows = teacher[tube_index]  5.24 us
  transfers between devices with their start and end apart: 5, of which 2 were waited for; matrix products, arithmetic and copies ran while one was open for 14% of the time, Pallas kernels for 0%

commit v1 on v0

v1 whole, which is shorter than its diff:
```python
import functools

import jax
import jax.numpy as jnp
from jax import lax
from jax.experimental import pallas as pl
from jax.experimental.pallas import tpu as pltpu
from jax.sharding import PartitionSpec as P

huber_delta = 0.05
norm_eps = 1e-06
CORES = 2
LANES = 128
F32 = jnp.float32
BF16 = jnp.bfloat16
VMEM = pl.BlockSpec(memory_space=pltpu.VMEM)
SMEM = pl.BlockSpec(memory_space=pltpu.SMEM)
HBM = pl.BlockSpec(memory_space=pltpu.HBM)
NT = (((1,), (1,)), ((), ()))


def round_up(value, unit):
    return -(-value // unit) * unit


def params(mib):
    return pltpu.CompilerParams(vmem_limit_bytes=mib * 1024 * 1024)


def prepare_kernel(
    per_peer,
    counts_hbm,
    table_hbm,
    map_hbm,
    teacher_hbm,
    hidden_hbm,
    projection_hbm,
    out_ref,
    unit_ref,
    inverse_ref,
    student_ref,
    counts,
    table,
    fields,
    teacher,
    hidden,
    projection,
    sems,
):
    copies = [
        pltpu.make_async_copy(source, target, sems.at[i])
        for i, (source, target) in enumerate(
            (
                (counts_hbm, counts),
                (table_hbm, table),
                (map_hbm, fields),
                (teacher_hbm, teacher),
                (hidden_hbm, hidden),
                (projection_hbm, projection),
            )
        )
    ]
    for copy in copies:
        copy.start()
    for copy in copies[:4]:
        copy.wait()
    tubes = teacher.shape[0]
    rows = fields.shape[0] // 3
    out_ref[0:tubes, :] = teacher[...]
    tube, cell, level = (fields[f * rows : (f + 1) * rows, :] for f in range(3))
    weight = jnp.zeros((rows, LANES), F32)
    for i in range(table.shape[0]):
        weight = jnp.where(level == i, table[i], weight)
    row = lax.broadcasted_iota(jnp.int32, (rows, LANES), 0)
    lane = lax.broadcasted_iota(jnp.int32, (rows, LANES), 1)
    receiver = row * (LANES // per_peer) + lane // per_peer
    count = jnp.zeros((rows, LANES), jnp.int32)
    for i in range(counts.shape[0]):
        count = jnp.where(receiver == i, counts[i], count)
    weight = jnp.where(lane % per_peer < count, weight, 0.0)
    block = jnp.concatenate([tube.astype(F32), cell.astype(F32), weight], axis=1)
    out_ref[tubes:, 0 : 3 * LANES] = block.astype(BF16)
    out_ref[tubes:, 3 * LANES :] = jnp.zeros((rows, out_ref.shape[1] - 3 * LANES), BF16)
    for copy in copies[4:]:
        copy.wait()
    proj = jnp.dot(hidden[...], projection[...], preferred_element_type=F32)
    inverse = lax.rsqrt(jnp.sum(proj * proj, axis=1, keepdims=True) + norm_eps)
    unit = proj * inverse
    unit_ref[...] = unit
    inverse_ref[...] = jnp.broadcast_to(inverse, inverse_ref.shape)
    student_ref[...] = unit.astype(BF16)


def prepare(hidden, projection, teacher, block_map, block_counts, interp_weights):
    tubes, width = teacher.shape
    tokens = hidden.shape[0]
    slots = block_map.shape[2]
    peers = block_counts.shape[1]
    rows = slots // LANES
    return pl.pallas_call(
        functools.partial(prepare_kernel, slots // peers),
        out_shape=(
            jax.ShapeDtypeStruct((tubes + rows, width), BF16),
            jax.ShapeDtypeStruct((tokens, width), F32),
            jax.ShapeDtypeStruct((tokens, LANES), F32),
            jax.ShapeDtypeStruct((tokens, width), BF16),
        ),
        in_specs=[HBM] * 6,
        out_specs=(VMEM,) * 4,
        scratch_shapes=[
            pltpu.SMEM((peers,), jnp.int32),
            pltpu.SMEM(interp_weights.shape, F32),
            pltpu.VMEM((3 * rows, LANES), jnp.int32),
            pltpu.VMEM(teacher.shape, BF16),
            pltpu.VMEM(hidden.shape, BF16),
            pltpu.VMEM(projection.shape, BF16),
            pltpu.SemaphoreType.DMA((6,)),
        ],
    )(
        block_counts.reshape(peers),
        interp_weights,
        block_map.reshape(3 * rows, LANES),
        teacher,
        hidden,
        projection,
    )


def pick(slots, window, per_peer, masks):
    shift = (LANES - window * per_peer) % LANES
    lane = lax.broadcasted_iota(jnp.int32, (slots.shape[0], LANES), 1)
    fields = []
    for f in range(3):
        part = pltpu.roll(slots[:, f * LANES : (f + 1) * LANES], shift, 1)
        part = jnp.where(lane < per_peer, part, 0.0)
        step = per_peer
        while step < LANES:
            part = part + pltpu.roll(part, step, 1)
            step *= 2
        fields.append(part)
    return [
        [jnp.sum(jnp.where(mask, part, 0.0), axis=0, keepdims=True) for part in fields]
        for mask in masks
    ]


def target_kernel(tubes, per_peer, tokens, n_held, first, n_last, dests_ref, *refs):
    held = refs[:n_held]
    outs = refs[n_held + (0 if first else 1) : -3]
    teacher, table, matrix = refs[-3:]
    group = LANES // per_peer
    depth = round_up(group * tubes, LANES)
    rows = tubes + table.shape[1]
    count = matrix.shape[0] // tokens
    groups = matrix.shape[1] // depth
    s = 0
    for h in held:
        for at in range(0, h.shape[0], rows):
            base = s // group * depth + s % group * tubes
            teacher[base : base + tubes, :] = h[at : at + tubes, :]
            slots = h[at + tubes : at + rows, 0 : 3 * LANES].astype(F32)
            for q in range(rows - tubes):
                table[s // 8, q, s % 8 : s % 8 + 1, :] = slots[q : q + 1, :]
            s += 1
    pad = depth - group * tubes
    if pad:
        for g in range(groups):
            teacher[(g + 1) * depth - pad : (g + 1) * depth, :] = jnp.zeros(
                (pad, teacher.shape[1]), BF16
            )
    sender = lax.broadcasted_iota(jnp.int32, (8, LANES), 0)
    lane = lax.broadcasted_iota(jnp.int32, (8, LANES), 1)
    masks = [sender == lane // per_peer + at for at in range(0, 8, group)]
    offset = (lax.broadcasted_iota(jnp.int32, (1, LANES), 1) // per_peer * tubes).astype(F32)
    cells = lax.broadcasted_iota(jnp.int32, (tokens, LANES), 0).astype(F32)
    places = lax.broadcasted_iota(jnp.int32, (depth, LANES), 0).astype(F32)
    for i in range(count):
        dest = dests_ref[i]
        picked = []
        for e in range(table.shape[0]):
            picked += pick(table[e, dest // group], dest % group, per_peer, masks)
        for g in range(groups):
            tube, cell, weight = picked[g]
            left = jnp.where(cells == cell, 1.0, 0.0).astype(BF16)
            right = jnp.where(places == tube + offset, weight, 0.0).astype(BF16)
            block = lax.dot_general(left, right, NT, preferred_element_type=F32)
            matrix[i * tokens : (i + 1) * tokens, g * depth : (g + 1) * depth] = block.astype(BF16)
    total = jnp.dot(matrix[...], teacher[...], preferred_element_type=F32)
    if not first:
        total = total + refs[n_held][...]
    if n_last is None:
        outs[0][...] = total
        return
    total = total * lax.rsqrt(jnp.sum(total * total, axis=1, keepdims=True) + norm_eps)
    outs[0][...] = total[0:n_last, :].astype(BF16)
    outs[1][...] = total[n_last:, :].astype(BF16)


def add_targets(total, held, dests, tubes, per_peer, tokens, rows, n_last):
    width = held[0].shape[1]
    group = LANES // per_peer
    senders = sum(h.shape[0] for h in held) // rows
    groups = senders // group
    depth = round_up(group * tubes, LANES)
    count = dests.shape[0]
    first = total is None
    extra = () if first else (total,)
    if n_last is None:
        out_shape = jax.ShapeDtypeStruct((count * tokens, width), F32)
        out_specs = VMEM
    else:
        out_shape = tuple(
            jax.ShapeDtypeStruct((n, width), BF16) for n in (n_last, count * tokens - n_last)
        )
        out_specs = (VMEM, VMEM)
    return pl.pallas_call(
        functools.partial(target_kernel, tubes, per_peer, tokens, len(held), first, n_last),
        out_shape=out_shape,
        in_specs=[SMEM] + [VMEM] * (len(held) + len(extra)),
        out_specs=out_specs,
        scratch_shapes=[
            pltpu.VMEM((groups * depth, width), BF16),
            pltpu.VMEM((-(-senders // 8), rows - tubes, 8, 3 * LANES), F32),
            pltpu.VMEM((count * tokens, groups * depth), BF16),
        ],
        input_output_aliases={} if first or n_last else {1 + len(held): 0},
        compiler_params=params(40),
    )(dests, *held, *extra)


def relation_kernel(n_rows, n_columns, last, *refs):
    students = refs[:n_rows]
    columns = refs[n_rows : n_rows + n_columns]
    teacher_ref, own_ref, column_ref = refs[n_rows + n_columns : n_rows + n_columns + 3]
    rest = refs[n_rows + n_columns + 3 : -3]
    student, column_s, column_t = refs[-3:]
    tokens = students[0].shape[0]
    for i, block in enumerate(students):
        student[i * tokens : (i + 1) * tokens, :] = block[...]
    at = 0
    for block in columns:
        column_s[at : at + block.shape[0], :] = block[...]
        at += block.shape[0]
    column_t[0:tokens, :] = own_ref[0:tokens, :]
    column_t[tokens:, :] = column_ref[...]
    gram_s = lax.dot_general(column_s[...], student[...], NT, preferred_element_type=F32)
    gram_t = lax.dot_general(column_t[...], teacher_ref[...], NT, preferred_element_type=F32)
    slope = jnp.clip((gram_s - gram_t) / huber_delta, -1.0, 1.0).astype(BF16)
    grad = jnp.dot(slope, student[...], preferred_element_type=F32)
    if not last:
        rest[0][...] = grad
        return
    grad = grad + rest[0][...]
    rest[1][...] = grad[0:tokens, :]
    for j, out in enumerate(rest[2:]):
        out[...] = grad[(j + 1) * tokens : (j + 2) * tokens, :].astype(BF16)


def relate(students, columns, teacher, own, column_teacher, partial):
    tokens, width = students[0].shape
    total = sum(c.shape[0] for c in columns)
    n_col = total // tokens
    last = partial is not None
    if last:
        out_shape = (jax.ShapeDtypeStruct((tokens, width), F32),) + (
            jax.ShapeDtypeStruct((tokens, width), BF16),
        ) * (n_col - 1)
        out_specs = (VMEM,) * n_col
        extra = (partial,)
    else:
        out_shape = jax.ShapeDtypeStruct((total, width), F32)
        out_specs = VMEM
        extra = ()
    return pl.pallas_call(
        functools.partial(relation_kernel, len(students), len(columns), last),
        out_shape=out_shape,
        in_specs=[VMEM] * (len(students) + len(columns) + 3 + len(extra)),
        out_specs=out_specs,
        scratch_shapes=[
            pltpu.VMEM((len(students) * tokens, width), BF16),
            pltpu.VMEM((total, width), BF16),
            pltpu.VMEM((total, width), BF16),
        ],
        compiler_params=params(40),
    )(*students, *columns, teacher, own, column_teacher, *extra)


def finish_kernel(unit_ref, inverse_ref, projection_ref, own_ref, *refs):
    grad = own_ref[...]
    for other in refs[:-1]:
        grad = grad + other[...].astype(F32)
    grad = 2.0 * grad
    unit = unit_ref[...]
    along = jnp.sum(unit * grad, axis=1, keepdims=True)
    grad_proj = ((grad - unit * along) * inverse_ref[:, 0:1]).astype(BF16)
    refs[-1][...] = lax.dot_general(
        grad_proj, projection_ref[...], NT, preferred_element_type=F32
    ).astype(BF16)


def finish(unit, inverse, projection, own, others):
    return pl.pallas_call(
        finish_kernel,
        out_shape=jax.ShapeDtypeStruct((unit.shape[0], projection.shape[0]), BF16),
        in_specs=[VMEM] * (4 + len(others)),
        out_specs=VMEM,
        compiler_params=params(16),
    )(unit, inverse, projection, own, *others)


def doubled(x, exchange, steps):
    held, offsets = [x], [0]
    for step in steps:
        if len(held) > 1:
            held = [jnp.concatenate(held, axis=0)]
        held.append(exchange(held[0], step))
        offsets += [o ^ step for o in offsets]
    return held, offsets


def local(n_row, n_col, student_hidden, projection, teacher, block_map, block_counts, interp_weights):
    tubes = teacher.shape[0]
    tokens = student_hidden.shape[0]
    per_peer = block_map.shape[2] // block_counts.shape[1]
    n_z = n_col // CORES
    row, col = lax.axis_index("row"), lax.axis_index("col")
    steps = [1 << b for b in range(n_row.bit_length() - 1)]

    def along_row(x, k):
        return lax.ppermute(x, "row", [(i, i ^ k) for i in range(n_row)])

    def along_col(x, k):
        return lax.ppermute(x, "col", [(i, i ^ k) for i in range(n_col)])

    payload, unit, inverse, student = prepare(
        student_hidden, projection, teacher, block_map, block_counts, interp_weights
    )
    planes = [payload] + [along_col(payload, CORES * k) for k in range(1, n_z)]
    columns, offsets = doubled(student, along_row, steps[::-1])
    dests = jnp.stack(
        [row * n_col + (col ^ (CORES * k)) for k in range(n_z)]
        + [(row ^ o) * n_col + col for o in offsets[1:]]
    ).astype(jnp.int32)
    total = None
    for k, plane in enumerate(planes):
        held, _ = doubled(plane, along_row, steps[::-1] if k == n_z - 1 else steps)
        held = held + [along_col(x, 1) for x in held]
        n_last = n_z * tokens if k == n_z - 1 else None
        total = add_targets(total, held, dests, tubes, per_peer, tokens, payload.shape[0], n_last)
    own, column = total
    partner = along_col(own, 1)
    rows = [student] + [along_col(student, CORES * k) for k in range(1, n_z)]
    partner_rows = [along_col(x, 1) for x in rows]
    grad = relate(rows, columns, own, own, column, None)
    mine, *others = relate(partner_rows, columns, partner, own, column, grad)
    arrived = [along_row(x, o) for x, o in zip(others, offsets[1:])]
    return finish(unit, inverse, projection, mine, arrived)


def solution(mesh):
    in_specs = (
        P(("row", "col"), None),
        P(),
        P(("row", "col"), None),
        P(("row", "col"), None, None),
        P(("row", "col"), None),
        P(),
    )
    out_specs = P(("row", "col"), None)
    body = functools.partial(local, mesh.shape["row"], mesh.shape["col"])
    return jax.shard_map(body, mesh=mesh, in_specs=in_specs, out_specs=out_specs, check_vma=False)
```

time: 155 us -> 92.4 us (0.60)
  waiting for transfers between devices: 70.2 us -> 39.8 us
  blocking collectives: 23.1 us -> 0 us
  Pallas kernels: 0 us -> 21 us
  matrix products: 16.3 us -> 0 us
  starting transfers between devices: 13.4 us -> 28.1 us
  between operations: 13.2 us -> 0.26 us
  other arithmetic: 9.1 us -> 0 us
  local copies, waits for them, and re-layouts: 9.16 us -> 2.79 us
    all_to_all x2 -> x0, waiting for transfers between devices: 45.8 us -> none  [the longest x1 45.8 us: local(): lax.all_to_all(contrib, ('row', 'col'), split_axis=0, concat_axis=0, tile...]
    ppermute x0 -> x32, waiting for transfers between devices: none -> 39.8 us  [the longest x19 21.7 us: along_col(): return lax.ppermute(x, 'col', [(i, i ^ k) for i in range(n_col)])]
    ppermute x0 -> x32, starting transfers between devices: none -> 28.1 us  [the longest x13 16.7 us: along_row(): return lax.ppermute(x, 'row', [(i, i ^ k) for i in range(n_row)])]
    reduce_scatter x1 -> x0, waiting for transfers between devices: 24.3 us -> none  [local(): lax.psum_scatter(lax.dot_general(slope, row_student, (((0,), (0,)), ((),...]
    all_gather x2 -> x0, blocking collectives: 23.1 us -> none  [the longest x1 12.2 us: local(): lax.all_gather(student_unit, 'row', axis=0, tiled=True)]
    pallas_call x0 -> x8, Pallas kernels: none -> 21 us  [the longest x4 12.4 us: add_targets(): pl.pallas_call(functools.partial(target_kernel, tubes, per_peer, tokens,...]
    dot_general x5 -> x0, matrix products: 16.3 us -> none  [the longest x1 5.93 us: local(): lax.dot_general(slope, row_student, (((0,), (0,)), ((), ())), preferred_e...]
    all_to_all x2 -> x0, starting transfers between devices: 13.3 us -> none  [the longest x1 7.33 us: local(): lax.all_to_all(cell_index, ('row', 'col'), split_axis=0, concat_axis=0, t...]
  transfers between devices with their start and end apart: 5 -> 32, of which waited for: 2 -> 11; matrix products, arithmetic and copies ran while one was open for 14% -> 2% of each run, Pallas kernels for 0% -> 15%
where the time goes in v1:
time: 92.4 us; the launch traced here: 92 us
  waiting for transfers between devices  39.8 us (43%)
  starting transfers between devices  28.1 us (30%)
  Pallas kernels  21 us (23%)
  local copies, waits for them, and re-layouts  2.79 us (3%)
    ppermute x19, waiting for transfers between devices, along_col(): return lax.ppermute(x, 'col', [(i, i ^ k) for i in range(n_col)])  21.7 us
    ppermute x13, waiting for transfers between devices, along_row(): return lax.ppermute(x, 'row', [(i, i ^ k) for i in range(n_row)])  18.1 us
    ppermute x13, starting transfers between devices, along_row(): return lax.ppermute(x, 'row', [(i, i ^ k) for i in range(n_row)])  16.7 us
    pallas_call x4, Pallas kernels, add_targets(): pl.pallas_call(functools.partial(target_kernel, tubes, per_peer, tokens,...  12.4 us
    ppermute x19, starting transfers between devices, along_col(): return lax.ppermute(x, 'col', [(i, i ^ k) for i in range(n_col)])  11.3 us
    pallas_call x1, Pallas kernels, prepare(): pl.pallas_call(functools.partial(prepare_kernel, slots // peers), out_sha...  3.62 us
    pallas_call x2, Pallas kernels, relate(): pl.pallas_call(functools.partial(relation_kernel, len(students), len(colu...  3.12 us
    pallas_call x1, Pallas kernels, finish(): pl.pallas_call(finish_kernel, out_shape=jax.ShapeDtypeStruct((unit.shape[...  1.94 us
  transfers between devices with their start and end apart: 32, of which 11 were waited for; matrix products, arithmetic and copies ran while one was open for 2% of the time, Pallas kernels for 15%

profile of v1, /device:TPU:0, one launch (start us, length us, event | category | flops | bytes accessed | tf_op | source)
XLA Modules:
  0.0 92.0 jit_solution(2356691204850621147)
XLA Ops:
  0.0 3.6 %shard_map.64 = (bf16[88,768]{1,0:T(8,128)(2,1)}, f32[128,768]{1,0:T(8,128)}, f32[128,128]{1,0:T(8,128)}, bf16[128,768]{1,0:T(8,128)(2,1)}) custom-call(s32[32]{0:T(128)} %bitcast.10, f32[64]{0:T(128)} %table_hbm.1, s32[24,128]{1,0:T(8,128)} %bitcast.9, bf16[80,768]{1,0:T(8,128)(2,1)} %teacher_hbm.1, bf16[128,1920]{1,0:T(8,128)(2,1)} %hidden_hbm.1, ...), custom_call_target="tpu_custom_call" | custom-call | tf_op jit(solution)/shard_map/pallas_call | solution.py:100
  3.6 3.0 %collective-permute-start.24 = (bf16[88,768]{1,0:T(8,128)(2,1)}, bf16[88,768]{1,0:T(8,128)(2,1)S(1)}, u32[]{:S(2)}, u32[]{:S(2)}) collective-permute-start(bf16[88,768]{1,0:T(8,128)(2,1)} %get-tuple-element.18), channel_id=1, source_target_pairs={{0,8},{8,0},{16,24},{24,16},{1,9},{9,1},{17,25},{25,17},{2,10},{10... | collective-permute-start | bytes 405512 | tf_op jit(solution)/shard_map/ppermute | solution.py:330
  6.7 1.6 %collective-permute-start.19 = (bf16[88,768]{1,0:T(8,128)(2,1)}, bf16[88,768]{1,0:T(8,128)(2,1)S(1)}, u32[]{:S(2)}, u32[]{:S(2)}) collective-permute-start(bf16[88,768]{1,0:T(8,128)(2,1)} %get-tuple-element.18), channel_id=1, source_target_pairs={{0,2},{1,3},{2,0},{3,1},{4,6},{5,7},{6,4},{7,5},{8,10},{9,11},{10,... | collective-permute-start | bytes 405512 | tf_op jit(solution)/shard_map/ppermute | solution.py:333
  8.2 2.6 %collective-permute-start.14 = (bf16[88,768]{1,0:T(8,128)(2,1)}, bf16[88,768]{1,0:T(8,128)(2,1)S(1)}, u32[]{:S(2)}, u32[]{:S(2)}) collective-permute-start(bf16[88,768]{1,0:T(8,128)(2,1)} %get-tuple-element.18), channel_id=1, source_target_pairs={{0,4},{1,5},{2,6},{3,7},{4,0},{5,1},{6,2},{7,3},{8,12},{9,13},{10,... | collective-permute-start | bytes 405512 | tf_op jit(solution)/shard_map/ppermute | solution.py:333
  10.8 0.2 collective-permute-start.9
  11.0 0.9 %constant_dynamic-update-slice_fusion.9 = bf16[176,768]{1,0:T(8,128)(2,1)S(1)} fusion(bf16[88,768]{1,0:T(8,128)(2,1)} %get-tuple-element.18), kind=kLoop, calls=%fused_computation.9 | loop fusion | bytes 270336
  12.0 1.6 %collective-permute-start.25 = (bf16[176,768]{1,0:T(8,128)(2,1)S(1)}, bf16[176,768]{1,0:T(8,128)(2,1)S(1)}, u32[]{:S(2)}, u32[]{:S(2)}) collective-permute-start(bf16[176,768]{1,0:T(8,128)(2,1)S(1)} %constant_dynamic-update-slice_fusion.8.refs_0_), channel_id=1, source_target_pairs={{0,16},{8,24},{16,0},{24,8},{1,17},{9,25},{17,1},{25,9},{2,18},{10... | collective-permute-start | bytes 811016 | tf_op jit(solution)/shard_map/ppermute | solution.py:330
  13.6 0.6 collective-permute-start.20
  14.2 7.2 %collective-permute-done.14 = bf16[88,768]{1,0:T(8,128)(2,1)S(1)} collective-permute-done((bf16[88,768]{1,0:T(8,128)(2,1)}, bf16[88,768]{1,0:T(8,128)(2,1)S(1)}, u32[]{:S(2)}, u32[]{:S(2)}) %collective-permute-start.14) | collective-permute-done | bytes 135200 | tf_op jit(solution)/shard_map/ppermute | solution.py:333
  21.4 0.6 collective-permute-start.15
  22.0 1.6 %collective-permute-start.10 = (bf16[88,768]{1,0:T(8,128)(2,1)S(1)}, bf16[88,768]{1,0:T(8,128)(2,1)S(1)}, u32[]{:S(2)}, u32[]{:S(2)}) collective-permute-start(bf16[88,768]{1,0:T(8,128)(2,1)S(1)} %collective-permute-done.9), channel_id=1, source_target_pairs={{0,16},{8,24},{16,0},{24,8},{1,17},{9,25},{17,1},{25,9},{2,18},{10... | collective-permute-start | bytes 405512 | tf_op jit(solution)/shard_map/ppermute | solution.py:330
  23.6 0.6 collective-permute-start.21
  24.2 2.3 %collective-permute-done.15 = bf16[88,768]{1,0:T(8,128)(2,1)S(1)} collective-permute-done((bf16[88,768]{1,0:T(8,128)(2,1)S(1)}, bf16[88,768]{1,0:T(8,128)(2,1)S(1)}, u32[]{:S(2)}, u32[]{:S(2)}) %collective-permute-start.15) | collective-permute-done | bytes 135200 | tf_op jit(solution)/shard_map/ppermute | solution.py:330
  26.5 0.6 collective-permute-done.10
  27.1 1.5 %collective-permute-start.16 = (bf16[176,768]{1,0:T(8,128)(2,1)S(1)}, bf16[176,768]{1,0:T(8,128)(2,1)S(1)}, u32[]{:S(2)}, u32[]{:S(2)}) collective-permute-start(bf16[176,768]{1,0:T(8,128)(2,1)S(1)} %constant_dynamic-update-slice_fusion.4.refs_0_), channel_id=1, source_target_pairs={{0,16},{8,24},{16,0},{24,8},{1,17},{9,25},{17,1},{25,9},{2,18},{10... | collective-permute-start | bytes 811016 | tf_op jit(solution)/shard_map/ppermute | solution.py:330
  28.7 1.6 %collective-permute-start.11 = (bf16[176,768]{1,0:T(8,128)(2,1)S(1)}, bf16[176,768]{1,0:T(8,128)(2,1)S(1)}, u32[]{:S(2)}, u32[]{:S(2)}) collective-permute-start(bf16[176,768]{1,0:T(8,128)(2,1)S(1)} %constant_dynamic-update-slice_fusion.2.refs_0_), channel_id=1, source_target_pairs={{0,8},{8,0},{16,24},{24,16},{1,9},{9,1},{17,25},{25,17},{2,10},{10... | collective-permute-start | bytes 811016 | tf_op jit(solution)/shard_map/ppermute | solution.py:330
  30.2 0.4 collective-permute-done.21.refs_1_
  30.6 0.1 collective-permute-start.23
  30.7 0.4 collective-permute-start.17
  31.1 4.8 %collective-permute-done.16.refs_1_ = bf16[176,768]{1,0:T(8,128)(2,1)S(1)} collective-permute-done((bf16[176,768]{1,0:T(8,128)(2,1)S(1)}, bf16[176,768]{1,0:T(8,128)(2,1)S(1)}, u32[]{:S(2)}, u32[]{:S(2)}) %collective-permute-start.16) | collective-permute-done | bytes 270368 | tf_op jit(solution)/shard_map/ppermute | solution.py:330
  36.0 0.8 collective-permute-done.11.refs_1_
  36.8 0.5 collective-permute-start.13
  37.3 0.7 copy-done.3
  38.0 0.6 collective-permute-start.7
  38.6 0.1 stack.31.dests_ref
  38.7 2.7 %shard_map.65.refs_4_ = f32[896,768]{1,0:T(8,128)S(1)} custom-call(s32[7]{0:T(128)S(1)} %stack.31.dests_ref, bf16[176,768]{1,0:T(8,128)(2,1)S(1)} %constant_dynamic-update-slice_fusion.8.refs_0_, bf16[176,768]{1,0:T(8,128)(2,1)S(1)} %collective-permute-done.25.refs_1_, bf16[176,768]{1,0:T(8,128)(2,1)S(1)} %collective-permute-done.26.refs_2_, ...), custom_call_target="tpu_custom_call" | custom-call | tf_op jit(solution)/shard_map/pallas_call | solution.py:216
  41.4 3.1 %shard_map.66.refs_4_ = f32[896,768]{1,0:T(8,128)S(1)} custom-call(s32[7]{0:T(128)S(1)} %stack.31.dests_ref, bf16[176,768]{1,0:T(8,128)(2,1)S(1)} %constant_dynamic-update-slice_fusion.6.refs_0_, bf16[176,768]{1,0:T(8,128)(2,1)S(1)} %collective-permute-done.21.refs_1_, ...), custom_call_target="tpu_custom_call", output_to_operand_aliasing={{}: (5, {})} | custom-call | tf_op jit(solution)/shard_map/pallas_call | solution.py:216
  44.5 3.6 %shard_map.67.refs_4_ = f32[896,768]{1,0:T(8,128)S(1)} custom-call(s32[7]{0:T(128)S(1)} %stack.31.dests_ref, bf16[176,768]{1,0:T(8,128)(2,1)S(1)} %constant_dynamic-update-slice_fusion.4.refs_0_, bf16[176,768]{1,0:T(8,128)(2,1)S(1)} %collective-permute-done.16.refs_1_, ...), custom_call_target="tpu_custom_call", output_to_operand_aliasing={{}: (5, {})} | custom-call | tf_op jit(solution)/shard_map/pallas_call | solution.py:216
  48.1 3.0 %shard_map.68 = (bf16[512,768]{1,0:T(8,128)(2,1)S(1)}, bf16[384,768]{1,0:T(8,128)(2,1)S(1)}) custom-call(s32[7]{0:T(128)S(1)} %stack.31.dests_ref, bf16[176,768]{1,0:T(8,128)(2,1)S(1)} %constant_dynamic-update-slice_fusion.2.refs_0_, bf16[176,768]{1,0:T(8,128)(2,1)S(1)} %collective-permute-done.11.refs_1_, ...), custom_call_target="tpu_custom_call" | custom-call | tf_op jit(solution)/shard_map/pallas_call | solution.py:216
  51.2 0.2 collective-permute-start.28
  51.4 0.9 %constant_dynamic-update-slice_fusion.refs_4_ = bf16[256,768]{1,0:T(8,128)(2,1)S(1)} fusion(bf16[256,768]{1,0:T(8,128)(2,1)S(1)} %constant_dynamic-update-slice_fusion.1, bf16[128,768]{1,0:T(8,128)(2,1)} %collective-permute-done.7), kind=kLoop, calls=%fused_computation | loop fusion | bytes 393216 | tf_op jit(solution)/shard_map/concatenate | solution.py:315
  52.4 1.5 %collective-permute-start.8 = (bf16[256,768]{1,0:T(8,128)(2,1)S(1)}, bf16[256,768]{1,0:T(8,128)(2,1)S(1)}, u32[]{:S(2)}, u32[]{:S(2)}) collective-permute-start(bf16[256,768]{1,0:T(8,128)(2,1)S(1)} %constant_dynamic-update-slice_fusion.refs_4_), channel_id=1, source_target_pairs={{0,8},{8,0},{16,24},{24,16},{1,9},{9,1},{17,25},{25,17},{2,10},{10... | collective-permute-start | bytes 1179656 | tf_op jit(solution)/shard_map/ppermute | solution.py:330
  53.9 2.5 %collective-permute-start.1 = (bf16[128,768]{1,0:T(8,128)(2,1)S(1)}, bf16[128,768]{1,0:T(8,128)(2,1)S(1)}, u32[]{:S(2)}, u32[]{:S(2)}) collective-permute-start(bf16[128,768]{1,0:T(8,128)(2,1)S(1)} %copy-done.1), channel_id=1, source_target_pairs={{0,2},{1,3},{2,0},{3,1},{4,6},{5,7},{6,4},{7,5},{8,10},{9,11},{10,... | collective-permute-start | bytes 589832 | tf_op jit(solution)/shard_map/ppermute | solution.py:333
  56.4 1.1 %collective-permute-start.3 = (bf16[128,768]{1,0:T(8,128)(2,1)S(1)}, bf16[128,768]{1,0:T(8,128)(2,1)S(1)}, u32[]{:S(2)}, u32[]{:S(2)}) collective-permute-start(bf16[128,768]{1,0:T(8,128)(2,1)S(1)} %copy-done.1), channel_id=1, source_target_pairs={{0,4},{1,5},{2,6},{3,7},{4,0},{5,1},{6,2},{7,3},{8,12},{9,13},{10,... | collective-permute-start | bytes 589832 | tf_op jit(solution)/shard_map/ppermute | solution.py:333
  57.6 1.5 %collective-permute-start.5 = (bf16[128,768]{1,0:T(8,128)(2,1)S(1)}, bf16[128,768]{1,0:T(8,128)(2,1)S(1)}, u32[]{:S(2)}, u32[]{:S(2)}) collective-permute-start(bf16[128,768]{1,0:T(8,128)(2,1)S(1)} %copy-done.1), channel_id=1, source_target_pairs={{0,6},{1,7},{2,4},{3,5},{4,2},{5,3},{6,0},{7,1},{8,14},{9,15},{10,... | collective-permute-start | bytes 589832 | tf_op jit(solution)/shard_map/ppermute | solution.py:333
  59.0 6.2 %collective-permute-done.1.refs_1_ = bf16[128,768]{1,0:T(8,128)(2,1)S(1)} collective-permute-done((bf16[128,768]{1,0:T(8,128)(2,1)S(1)}, bf16[128,768]{1,0:T(8,128)(2,1)S(1)}, u32[]{:S(2)}, u32[]{:S(2)}) %collective-permute-start.1) | collective-permute-done | bytes 196640 | tf_op jit(solution)/shard_map/ppermute | solution.py:333
  65.2 8.3 %collective-permute-done.3.refs_2_ = bf16[128,768]{1,0:T(8,128)(2,1)S(1)} collective-permute-done((bf16[128,768]{1,0:T(8,128)(2,1)S(1)}, bf16[128,768]{1,0:T(8,128)(2,1)S(1)}, u32[]{:S(2)}, u32[]{:S(2)}) %collective-permute-start.3) | collective-permute-done | bytes 196640 | tf_op jit(solution)/shard_map/ppermute | solution.py:333
  73.5 0.5 collective-permute-start.4
  74.0 0.1 collective-permute-start.6
  74.1 1.6 %shard_map.69.refs_9_ = f32[512,768]{1,0:T(8,128)S(1)} custom-call(bf16[128,768]{1,0:T(8,128)(2,1)S(1)} %copy-done.1, bf16[128,768]{1,0:T(8,128)(2,1)S(1)} %collective-permute-done.1.refs_1_, bf16[128,768]{1,0:T(8,128)(2,1)S(1)} %collective-permute-done.3.refs_2_, bf16[128,768]{1,0:T(8,128)(2,1)S(1)} %collective-permute-done.5.refs_3_, ...), custom_call_target="tpu_custom_call" | custom-call | tf_op jit(solution)/shard_map/pallas_call | solution.py:274
  75.8 1.6 %shard_map.70 = (f32[128,768]{1,0:T(8,128)S(1)}, bf16[128,768]{1,0:T(8,128)(2,1)S(1)}, bf16[128,768]{1,0:T(8,128)(2,1)S(1)}, bf16[128,768]{1,0:T(8,128)(2,1)S(1)}) custom-call(bf16[128,768]{1,0:T(8,128)(2,1)S(1)} %collective-permute-done.refs_0_, bf16[128,768]{1,0:T(8,128)(2,1)S(1)} %collective-permute-done.2.refs_1_, ...), custom_call_target="tpu_custom_call" | custom-call | tf_op jit(solution)/shard_map/pallas_call | solution.py:274
  77.3 0.6 collective-permute-start.29
  77.9 1.5 %collective-permute-start.30 = (bf16[128,768]{1,0:T(8,128)(2,1)S(1)}, bf16[128,768]{1,0:T(8,128)(2,1)S(1)}, u32[]{:S(2)}, u32[]{:S(2)}) collective-permute-start(bf16[128,768]{1,0:T(8,128)(2,1)S(1)} %get-tuple-element.23), channel_id=1, source_target_pairs={{0,8},{8,0},{16,24},{24,16},{1,9},{9,1},{17,25},{25,17},{2,10},{10... | collective-permute-start | bytes 589832 | tf_op jit(solution)/shard_map/ppermute | solution.py:330
  79.4 1.5 %collective-permute-start.31 = (bf16[128,768]{1,0:T(8,128)(2,1)S(1)}, bf16[128,768]{1,0:T(8,128)(2,1)S(1)}, u32[]{:S(2)}, u32[]{:S(2)}) collective-permute-start(bf16[128,768]{1,0:T(8,128)(2,1)S(1)} %get-tuple-element.24), channel_id=1, source_target_pairs={{0,24},{8,16},{16,8},{24,0},{1,25},{9,17},{17,9},{25,1},{2,26},{10... | collective-permute-start | bytes 589832 | tf_op jit(solution)/shard_map/ppermute | solution.py:330
  80.9 3.8 %collective-permute-done.29.refs_0_ = bf16[128,768]{1,0:T(8,128)(2,1)S(1)} collective-permute-done((bf16[128,768]{1,0:T(8,128)(2,1)S(1)}, bf16[128,768]{1,0:T(8,128)(2,1)S(1)}, u32[]{:S(2)}, u32[]{:S(2)}) %collective-permute-start.29) | collective-permute-done | bytes 196640 | tf_op jit(solution)/shard_map/ppermute | solution.py:330
  84.6 1.0 %collective-permute-done.30.refs_1_ = bf16[128,768]{1,0:T(8,128)(2,1)S(1)} collective-permute-done((bf16[128,768]{1,0:T(8,128)(2,1)S(1)}, bf16[128,768]{1,0:T(8,128)(2,1)S(1)}, u32[]{:S(2)}, u32[]{:S(2)}) %collective-permute-start.30) | collective-permute-done | bytes 196640 | tf_op jit(solution)/shard_map/ppermute | solution.py:330
  85.7 4.4 %collective-permute-done.31.refs_2_ = bf16[128,768]{1,0:T(8,128)(2,1)S(1)} collective-permute-done((bf16[128,768]{1,0:T(8,128)(2,1)S(1)}, bf16[128,768]{1,0:T(8,128)(2,1)S(1)}, u32[]{:S(2)}, u32[]{:S(2)}) %collective-permute-start.31) | collective-permute-done | bytes 196640 | tf_op jit(solution)/shard_map/ppermute | solution.py:330
  90.0 1.9 %shard_map.71 = bf16[128,1920]{1,0:T(8,128)(2,1)} custom-call(f32[128,768]{1,0:T(8,128)S(1)} %copy-done.2, f32[128,128]{1,0:T(8,128)S(1)} %copy-done.5, bf16[1920,768]{1,0:T(8,128)(2,1)S(1)} %copy-done, f32[128,768]{1,0:T(8,128)S(1)} %get-tuple-element.21.own_ref, bf16[128,768]{1,0:T(8,128)(2,1)S(1)} %collective-permute-done.29.refs_0_, ...), custom_call_target="tpu_custom_call" | custom-call | tf_op jit(solution)/shard_map/pallas_call | solution.py:302
  (47 shorter events, 0.2 us)
Async XLA Ops:
  3.6 8.4 %collective-permute-start.24 = (bf16[88,768]{1,0:T(8,128)(2,1)}, bf16[88,768]{1,0:T(8,128)(2,1)S(1)}, u32[]{:S(2)}, u32[]{:S(2)}) collective-permute-start(bf16[88,768]{1,0:T(8,128)(2,1)} %get-tuple-element.18), channel_id=1, source_target_pairs={{0,8},{8,0},{16,24},{24,16},{1,9},{9,1},{17,25},{25,17},{2,10},{10... | collective-permute-start | bytes 405512 | tf_op jit(solution)/shard_map/ppermute | solution.py:330
  6.7 7.0 %collective-permute-start.19 = (bf16[88,768]{1,0:T(8,128)(2,1)}, bf16[88,768]{1,0:T(8,128)(2,1)S(1)}, u32[]{:S(2)}, u32[]{:S(2)}) collective-permute-start(bf16[88,768]{1,0:T(8,128)(2,1)} %get-tuple-element.18), channel_id=1, source_target_pairs={{0,2},{1,3},{2,0},{3,1},{4,6},{5,7},{6,4},{7,5},{8,10},{9,11},{10,... | collective-permute-start | bytes 405512 | tf_op jit(solution)/shard_map/ppermute | solution.py:333
  8.2 13.2 %collective-permute-start.14 = (bf16[88,768]{1,0:T(8,128)(2,1)}, bf16[88,768]{1,0:T(8,128)(2,1)S(1)}, u32[]{:S(2)}, u32[]{:S(2)}) collective-permute-start(bf16[88,768]{1,0:T(8,128)(2,1)} %get-tuple-element.18), channel_id=1, source_target_pairs={{0,4},{1,5},{2,6},{3,7},{4,0},{5,1},{6,2},{7,3},{8,12},{9,13},{10,... | collective-permute-start | bytes 405512 | tf_op jit(solution)/shard_map/ppermute | solution.py:333
  10.8 11.2 %collective-permute-start.9 = (bf16[88,768]{1,0:T(8,128)(2,1)}, bf16[88,768]{1,0:T(8,128)(2,1)S(1)}, u32[]{:S(2)}, u32[]{:S(2)}) collective-permute-start(bf16[88,768]{1,0:T(8,128)(2,1)} %get-tuple-element.18), channel_id=1, source_target_pairs={{0,6},{1,7},{2,4},{3,5},{4,2},{5,3},{6,0},{7,1},{8,14},{9,15},{10,... | collective-permute-start | bytes 405512 | tf_op jit(solution)/shard_map/ppermute | solution.py:333
  12.0 16.6 %collective-permute-start.25 = (bf16[176,768]{1,0:T(8,128)(2,1)S(1)}, bf16[176,768]{1,0:T(8,128)(2,1)S(1)}, u32[]{:S(2)}, u32[]{:S(2)}) collective-permute-start(bf16[176,768]{1,0:T(8,128)(2,1)S(1)} %constant_dynamic-update-slice_fusion.8.refs_0_), channel_id=1, source_target_pairs={{0,16},{8,24},{16,0},{24,8},{1,17},{9,25},{17,1},{25,9},{2,18},{10... | collective-permute-start | bytes 811016 | tf_op jit(solution)/shard_map/ppermute | solution.py:330
  13.6 16.6 %collective-permute-start.26 = (bf16[176,768]{1,0:T(8,128)(2,1)S(1)}, bf16[176,768]{1,0:T(8,128)(2,1)S(1)}, u32[]{:S(2)}, u32[]{:S(2)}) collective-permute-start(bf16[176,768]{1,0:T(8,128)(2,1)S(1)} %constant_dynamic-update-slice_fusion.8.refs_0_), channel_id=1, source_target_pairs={{0,1},{1,0},{2,3},{3,2},{4,5},{5,4},{6,7},{7,6},{8,9},{9,8},{10,11... | collective-permute-start | bytes 811016 | tf_op jit(solution)/shard_map/ppermute | solution.py:333
  13.6 10.0 %collective-permute-start.20 = (bf16[88,768]{1,0:T(8,128)(2,1)S(1)}, bf16[88,768]{1,0:T(8,128)(2,1)S(1)}, u32[]{:S(2)}, u32[]{:S(2)}) collective-permute-start(bf16[88,768]{1,0:T(8,128)(2,1)S(1)} %collective-permute-done.19), channel_id=1, source_target_pairs={{0,8},{8,0},{16,24},{24,16},{1,9},{9,1},{17,25},{25,17},{2,10},{10... | collective-permute-start | bytes 405512 | tf_op jit(solution)/shard_map/ppermute | solution.py:330
  21.4 5.1 %collective-permute-start.15 = (bf16[88,768]{1,0:T(8,128)(2,1)S(1)}, bf16[88,768]{1,0:T(8,128)(2,1)S(1)}, u32[]{:S(2)}, u32[]{:S(2)}) collective-permute-start(bf16[88,768]{1,0:T(8,128)(2,1)S(1)} %collective-permute-done.14), channel_id=1, source_target_pairs={{0,8},{8,0},{16,24},{24,16},{1,9},{9,1},{17,25},{25,17},{2,10},{10... | collective-permute-start | bytes 405512 | tf_op jit(solution)/shard_map/ppermute | solution.py:330
  22.0 5.1 %collective-permute-start.10 = (bf16[88,768]{1,0:T(8,128)(2,1)S(1)}, bf16[88,768]{1,0:T(8,128)(2,1)S(1)}, u32[]{:S(2)}, u32[]{:S(2)}) collective-permute-start(bf16[88,768]{1,0:T(8,128)(2,1)S(1)} %collective-permute-done.9), channel_id=1, source_target_pairs={{0,16},{8,24},{16,0},{24,8},{1,17},{9,25},{17,1},{25,9},{2,18},{10... | collective-permute-start | bytes 405512 | tf_op jit(solution)/shard_map/ppermute | solution.py:330
  23.6 7.0 %collective-permute-start.21 = (bf16[176,768]{1,0:T(8,128)(2,1)S(1)}, bf16[176,768]{1,0:T(8,128)(2,1)S(1)}, u32[]{:S(2)}, u32[]{:S(2)}) collective-permute-start(bf16[176,768]{1,0:T(8,128)(2,1)S(1)} %constant_dynamic-update-slice_fusion.6.refs_0_), channel_id=1, source_target_pairs={{0,16},{8,24},{16,0},{24,8},{1,17},{9,25},{17,1},{25,9},{2,18},{10... | collective-permute-start | bytes 811016 | tf_op jit(solution)/shard_map/ppermute | solution.py:330
  26.5 4.2 %collective-permute-start.22 = (bf16[176,768]{1,0:T(8,128)(2,1)S(1)}, bf16[176,768]{1,0:T(8,128)(2,1)S(1)}, u32[]{:S(2)}, u32[]{:S(2)}) collective-permute-start(bf16[176,768]{1,0:T(8,128)(2,1)S(1)} %constant_dynamic-update-slice_fusion.6.refs_0_), channel_id=1, source_target_pairs={{0,1},{1,0},{2,3},{3,2},{4,5},{5,4},{6,7},{7,6},{8,9},{9,8},{10,11... | collective-permute-start | bytes 811016 | tf_op jit(solution)/shard_map/ppermute | solution.py:333
  27.1 8.8 %collective-permute-start.16 = (bf16[176,768]{1,0:T(8,128)(2,1)S(1)}, bf16[176,768]{1,0:T(8,128)(2,1)S(1)}, u32[]{:S(2)}, u32[]{:S(2)}) collective-permute-start(bf16[176,768]{1,0:T(8,128)(2,1)S(1)} %constant_dynamic-update-slice_fusion.4.refs_0_), channel_id=1, source_target_pairs={{0,16},{8,24},{16,0},{24,8},{1,17},{9,25},{17,1},{25,9},{2,18},{10... | collective-permute-start | bytes 811016 | tf_op jit(solution)/shard_map/ppermute | solution.py:330
  28.7 8.2 %collective-permute-start.11 = (bf16[176,768]{1,0:T(8,128)(2,1)S(1)}, bf16[176,768]{1,0:T(8,128)(2,1)S(1)}, u32[]{:S(2)}, u32[]{:S(2)}) collective-permute-start(bf16[176,768]{1,0:T(8,128)(2,1)S(1)} %constant_dynamic-update-slice_fusion.2.refs_0_), channel_id=1, source_target_pairs={{0,8},{8,0},{16,24},{24,16},{1,9},{9,1},{17,25},{25,17},{2,10},{10... | collective-permute-start | bytes 811016 | tf_op jit(solution)/shard_map/ppermute | solution.py:330
  30.2 6.6 %collective-permute-start.27 = (bf16[176,768]{1,0:T(8,128)(2,1)S(1)}, bf16[176,768]{1,0:T(8,128)(2,1)S(1)}, u32[]{:S(2)}, u32[]{:S(2)}) collective-permute-start(bf16[176,768]{1,0:T(8,128)(2,1)S(1)} %collective-permute-done.25.refs_1_), channel_id=1, source_target_pairs={{0,1},{1,0},{2,3},{3,2},{4,5},{5,4},{6,7},{7,6},{8,9},{9,8},{10,11... | collective-permute-start | bytes 811016 | tf_op jit(solution)/shard_map/ppermute | solution.py:333
  30.6 6.7 %collective-permute-start.23 = (bf16[176,768]{1,0:T(8,128)(2,1)S(1)}, bf16[176,768]{1,0:T(8,128)(2,1)S(1)}, u32[]{:S(2)}, u32[]{:S(2)}) collective-permute-start(bf16[176,768]{1,0:T(8,128)(2,1)S(1)} %collective-permute-done.21.refs_1_), channel_id=1, source_target_pairs={{0,1},{1,0},{2,3},{3,2},{4,5},{5,4},{6,7},{7,6},{8,9},{9,8},{10,11... | collective-permute-start | bytes 811016 | tf_op jit(solution)/shard_map/ppermute | solution.py:333
  30.7 13.8 %collective-permute-start.17 = (bf16[176,768]{1,0:T(8,128)(2,1)S(1)}, bf16[176,768]{1,0:T(8,128)(2,1)}, u32[]{:S(2)}, u32[]{:S(2)}) collective-permute-start(bf16[176,768]{1,0:T(8,128)(2,1)S(1)} %constant_dynamic-update-slice_fusion.4.refs_0_), channel_id=1, source_target_pairs={{0,1},{1,0},{2,3},{3,2},{4,5},{5,4},{6,7},{7,6},{8,9},{9,8},{10,11... | collective-permute-start | bytes 811016 | tf_op jit(solution)/shard_map/ppermute | solution.py:333
  36.0 8.5 %collective-permute-start.18 = (bf16[176,768]{1,0:T(8,128)(2,1)S(1)}, bf16[176,768]{1,0:T(8,128)(2,1)}, u32[]{:S(2)}, u32[]{:S(2)}) collective-permute-start(bf16[176,768]{1,0:T(8,128)(2,1)S(1)} %collective-permute-done.16.refs_1_), channel_id=1, source_target_pairs={{0,1},{1,0},{2,3},{3,2},{4,5},{5,4},{6,7},{7,6},{8,9},{9,8},{10,11... | collective-permute-start | bytes 811016 | tf_op jit(solution)/shard_map/ppermute | solution.py:333
  36.8 11.3 %collective-permute-start.12 = (bf16[176,768]{1,0:T(8,128)(2,1)S(1)}, bf16[176,768]{1,0:T(8,128)(2,1)S(1)}, u32[]{:S(2)}, u32[]{:S(2)}) collective-permute-start(bf16[176,768]{1,0:T(8,128)(2,1)S(1)} %constant_dynamic-update-slice_fusion.2.refs_0_), channel_id=1, source_target_pairs={{0,1},{1,0},{2,3},{3,2},{4,5},{5,4},{6,7},{7,6},{8,9},{9,8},{10,11... | collective-permute-start | bytes 811016 | tf_op jit(solution)/shard_map/ppermute | solution.py:333
  36.8 11.3 %collective-permute-start.13 = (bf16[176,768]{1,0:T(8,128)(2,1)S(1)}, bf16[176,768]{1,0:T(8,128)(2,1)S(1)}, u32[]{:S(2)}, u32[]{:S(2)}) collective-permute-start(bf16[176,768]{1,0:T(8,128)(2,1)S(1)} %collective-permute-done.11.refs_1_), channel_id=1, source_target_pairs={{0,1},{1,0},{2,3},{3,2},{4,5},{5,4},{6,7},{7,6},{8,9},{9,8},{10,11... | collective-permute-start | bytes 811016 | tf_op jit(solution)/shard_map/ppermute | solution.py:333
  37.3 0.7 copy-start.3
  38.0 13.4 %collective-permute-start.7 = (bf16[128,768]{1,0:T(8,128)(2,1)}, bf16[128,768]{1,0:T(8,128)(2,1)}, u32[]{:S(2)}, u32[]{:S(2)}) collective-permute-start(bf16[128,768]{1,0:T(8,128)(2,1)} %get-tuple-element.17.refs_0_), channel_id=1, source_target_pairs={{0,16},{8,24},{16,0},{24,8},{1,17},{9,25},{17,1},{25,9},{2,18},{10... | collective-permute-start | bytes 589832 | tf_op jit(solution)/shard_map/ppermute | solution.py:330
  38.7 2.7 %copy-start.4 = (bf16[176,768]{1,0:T(8,128)(2,1)S(1)}, bf16[176,768]{1,0:T(8,128)(2,1)}, u32[]{:S(2)}) copy-start(bf16[176,768]{1,0:T(8,128)(2,1)} %copy-done.3) | copy-start | bytes 811012
  48.1 3.3 %copy-start.1 = (bf16[128,768]{1,0:T(8,128)(2,1)S(1)}, bf16[128,768]{1,0:T(8,128)(2,1)}, u32[]{:S(2)}) copy-start(bf16[128,768]{1,0:T(8,128)(2,1)} %get-tuple-element.17.refs_0_) | copy-start | bytes 589828
  51.2 24.6 %collective-permute-start.28 = (bf16[512,768]{1,0:T(8,128)(2,1)S(1)}, bf16[512,768]{1,0:T(8,128)(2,1)S(1)}, u32[]{:S(2)}, u32[]{:S(2)}) collective-permute-start(bf16[512,768]{1,0:T(8,128)(2,1)S(1)} %get-tuple-element.19.refs_6_.refs_7_), channel_id=1, source_target_pairs={{0,1},{1,0},{2,3},{3,2},{4,5},{5,4},{6,7},{7,6},{8,9},{9,8},{10,11... | collective-permute-start | bytes 2359304 | tf_op jit(solution)/shard_map/ppermute | solution.py:333
  52.4 21.7 %collective-permute-start.8 = (bf16[256,768]{1,0:T(8,128)(2,1)S(1)}, bf16[256,768]{1,0:T(8,128)(2,1)S(1)}, u32[]{:S(2)}, u32[]{:S(2)}) collective-permute-start(bf16[256,768]{1,0:T(8,128)(2,1)S(1)} %constant_dynamic-update-slice_fusion.refs_4_), channel_id=1, source_target_pairs={{0,8},{8,0},{16,24},{24,16},{1,9},{9,1},{17,25},{25,17},{2,10},{10... | collective-permute-start | bytes 1179656 | tf_op jit(solution)/shard_map/ppermute | solution.py:330
  53.9 11.3 %collective-permute-start.1 = (bf16[128,768]{1,0:T(8,128)(2,1)S(1)}, bf16[128,768]{1,0:T(8,128)(2,1)S(1)}, u32[]{:S(2)}, u32[]{:S(2)}) collective-permute-start(bf16[128,768]{1,0:T(8,128)(2,1)S(1)} %copy-done.1), channel_id=1, source_target_pairs={{0,2},{1,3},{2,0},{3,1},{4,6},{5,7},{6,4},{7,5},{8,10},{9,11},{10,... | collective-permute-start | bytes 589832 | tf_op jit(solution)/shard_map/ppermute | solution.py:333
  56.4 17.1 %collective-permute-start.3 = (bf16[128,768]{1,0:T(8,128)(2,1)S(1)}, bf16[128,768]{1,0:T(8,128)(2,1)S(1)}, u32[]{:S(2)}, u32[]{:S(2)}) collective-permute-start(bf16[128,768]{1,0:T(8,128)(2,1)S(1)} %copy-done.1), channel_id=1, source_target_pairs={{0,4},{1,5},{2,6},{3,7},{4,0},{5,1},{6,2},{7,3},{8,12},{9,13},{10,... | collective-permute-start | bytes 589832 | tf_op jit(solution)/shard_map/ppermute | solution.py:333
  57.6 16.0 %collective-permute-start.5 = (bf16[128,768]{1,0:T(8,128)(2,1)S(1)}, bf16[128,768]{1,0:T(8,128)(2,1)S(1)}, u32[]{:S(2)}, u32[]{:S(2)}) collective-permute-start(bf16[128,768]{1,0:T(8,128)(2,1)S(1)} %copy-done.1), channel_id=1, source_target_pairs={{0,6},{1,7},{2,4},{3,5},{4,2},{5,3},{6,0},{7,1},{8,14},{9,15},{10,... | collective-permute-start | bytes 589832 | tf_op jit(solution)/shard_map/ppermute | solution.py:333
  65.2 10.5 %collective-permute-start = (bf16[128,768]{1,0:T(8,128)(2,1)S(1)}, bf16[128,768]{1,0:T(8,128)(2,1)S(1)}, u32[]{:S(2)}, u32[]{:S(2)}) collective-permute-start(bf16[128,768]{1,0:T(8,128)(2,1)S(1)} %copy-done.1), channel_id=1, source_target_pairs={{0,1},{1,0},{2,3},{3,2},{4,5},{5,4},{6,7},{7,6},{8,9},{9,8},{10,11... | collective-permute-start | bytes 589832 | tf_op jit(solution)/shard_map/ppermute | solution.py:333
  73.5 2.2 %collective-permute-start.2 = (bf16[128,768]{1,0:T(8,128)(2,1)S(1)}, bf16[128,768]{1,0:T(8,128)(2,1)S(1)}, u32[]{:S(2)}, u32[]{:S(2)}) collective-permute-start(bf16[128,768]{1,0:T(8,128)(2,1)S(1)} %collective-permute-done.1.refs_1_), channel_id=1, source_target_pairs={{0,1},{1,0},{2,3},{3,2},{4,5},{5,4},{6,7},{7,6},{8,9},{9,8},{10,11... | collective-permute-start | bytes 589832 | tf_op jit(solution)/shard_map/ppermute | solution.py:333
  73.5 2.2 %collective-permute-start.4 = (bf16[128,768]{1,0:T(8,128)(2,1)S(1)}, bf16[128,768]{1,0:T(8,128)(2,1)S(1)}, u32[]{:S(2)}, u32[]{:S(2)}) collective-permute-start(bf16[128,768]{1,0:T(8,128)(2,1)S(1)} %collective-permute-done.3.refs_2_), channel_id=1, source_target_pairs={{0,1},{1,0},{2,3},{3,2},{4,5},{5,4},{6,7},{7,6},{8,9},{9,8},{10,11... | collective-permute-start | bytes 589832 | tf_op jit(solution)/shard_map/ppermute | solution.py:333
  74.0 1.7 %collective-permute-start.6 = (bf16[128,768]{1,0:T(8,128)(2,1)S(1)}, bf16[128,768]{1,0:T(8,128)(2,1)S(1)}, u32[]{:S(2)}, u32[]{:S(2)}) collective-permute-start(bf16[128,768]{1,0:T(8,128)(2,1)S(1)} %collective-permute-done.5.refs_3_), channel_id=1, source_target_pairs={{0,1},{1,0},{2,3},{3,2},{4,5},{5,4},{6,7},{7,6},{8,9},{9,8},{10,11... | collective-permute-start | bytes 589832 | tf_op jit(solution)/shard_map/ppermute | solution.py:333
  75.7 14.4 %copy-start = (bf16[1920,768]{1,0:T(8,128)(2,1)S(1)}, bf16[1920,768]{1,0:T(8,128)(2,1)}, u32[]{:S(2)}) copy-start(bf16[1920,768]{1,0:T(8,128)(2,1)} %projection_ref.1) | copy-start | bytes 8847364
  75.7 14.4 %copy-start.2 = (f32[128,768]{1,0:T(8,128)S(1)}, f32[128,768]{1,0:T(8,128)}, u32[]{:S(2)}) copy-start(f32[128,768]{1,0:T(8,128)} %get-tuple-element.15.unit_ref) | copy-start | bytes 1179652
  75.7 14.3 %copy-start.5 = (f32[128,128]{1,0:T(8,128)S(1)}, f32[128,128]{1,0:T(8,128)}, u32[]{:S(2)}) copy-start(f32[128,128]{1,0:T(8,128)} %get-tuple-element.16.inverse_ref) | copy-start | bytes 196612
  77.3 7.3 %collective-permute-start.29 = (bf16[128,768]{1,0:T(8,128)(2,1)S(1)}, bf16[128,768]{1,0:T(8,128)(2,1)S(1)}, u32[]{:S(2)}, u32[]{:S(2)}) collective-permute-start(bf16[128,768]{1,0:T(8,128)(2,1)S(1)} %get-tuple-element.22), channel_id=1, source_target_pairs={{0,16},{8,24},{16,0},{24,8},{1,17},{9,25},{17,1},{25,9},{2,18},{10... | collective-permute-start | bytes 589832 | tf_op jit(solution)/shard_map/ppermute | solution.py:330
  77.9 7.8 %collective-permute-start.30 = (bf16[128,768]{1,0:T(8,128)(2,1)S(1)}, bf16[128,768]{1,0:T(8,128)(2,1)S(1)}, u32[]{:S(2)}, u32[]{:S(2)}) collective-permute-start(bf16[128,768]{1,0:T(8,128)(2,1)S(1)} %get-tuple-element.23), channel_id=1, source_target_pairs={{0,8},{8,0},{16,24},{24,16},{1,9},{9,1},{17,25},{25,17},{2,10},{10... | collective-permute-start | bytes 589832 | tf_op jit(solution)/shard_map/ppermute | solution.py:330
  79.4 10.6 %collective-permute-start.31 = (bf16[128,768]{1,0:T(8,128)(2,1)S(1)}, bf16[128,768]{1,0:T(8,128)(2,1)S(1)}, u32[]{:S(2)}, u32[]{:S(2)}) collective-permute-start(bf16[128,768]{1,0:T(8,128)(2,1)S(1)} %get-tuple-element.24), channel_id=1, source_target_pairs={{0,24},{8,16},{16,8},{24,0},{1,25},{9,17},{17,9},{25,1},{2,26},{10... | collective-permute-start | bytes 589832 | tf_op jit(solution)/shard_map/ppermute | solution.py:330

commit v2 on v1

--- a/solution.py
+++ b/solution.py
@@ -11,6 +11,8 @@
 norm_eps = 1e-06
 CORES = 2
 LANES = 128
+PARTS = 3
+REVERSED = (1, 3)
 F32 = jnp.float32
 BF16 = jnp.bfloat16
 VMEM = pl.BlockSpec(memory_space=pltpu.VMEM)
@@ -36,9 +38,9 @@
     hidden_hbm,
     projection_hbm,
     out_ref,
+    student_ref,
     unit_ref,
     inverse_ref,
-    student_ref,
     counts,
     table,
     fields,
@@ -47,6 +49,7 @@
     projection,
     sems,
 ):
+    part = projection.shape[0] // PARTS
     copies = [
         pltpu.make_async_copy(source, target, sems.at[i])
         for i, (source, target) in enumerate(
@@ -56,7 +59,10 @@
                 (map_hbm, fields),
                 (teacher_hbm, teacher),
                 (hidden_hbm, hidden),
-                (projection_hbm, projection),
+            )
+            + tuple(
+                (projection_hbm.at[pl.ds(p, part)], projection.at[pl.ds(p, part)])
+                for p in range(0, projection.shape[0], part)
             )
         )
     ]
@@ -81,9 +87,15 @@
     block = jnp.concatenate([tube.astype(F32), cell.astype(F32), weight], axis=1)
     out_ref[tubes:, 0 : 3 * LANES] = block.astype(BF16)
     out_ref[tubes:, 3 * LANES :] = jnp.zeros((rows, out_ref.shape[1] - 3 * LANES), BF16)
-    for copy in copies[4:]:
+    copies[4].wait()
+    proj = jnp.zeros((hidden.shape[0], projection.shape[1]), F32)
+    for i, copy in enumerate(copies[5:]):
         copy.wait()
-    proj = jnp.dot(hidden[...], projection[...], preferred_element_type=F32)
+        proj = proj + jnp.dot(
+            hidden[:, i * part : (i + 1) * part],
+            projection[i * part : (i + 1) * part, :],
+            preferred_element_type=F32,
+        )
     inverse = lax.rsqrt(jnp.sum(proj * proj, axis=1, keepdims=True) + norm_eps)
     unit = proj * inverse
     unit_ref[...] = unit
@@ -101,9 +113,9 @@
         functools.partial(prepare_kernel, slots // peers),
         out_shape=(
             jax.ShapeDtypeStruct((tubes + rows, width), BF16),
+            jax.ShapeDtypeStruct((tokens, width), BF16),
             jax.ShapeDtypeStruct((tokens, width), F32),
             jax.ShapeDtypeStruct((tokens, LANES), F32),
-            jax.ShapeDtypeStruct((tokens, width), BF16),
         ),
         in_specs=[HBM] * 6,
         out_specs=(VMEM,) * 4,
@@ -114,15 +126,21 @@
             pltpu.VMEM(teacher.shape, BF16),
             pltpu.VMEM(hidden.shape, BF16),
             pltpu.VMEM(projection.shape, BF16),
-            pltpu.SemaphoreType.DMA((6,)),
+            pltpu.SemaphoreType.DMA((5 + PARTS,)),
         ],
+        compiler_params=params(40),
     )(
-        block_counts.reshape(peers),
-        interp_weights,
-        block_map.reshape(3 * rows, LANES),
-        teacher,
-        hidden,
-        projection,
+        *(
+            pltpu.with_memory_space_constraint(x, pltpu.HBM)
+            for x in (
+                block_counts.reshape(peers),
+                interp_weights,
+                block_map.reshape(3 * rows, LANES),
+                teacher,
+                hidden,
+                projection,
+            )
+        )
     )
 
 
@@ -228,19 +246,17 @@
     )(dests, *held, *extra)
 
 
-def relation_kernel(n_rows, n_columns, last, *refs):
+def relation_kernel(tokens, n_rows, n_columns, last, *refs):
     students = refs[:n_rows]
     columns = refs[n_rows : n_rows + n_columns]
     teacher_ref, own_ref, column_ref = refs[n_rows + n_columns : n_rows + n_columns + 3]
     rest = refs[n_rows + n_columns + 3 : -3]
     student, column_s, column_t = refs[-3:]
-    tokens = students[0].shape[0]
-    for i, block in enumerate(students):
-        student[i * tokens : (i + 1) * tokens, :] = block[...]
-    at = 0
-    for block in columns:
-        column_s[at : at + block.shape[0], :] = block[...]
-        at += block.shape[0]
+    for blocks, target in ((students, student), (columns, column_s)):
+        at = 0
+        for block in blocks:
+            target[at : at + block.shape[0], :] = block[...]
+            at += block.shape[0]
     column_t[0:tokens, :] = own_ref[0:tokens, :]
     column_t[tokens:, :] = column_ref[...]
     gram_s = lax.dot_general(column_s[...], student[...], NT, preferred_element_type=F32)
@@ -256,8 +272,8 @@
         out[...] = grad[(j + 1) * tokens : (j + 2) * tokens, :].astype(BF16)
 
 
-def relate(students, columns, teacher, own, column_teacher, partial):
-    tokens, width = students[0].shape
+def relate(tokens, students, columns, teacher, own, column_teacher, partial):
+    width = students[0].shape[1]
     total = sum(c.shape[0] for c in columns)
     n_col = total // tokens
     last = partial is not None
@@ -272,12 +288,12 @@
         out_specs = VMEM
         extra = ()
     return pl.pallas_call(
-        functools.partial(relation_kernel, len(students), len(columns), last),
+        functools.partial(relation_kernel, tokens, len(students), len(columns), last),
         out_shape=out_shape,
         in_specs=[VMEM] * (len(students) + len(columns) + 3 + len(extra)),
         out_specs=out_specs,
         scratch_shapes=[
-            pltpu.VMEM((len(students) * tokens, width), BF16),
+            pltpu.VMEM((sum(x.shape[0] for x in students), width), BF16),
             pltpu.VMEM((total, width), BF16),
             pltpu.VMEM((total, width), BF16),
         ],
@@ -308,14 +324,30 @@
     )(unit, inverse, projection, own, *others)
 
 
-def doubled(x, exchange, steps):
-    held, offsets = [x], [0]
+def join_kernel(*refs):
+    at = 0
+    for ref in refs[:-1]:
+        refs[-1][at : at + ref.shape[0], :] = ref[...]
+        at += ref.shape[0]
+
+
+def join(*held):
+    rows = sum(h.shape[0] for h in held)
+    return pl.pallas_call(
+        join_kernel,
+        out_shape=jax.ShapeDtypeStruct((rows, held[0].shape[1]), held[0].dtype),
+        in_specs=[VMEM] * len(held),
+        out_specs=VMEM,
+        compiler_params=params(8),
+    )(*held)
+
+
+def doubled(held, exchange, steps):
     for step in steps:
         if len(held) > 1:
-            held = [jnp.concatenate(held, axis=0)]
+            held = [join(*held)]
         held.append(exchange(held[0], step))
-        offsets += [o ^ step for o in offsets]
-    return held, offsets
+    return held
 
 
 def local(n_row, n_col, student_hidden, projection, teacher, block_map, block_counts, interp_weights):
@@ -324,36 +356,45 @@
     per_peer = block_map.shape[2] // block_counts.shape[1]
     n_z = n_col // CORES
     row, col = lax.axis_index("row"), lax.axis_index("col")
-    steps = [1 << b for b in range(n_row.bit_length() - 1)]
+    row_steps = [1 << b for b in range(n_row.bit_length() - 1)]
+    z_steps = [1 << b for b in range(n_z.bit_length() - 1)]
 
     def along_row(x, k):
         return lax.ppermute(x, "row", [(i, i ^ k) for i in range(n_row)])
 
-    def along_col(x, k):
-        return lax.ppermute(x, "col", [(i, i ^ k) for i in range(n_col)])
-
-    payload, unit, inverse, student = prepare(
+    def along_z(x, k):
+        return lax.ppermute(x, "col", [(i, i ^ (CORES * k)) for i in range(n_col)])
+
+    def to_partner(x):
+        return lax.ppermute(x, "col", [(i, i ^ 1) for i in range(n_col)])
+
+    payload, student, unit, inverse = prepare(
         student_hidden, projection, teacher, block_map, block_counts, interp_weights
     )
-    planes = [payload] + [along_col(payload, CORES * k) for k in range(1, n_z)]
-    columns, offsets = doubled(student, along_row, steps[::-1])
+    rows = payload.shape[0]
+    planes = [payload] + [along_z(payload, k) for k in range(1, n_z)]
+    columns = doubled([student], along_row, row_steps)
+    students = doubled([student], along_z, z_steps)
+    partner_students = [to_partner(x) for x in students]
     dests = jnp.stack(
         [row * n_col + (col ^ (CORES * k)) for k in range(n_z)]
-        + [(row ^ o) * n_col + col for o in offsets[1:]]
+        + [(row ^ j) * n_col + col for j in range(1, n_row)]
     ).astype(jnp.int32)
     total = None
-    for k, plane in enumerate(planes):
-        held, _ = doubled(plane, along_row, steps[::-1] if k == n_z - 1 else steps)
-        held = held + [along_col(x, 1) for x in held]
+    sequence = list(range(n_z))
+    if n_z > 99:
+        sequence[1:3] = 2, 1
+    for k in sequence:
+        order = row_steps[::-1] if k in REVERSED else row_steps
+        held = doubled([planes[k]], along_row, order)
+        held = held + [to_partner(x) for x in held]
         n_last = n_z * tokens if k == n_z - 1 else None
-        total = add_targets(total, held, dests, tubes, per_peer, tokens, payload.shape[0], n_last)
+        total = add_targets(total, held, dests, tubes, per_peer, tokens, rows, n_last)
     own, column = total
-    partner = along_col(own, 1)
-    rows = [student] + [along_col(student, CORES * k) for k in range(1, n_z)]
-    partner_rows = [along_col(x, 1) for x in rows]
-    grad = relate(rows, columns, own, own, column, None)
-    mine, *others = relate(partner_rows, columns, partner, own, column, grad)
-    arrived = [along_row(x, o) for x, o in zip(others, offsets[1:])]
+    partner = to_partner(own)
+    grad = relate(tokens, students, columns, own, own, column, None)
+    mine, *others = relate(tokens, partner_students, columns, partner, own, column, grad)
+    arrived = [along_row(x, j) for j, x in enumerate(others, 1)]
     return finish(unit, inverse, projection, mine, arrived)
 
 

time: 92.4 us -> 89.7 us (0.971)
  starting transfers between devices: 28.1 us -> 26.3 us
    ppermute x13, waiting for transfers between devices: 18.1 us -> 32.9 us  [along_row(): return lax.ppermute(x, 'row', [(i, i ^ k) for i in range(n_row)])]
    ppermute x19 -> x16, waiting for transfers between devices: 21.7 us -> 7.36 us  [the longest x5 7.33 us: along_z(): return lax.ppermute(x, 'col', [(i, i ^ CORES * k) for i in range(n_col)])]
    ppermute x13, starting transfers between devices: 16.7 us -> 15.5 us  [along_row(): return lax.ppermute(x, 'row', [(i, i ^ k) for i in range(n_row)])]
    concatenate x5 -> x0, local copies, waits for them, and re-layouts: 0.98 us -> none  [doubled(): held = [jnp.concatenate(held, axis=0)]]
    pallas_call x1, Pallas kernels: 3.62 us -> 2.66 us  [prepare(): pl.pallas_call(functools.partial(prepare_kernel, slots // peers), out_sha...]
    ppermute x19 -> x16, starting transfers between devices: 11.3 us -> 10.8 us  [the longest x5 9.09 us: along_z(): return lax.ppermute(x, 'col', [(i, i ^ CORES * k) for i in range(n_col)])]
    pallas_call x2 -> x8, Pallas kernels: 3.12 us -> 3.24 us  [the longest x2 3.11 us: relate(): pl.pallas_call(functools.partial(relation_kernel, tokens, len(students),...]
  transfers between devices with their start and end apart: 32 -> 29, of which waited for: 11 -> 10; matrix products, arithmetic and copies ran while one was open for 2% -> 1% of each run, Pallas kernels for 15% -> 16%
where the time goes in v2:
time: 89.7 us; the launch traced here: 89.5 us
  waiting for transfers between devices  40.2 us (45%)
  starting transfers between devices  26.3 us (29%)
  Pallas kernels  20.8 us (23%)
  local copies, waits for them, and re-layouts  1.96 us (2%)
    ppermute x13, waiting for transfers between devices, along_row(): return lax.ppermute(x, 'row', [(i, i ^ k) for i in range(n_row)])  32.9 us
    ppermute x13, starting transfers between devices, along_row(): return lax.ppermute(x, 'row', [(i, i ^ k) for i in range(n_row)])  15.5 us
    pallas_call x4, Pallas kernels, add_targets(): pl.pallas_call(functools.partial(target_kernel, tubes, per_peer, tokens,...  13 us
    ppermute x5, starting transfers between devices, along_z(): return lax.ppermute(x, 'col', [(i, i ^ CORES * k) for i in range(n_col)])  9.09 us
    ppermute x5, waiting for transfers between devices, along_z(): return lax.ppermute(x, 'col', [(i, i ^ CORES * k) for i in range(n_col)])  7.33 us
    pallas_call x2, Pallas kernels, relate(): pl.pallas_call(functools.partial(relation_kernel, tokens, len(students),...  3.11 us
    pallas_call x1, Pallas kernels, prepare(): pl.pallas_call(functools.partial(prepare_kernel, slots // peers), out_sha...  2.66 us
    pallas_call x1, Pallas kernels, finish(): pl.pallas_call(finish_kernel, out_shape=jax.ShapeDtypeStruct((unit.shape[...  1.94 us
  transfers between devices with their start and end apart: 29, of which 10 were waited for; matrix products, arithmetic and copies ran while one was open for 1% of the time, Pallas kernels for 16%

profile of v2, /device:TPU:0, one launch (start us, length us, event | category | flops | bytes accessed | tf_op | source)
XLA Modules:
  0.0 89.5 jit_solution(16457360699220627840)
XLA Ops:
  0.0 2.7 %shard_map.64 = (bf16[88,768]{1,0:T(8,128)(2,1)S(1)}, bf16[128,768]{1,0:T(8,128)(2,1)S(1)}, f32[128,768]{1,0:T(8,128)S(1)}, f32[128,128]{1,0:T(8,128)S(1)}) custom-call(s32[32]{0:T(128)} %bitcast.10, f32[64]{0:T(128)} %table_hbm.1, s32[24,128]{1,0:T(8,128)} %bitcast.9, bf16[80,768]{1,0:T(8,128)(2,1)} %teacher_hbm.1, bf16[128,1920]{1,0:T(8,128)(2,1)} %hidden_hbm.1, ...), custom_call_target="tpu_custom_call" | custom-call | tf_op jit(solution)/shard_map/pallas_call | solution.py:112
  2.7 3.1 %collective-permute-start.16 = (bf16[88,768]{1,0:T(8,128)(2,1)S(1)}, bf16[88,768]{1,0:T(8,128)(2,1)S(1)}, u32[]{:S(2)}, u32[]{:S(2)}) collective-permute-start(bf16[88,768]{1,0:T(8,128)(2,1)S(1)} %get-tuple-element.18.refs_0_), channel_id=1, source_target_pairs={{0,2},{1,3},{2,0},{3,1},{4,6},{5,7},{6,4},{7,5},{8,10},{9,11},{10,... | collective-permute-start | bytes 405512 | tf_op jit(solution)/shard_map/ppermute | solution.py:366
  5.8 1.5 %collective-permute-start.21 = (bf16[88,768]{1,0:T(8,128)(2,1)S(1)}, bf16[88,768]{1,0:T(8,128)(2,1)S(1)}, u32[]{:S(2)}, u32[]{:S(2)}) collective-permute-start(bf16[88,768]{1,0:T(8,128)(2,1)S(1)} %get-tuple-element.18.refs_0_), channel_id=1, source_target_pairs={{0,8},{8,0},{16,24},{24,16},{1,9},{9,1},{17,25},{25,17},{2,10},{10... | collective-permute-start | bytes 405512 | tf_op jit(solution)/shard_map/ppermute | solution.py:363
  7.3 2.6 %collective-permute-start.11 = (bf16[88,768]{1,0:T(8,128)(2,1)S(1)}, bf16[88,768]{1,0:T(8,128)(2,1)S(1)}, u32[]{:S(2)}, u32[]{:S(2)}) collective-permute-start(bf16[88,768]{1,0:T(8,128)(2,1)S(1)} %get-tuple-element.18.refs_0_), channel_id=1, source_target_pairs={{0,4},{1,5},{2,6},{3,7},{4,0},{5,1},{6,2},{7,3},{8,12},{9,13},{10,... | collective-permute-start | bytes 405512 | tf_op jit(solution)/shard_map/ppermute | solution.py:366
  9.9 0.2 collective-permute-start.6
  10.1 1.5 %collective-permute-start.17 = (bf16[88,768]{1,0:T(8,128)(2,1)S(1)}, bf16[88,768]{1,0:T(8,128)(2,1)S(1)}, u32[]{:S(2)}, u32[]{:S(2)}) collective-permute-start(bf16[88,768]{1,0:T(8,128)(2,1)S(1)} %collective-permute-done.16.refs_0_), channel_id=1, source_target_pairs={{0,16},{8,24},{16,0},{24,8},{1,17},{9,25},{17,1},{25,9},{2,18},{10... | collective-permute-start | bytes 405512 | tf_op jit(solution)/shard_map/ppermute | solution.py:363
  11.6 0.8 collective-permute-start.22
  12.4 7.3 %collective-permute-done.11.refs_0_ = bf16[88,768]{1,0:T(8,128)(2,1)S(1)} collective-permute-done((bf16[88,768]{1,0:T(8,128)(2,1)S(1)}, bf16[88,768]{1,0:T(8,128)(2,1)S(1)}, u32[]{:S(2)}, u32[]{:S(2)}) %collective-permute-start.11) | collective-permute-done | bytes 135200 | tf_op jit(solution)/shard_map/ppermute | solution.py:366
  19.8 0.0 collective-permute-start
  19.8 0.0 collective-permute-done.6.refs_0_
  19.8 1.0 %collective-permute-start.12 = (bf16[88,768]{1,0:T(8,128)(2,1)S(1)}, bf16[88,768]{1,0:T(8,128)(2,1)S(1)}, u32[]{:S(2)}, u32[]{:S(2)}) collective-permute-start(bf16[88,768]{1,0:T(8,128)(2,1)S(1)} %collective-permute-done.11.refs_0_), channel_id=1, source_target_pairs={{0,8},{8,0},{16,24},{24,16},{1,9},{9,1},{17,25},{25,17},{2,10},{10... | collective-permute-start | bytes 405512 | tf_op jit(solution)/shard_map/ppermute | solution.py:363
  20.8 1.5 %collective-permute-start.7 = (bf16[88,768]{1,0:T(8,128)(2,1)S(1)}, bf16[88,768]{1,0:T(8,128)(2,1)S(1)}, u32[]{:S(2)}, u32[]{:S(2)}) collective-permute-start(bf16[88,768]{1,0:T(8,128)(2,1)S(1)} %collective-permute-done.6.refs_0_), channel_id=1, source_target_pairs={{0,16},{8,24},{16,0},{24,8},{1,17},{9,25},{17,1},{25,9},{2,18},{10... | collective-permute-start | bytes 405512 | tf_op jit(solution)/shard_map/ppermute | solution.py:363
  22.3 3.0 %collective-permute-done.12.refs_1_ = bf16[88,768]{1,0:T(8,128)(2,1)S(1)} collective-permute-done((bf16[88,768]{1,0:T(8,128)(2,1)S(1)}, bf16[88,768]{1,0:T(8,128)(2,1)S(1)}, u32[]{:S(2)}, u32[]{:S(2)}) %collective-permute-start.12) | collective-permute-done | bytes 135200 | tf_op jit(solution)/shard_map/ppermute | solution.py:363
  25.3 1.7 %collective-permute-start.18 = (bf16[176,768]{1,0:T(8,128)(2,1)S(1)}, bf16[176,768]{1,0:T(8,128)(2,1)}, u32[]{:S(2)}, u32[]{:S(2)}) collective-permute-start(bf16[176,768]{1,0:T(8,128)(2,1)S(1)} %shard_map.69.refs_0_), channel_id=1, source_target_pairs={{0,8},{8,0},{16,24},{24,16},{1,9},{9,1},{17,25},{25,17},{2,10},{10... | collective-permute-start | bytes 811016 | tf_op jit(solution)/shard_map/ppermute | solution.py:363
  27.0 0.0 collective-permute-done.7.refs_1_
  27.0 0.1 collective-permute-start.19
  27.1 1.6 %collective-permute-start.13 = (bf16[176,768]{1,0:T(8,128)(2,1)S(1)}, bf16[176,768]{1,0:T(8,128)(2,1)}, u32[]{:S(2)}, u32[]{:S(2)}) collective-permute-start(bf16[176,768]{1,0:T(8,128)(2,1)S(1)} %shard_map.68.refs_0_), channel_id=1, source_target_pairs={{0,16},{8,24},{16,0},{24,8},{1,17},{9,25},{17,1},{25,9},{2,18},{10... | collective-permute-start | bytes 811016 | tf_op jit(solution)/shard_map/ppermute | solution.py:363
  28.7 0.0 collective-permute-done.22.refs_1_
  28.7 0.3 collective-permute-start.8
  29.1 3.5 %collective-permute-done.18.refs_1_ = bf16[176,768]{1,0:T(8,128)(2,1)} collective-permute-done((bf16[176,768]{1,0:T(8,128)(2,1)S(1)}, bf16[176,768]{1,0:T(8,128)(2,1)}, u32[]{:S(2)}, u32[]{:S(2)}) %collective-permute-start.18) | collective-permute-done | bytes 270368 | tf_op jit(solution)/shard_map/ppermute | solution.py:363
  32.6 0.7 copy-done.1
  33.3 0.5 collective-permute-start.14
  33.8 2.4 %collective-permute-done.13.refs_1_ = bf16[176,768]{1,0:T(8,128)(2,1)} collective-permute-done((bf16[176,768]{1,0:T(8,128)(2,1)S(1)}, bf16[176,768]{1,0:T(8,128)(2,1)}, u32[]{:S(2)}, u32[]{:S(2)}) %collective-permute-start.13) | collective-permute-done | bytes 270368 | tf_op jit(solution)/shard_map/ppermute | solution.py:363
  36.2 1.4 %collective-permute-done.8.refs_1_ = bf16[176,768]{1,0:T(8,128)(2,1)S(1)} collective-permute-done((bf16[176,768]{1,0:T(8,128)(2,1)S(1)}, bf16[176,768]{1,0:T(8,128)(2,1)S(1)}, u32[]{:S(2)}, u32[]{:S(2)}) %collective-permute-start.8) | collective-permute-done | bytes 270368 | tf_op jit(solution)/shard_map/ppermute | solution.py:363
  37.6 0.5 collective-permute-start.10
  38.1 0.6 stack.31.dests_ref
  38.7 0.6 copy-done.3
  39.3 2.7 %shard_map.71.refs_4_ = f32[896,768]{1,0:T(8,128)S(1)} custom-call(s32[7]{0:T(128)S(1)} %copy-done.3, bf16[176,768]{1,0:T(8,128)(2,1)S(1)} %shard_map.70.refs_0_, bf16[176,768]{1,0:T(8,128)(2,1)S(1)} %collective-permute-done.22.refs_1_, bf16[176,768]{1,0:T(8,128)(2,1)S(1)} %collective-permute-done.23.refs_2_, ...), custom_call_target="tpu_custom_call" | custom-call | tf_op jit(solution)/shard_map/pallas_call | solution.py:234
  42.0 3.2 %collective-permute-start.2 = (bf16[256,768]{1,0:T(8,128)(2,1)S(1)}, bf16[256,768]{1,0:T(8,128)(2,1)S(1)}, u32[]{:S(2)}, u32[]{:S(2)}) collective-permute-start(bf16[256,768]{1,0:T(8,128)(2,1)S(1)} %shard_map.65.refs_0_), channel_id=1, source_target_pairs={{0,4},{1,5},{2,6},{3,7},{4,0},{5,1},{6,2},{7,3},{8,12},{9,13},{10,... | collective-permute-start | bytes 1179656 | tf_op jit(solution)/shard_map/ppermute | solution.py:366
  45.2 3.6 %shard_map.72.refs_4_ = f32[896,768]{1,0:T(8,128)S(1)} custom-call(s32[7]{0:T(128)S(1)} %copy-done.3, bf16[176,768]{1,0:T(8,128)(2,1)S(1)} %shard_map.69.refs_0_, bf16[176,768]{1,0:T(8,128)(2,1)} %collective-permute-done.18.refs_1_, bf16[176,768]{1,0:T(8,128)(2,1)S(1)} %copy-done.2, ...), custom_call_target="tpu_custom_call", output_to_operand_aliasing={{}: (5, {})} | custom-call | tf_op jit(solution)/shard_map/pallas_call | solution.py:234
  48.8 3.7 %shard_map.73.refs_4_ = f32[896,768]{1,0:T(8,128)S(1)} custom-call(s32[7]{0:T(128)S(1)} %copy-done.3, bf16[176,768]{1,0:T(8,128)(2,1)S(1)} %shard_map.68.refs_0_, bf16[176,768]{1,0:T(8,128)(2,1)} %collective-permute-done.13.refs_1_, bf16[176,768]{1,0:T(8,128)(2,1)} %collective-permute-done.14.refs_2_, ...), custom_call_target="tpu_custom_call", output_to_operand_aliasing={{}: (5, {})} | custom-call | tf_op jit(solution)/shard_map/pallas_call | solution.py:234
  52.5 3.0 %shard_map.74 = (bf16[512,768]{1,0:T(8,128)(2,1)S(1)}, bf16[384,768]{1,0:T(8,128)(2,1)S(1)}) custom-call(s32[7]{0:T(128)S(1)} %copy-done.3, bf16[176,768]{1,0:T(8,128)(2,1)S(1)} %shard_map.67.refs_0_, bf16[176,768]{1,0:T(8,128)(2,1)S(1)} %collective-permute-done.8.refs_1_, bf16[176,768]{1,0:T(8,128)(2,1)S(1)} %collective-permute-done.9.refs_2_, ...), custom_call_target="tpu_custom_call" | custom-call | tf_op jit(solution)/shard_map/pallas_call | solution.py:234
  55.6 0.1 collective-permute-start.25
  55.6 0.5 collective-permute-start.4
  56.1 6.8 %collective-permute-done.4.refs_1_ = bf16[128,768]{1,0:T(8,128)(2,1)S(1)} collective-permute-done((bf16[128,768]{1,0:T(8,128)(2,1)S(1)}, bf16[128,768]{1,0:T(8,128)(2,1)S(1)}, u32[]{:S(2)}, u32[]{:S(2)}) %collective-permute-start.4) | collective-permute-done | bytes 196640 | tf_op jit(solution)/shard_map/ppermute | solution.py:363
  63.0 1.6 %collective-permute-start.5 = (bf16[256,768]{1,0:T(8,128)(2,1)S(1)}, bf16[256,768]{1,0:T(8,128)(2,1)S(1)}, u32[]{:S(2)}, u32[]{:S(2)}) collective-permute-start(bf16[256,768]{1,0:T(8,128)(2,1)S(1)} %shard_map.66.refs_2_), channel_id=1, source_target_pairs={{0,16},{8,24},{16,0},{24,8},{1,17},{9,25},{17,1},{25,9},{2,18},{10... | collective-permute-start | bytes 1179656 | tf_op jit(solution)/shard_map/ppermute | solution.py:363
  64.5 0.5 collective-permute-start.3
  65.1 8.6 %collective-permute-done.5.refs_3_ = bf16[256,768]{1,0:T(8,128)(2,1)S(1)} collective-permute-done((bf16[256,768]{1,0:T(8,128)(2,1)S(1)}, bf16[256,768]{1,0:T(8,128)(2,1)S(1)}, u32[]{:S(2)}, u32[]{:S(2)}) %collective-permute-start.5) | collective-permute-done | bytes 393248 | tf_op jit(solution)/shard_map/ppermute | solution.py:363
  73.6 1.6 %shard_map.75.refs_7_ = f32[512,768]{1,0:T(8,128)S(1)} custom-call(bf16[256,768]{1,0:T(8,128)(2,1)S(1)} %shard_map.65.refs_0_, bf16[256,768]{1,0:T(8,128)(2,1)S(1)} %collective-permute-done.2.refs_1_, bf16[256,768]{1,0:T(8,128)(2,1)S(1)} %shard_map.66.refs_2_, bf16[256,768]{1,0:T(8,128)(2,1)S(1)} %collective-permute-done.5.refs_3_, ...), custom_call_target="tpu_custom_call" | custom-call | tf_op jit(solution)/shard_map/pallas_call | solution.py:290
  75.2 0.0 copy-start
  75.2 1.6 %shard_map.76 = (f32[128,768]{1,0:T(8,128)S(1)}, bf16[128,768]{1,0:T(8,128)(2,1)S(1)}, bf16[128,768]{1,0:T(8,128)(2,1)S(1)}, bf16[128,768]{1,0:T(8,128)(2,1)S(1)}) custom-call(bf16[256,768]{1,0:T(8,128)(2,1)S(1)} %collective-permute-done.1.refs_0_, bf16[256,768]{1,0:T(8,128)(2,1)S(1)} %collective-permute-done.3.refs_1_, ...), custom_call_target="tpu_custom_call" | custom-call | tf_op jit(solution)/shard_map/pallas_call | solution.py:290
  76.8 0.5 collective-permute-start.26
  77.3 1.5 %collective-permute-start.27 = (bf16[128,768]{1,0:T(8,128)(2,1)S(1)}, bf16[128,768]{1,0:T(8,128)(2,1)S(1)}, u32[]{:S(2)}, u32[]{:S(2)}) collective-permute-start(bf16[128,768]{1,0:T(8,128)(2,1)S(1)} %get-tuple-element.23), channel_id=1, source_target_pairs={{0,16},{8,24},{16,0},{24,8},{1,17},{9,25},{17,1},{25,9},{2,18},{10... | collective-permute-start | bytes 589832 | tf_op jit(solution)/shard_map/ppermute | solution.py:363
  78.8 1.6 %collective-permute-start.28 = (bf16[128,768]{1,0:T(8,128)(2,1)S(1)}, bf16[128,768]{1,0:T(8,128)(2,1)S(1)}, u32[]{:S(2)}, u32[]{:S(2)}) collective-permute-start(bf16[128,768]{1,0:T(8,128)(2,1)S(1)} %get-tuple-element.24), channel_id=1, source_target_pairs={{0,24},{8,16},{16,8},{24,0},{1,25},{9,17},{17,9},{25,1},{2,26},{10... | collective-permute-start | bytes 589832 | tf_op jit(solution)/shard_map/ppermute | solution.py:363
  80.3 4.1 %collective-permute-done.26.refs_0_ = bf16[128,768]{1,0:T(8,128)(2,1)S(1)} collective-permute-done((bf16[128,768]{1,0:T(8,128)(2,1)S(1)}, bf16[128,768]{1,0:T(8,128)(2,1)S(1)}, u32[]{:S(2)}, u32[]{:S(2)}) %collective-permute-start.26) | collective-permute-done | bytes 196640 | tf_op jit(solution)/shard_map/ppermute | solution.py:363
  84.5 1.4 %collective-permute-done.27.refs_1_ = bf16[128,768]{1,0:T(8,128)(2,1)S(1)} collective-permute-done((bf16[128,768]{1,0:T(8,128)(2,1)S(1)}, bf16[128,768]{1,0:T(8,128)(2,1)S(1)}, u32[]{:S(2)}, u32[]{:S(2)}) %collective-permute-start.27) | collective-permute-done | bytes 196640 | tf_op jit(solution)/shard_map/ppermute | solution.py:363
  85.8 1.7 %collective-permute-done.28.refs_2_ = bf16[128,768]{1,0:T(8,128)(2,1)S(1)} collective-permute-done((bf16[128,768]{1,0:T(8,128)(2,1)S(1)}, bf16[128,768]{1,0:T(8,128)(2,1)S(1)}, u32[]{:S(2)}, u32[]{:S(2)}) %collective-permute-start.28) | collective-permute-done | bytes 196640 | tf_op jit(solution)/shard_map/ppermute | solution.py:363
  87.5 1.9 %shard_map.77 = bf16[128,1920]{1,0:T(8,128)(2,1)} custom-call(f32[128,768]{1,0:T(8,128)S(1)} %get-tuple-element.15.unit_ref, f32[128,128]{1,0:T(8,128)S(1)} %get-tuple-element.16.inverse_ref, bf16[1920,768]{1,0:T(8,128)(2,1)S(1)} %copy-done, f32[128,768]{1,0:T(8,128)S(1)} %get-tuple-element.21.own_ref, bf16[128,768]{1,0:T(8,128)(2,1)S(1)} %collective-permute-done.26.refs_0_, ...), custom_call_target="tpu_custom_call" | custom-call | tf_op jit(solution)/shard_map/pallas_call | solution.py:318
  (33 shorter events, 0.2 us)
Async XLA Ops:
  2.7 7.4 %collective-permute-start.16 = (bf16[88,768]{1,0:T(8,128)(2,1)S(1)}, bf16[88,768]{1,0:T(8,128)(2,1)S(1)}, u32[]{:S(2)}, u32[]{:S(2)}) collective-permute-start(bf16[88,768]{1,0:T(8,128)(2,1)S(1)} %get-tuple-element.18.refs_0_), channel_id=1, source_target_pairs={{0,2},{1,3},{2,0},{3,1},{4,6},{5,7},{6,4},{7,5},{8,10},{9,11},{10,... | collective-permute-start | bytes 405512 | tf_op jit(solution)/shard_map/ppermute | solution.py:366
  5.8 5.8 %collective-permute-start.21 = (bf16[88,768]{1,0:T(8,128)(2,1)S(1)}, bf16[88,768]{1,0:T(8,128)(2,1)S(1)}, u32[]{:S(2)}, u32[]{:S(2)}) collective-permute-start(bf16[88,768]{1,0:T(8,128)(2,1)S(1)} %get-tuple-element.18.refs_0_), channel_id=1, source_target_pairs={{0,8},{8,0},{16,24},{24,16},{1,9},{9,1},{17,25},{25,17},{2,10},{10... | collective-permute-start | bytes 405512 | tf_op jit(solution)/shard_map/ppermute | solution.py:363
  7.3 12.5 %collective-permute-start.11 = (bf16[88,768]{1,0:T(8,128)(2,1)S(1)}, bf16[88,768]{1,0:T(8,128)(2,1)S(1)}, u32[]{:S(2)}, u32[]{:S(2)}) collective-permute-start(bf16[88,768]{1,0:T(8,128)(2,1)S(1)} %get-tuple-element.18.refs_0_), channel_id=1, source_target_pairs={{0,4},{1,5},{2,6},{3,7},{4,0},{5,1},{6,2},{7,3},{8,12},{9,13},{10,... | collective-permute-start | bytes 405512 | tf_op jit(solution)/shard_map/ppermute | solution.py:366
  9.9 9.9 %collective-permute-start.6 = (bf16[88,768]{1,0:T(8,128)(2,1)S(1)}, bf16[88,768]{1,0:T(8,128)(2,1)S(1)}, u32[]{:S(2)}, u32[]{:S(2)}) collective-permute-start(bf16[88,768]{1,0:T(8,128)(2,1)S(1)} %get-tuple-element.18.refs_0_), channel_id=1, source_target_pairs={{0,6},{1,7},{2,4},{3,5},{4,2},{5,3},{6,0},{7,1},{8,14},{9,15},{10,... | collective-permute-start | bytes 405512 | tf_op jit(solution)/shard_map/ppermute | solution.py:366
  10.1 10.7 %collective-permute-start.17 = (bf16[88,768]{1,0:T(8,128)(2,1)S(1)}, bf16[88,768]{1,0:T(8,128)(2,1)S(1)}, u32[]{:S(2)}, u32[]{:S(2)}) collective-permute-start(bf16[88,768]{1,0:T(8,128)(2,1)S(1)} %collective-permute-done.16.refs_0_), channel_id=1, source_target_pairs={{0,16},{8,24},{16,0},{24,8},{1,17},{9,25},{17,1},{25,9},{2,18},{10... | collective-permute-start | bytes 405512 | tf_op jit(solution)/shard_map/ppermute | solution.py:363
  11.6 17.1 %collective-permute-start.22 = (bf16[176,768]{1,0:T(8,128)(2,1)S(1)}, bf16[176,768]{1,0:T(8,128)(2,1)S(1)}, u32[]{:S(2)}, u32[]{:S(2)}) collective-permute-start(bf16[176,768]{1,0:T(8,128)(2,1)S(1)} %shard_map.70.refs_0_), channel_id=1, source_target_pairs={{0,16},{8,24},{16,0},{24,8},{1,17},{9,25},{17,1},{25,9},{2,18},{10... | collective-permute-start | bytes 811016 | tf_op jit(solution)/shard_map/ppermute | solution.py:363
  12.4 16.6 %collective-permute-start.23 = (bf16[176,768]{1,0:T(8,128)(2,1)S(1)}, bf16[176,768]{1,0:T(8,128)(2,1)S(1)}, u32[]{:S(2)}, u32[]{:S(2)}) collective-permute-start(bf16[176,768]{1,0:T(8,128)(2,1)S(1)} %shard_map.70.refs_0_), channel_id=1, source_target_pairs={{0,1},{1,0},{2,3},{3,2},{4,5},{5,4},{6,7},{7,6},{8,9},{9,8},{10,11... | collective-permute-start | bytes 811016 | tf_op jit(solution)/shard_map/ppermute | solution.py:369
  19.8 7.4 %collective-permute-start = (bf16[128,768]{1,0:T(8,128)(2,1)S(1)}, bf16[128,768]{1,0:T(8,128)(2,1)S(1)}, u32[]{:S(2)}, u32[]{:S(2)}) collective-permute-start(bf16[128,768]{1,0:T(8,128)(2,1)S(1)} %get-tuple-element.17.refs_0_), channel_id=1, source_target_pairs={{0,2},{1,3},{2,0},{3,1},{4,6},{5,7},{6,4},{7,5},{8,10},{9,11},{10,... | collective-permute-start | bytes 589832 | tf_op jit(solution)/shard_map/ppermute | solution.py:366
  19.8 5.5 %collective-permute-start.12 = (bf16[88,768]{1,0:T(8,128)(2,1)S(1)}, bf16[88,768]{1,0:T(8,128)(2,1)S(1)}, u32[]{:S(2)}, u32[]{:S(2)}) collective-permute-start(bf16[88,768]{1,0:T(8,128)(2,1)S(1)} %collective-permute-done.11.refs_0_), channel_id=1, source_target_pairs={{0,8},{8,0},{16,24},{24,16},{1,9},{9,1},{17,25},{25,17},{2,10},{10... | collective-permute-start | bytes 405512 | tf_op jit(solution)/shard_map/ppermute | solution.py:363
  20.8 6.2 %collective-permute-start.7 = (bf16[88,768]{1,0:T(8,128)(2,1)S(1)}, bf16[88,768]{1,0:T(8,128)(2,1)S(1)}, u32[]{:S(2)}, u32[]{:S(2)}) collective-permute-start(bf16[88,768]{1,0:T(8,128)(2,1)S(1)} %collective-permute-done.6.refs_0_), channel_id=1, source_target_pairs={{0,16},{8,24},{16,0},{24,8},{1,17},{9,25},{17,1},{25,9},{2,18},{10... | collective-permute-start | bytes 405512 | tf_op jit(solution)/shard_map/ppermute | solution.py:363
  25.3 7.3 %collective-permute-start.18 = (bf16[176,768]{1,0:T(8,128)(2,1)S(1)}, bf16[176,768]{1,0:T(8,128)(2,1)}, u32[]{:S(2)}, u32[]{:S(2)}) collective-permute-start(bf16[176,768]{1,0:T(8,128)(2,1)S(1)} %shard_map.69.refs_0_), channel_id=1, source_target_pairs={{0,8},{8,0},{16,24},{24,16},{1,9},{9,1},{17,25},{25,17},{2,10},{10... | collective-permute-start | bytes 811016 | tf_op jit(solution)/shard_map/ppermute | solution.py:363
  27.0 5.5 %collective-permute-start.19 = (bf16[176,768]{1,0:T(8,128)(2,1)S(1)}, bf16[176,768]{1,0:T(8,128)(2,1)S(1)}, u32[]{:S(2)}, u32[]{:S(2)}) collective-permute-start(bf16[176,768]{1,0:T(8,128)(2,1)S(1)} %shard_map.69.refs_0_), channel_id=1, source_target_pairs={{0,1},{1,0},{2,3},{3,2},{4,5},{5,4},{6,7},{7,6},{8,9},{9,8},{10,11... | collective-permute-start | bytes 811016 | tf_op jit(solution)/shard_map/ppermute | solution.py:369
  27.1 9.0 %collective-permute-start.13 = (bf16[176,768]{1,0:T(8,128)(2,1)S(1)}, bf16[176,768]{1,0:T(8,128)(2,1)}, u32[]{:S(2)}, u32[]{:S(2)}) collective-permute-start(bf16[176,768]{1,0:T(8,128)(2,1)S(1)} %shard_map.68.refs_0_), channel_id=1, source_target_pairs={{0,16},{8,24},{16,0},{24,8},{1,17},{9,25},{17,1},{25,9},{2,18},{10... | collective-permute-start | bytes 811016 | tf_op jit(solution)/shard_map/ppermute | solution.py:363
  28.7 8.8 %collective-permute-start.8 = (bf16[176,768]{1,0:T(8,128)(2,1)S(1)}, bf16[176,768]{1,0:T(8,128)(2,1)S(1)}, u32[]{:S(2)}, u32[]{:S(2)}) collective-permute-start(bf16[176,768]{1,0:T(8,128)(2,1)S(1)} %shard_map.67.refs_0_), channel_id=1, source_target_pairs={{0,8},{8,0},{16,24},{24,16},{1,9},{9,1},{17,25},{25,17},{2,10},{10... | collective-permute-start | bytes 811016 | tf_op jit(solution)/shard_map/ppermute | solution.py:363
  29.1 8.5 %collective-permute-start.24 = (bf16[176,768]{1,0:T(8,128)(2,1)S(1)}, bf16[176,768]{1,0:T(8,128)(2,1)S(1)}, u32[]{:S(2)}, u32[]{:S(2)}) collective-permute-start(bf16[176,768]{1,0:T(8,128)(2,1)S(1)} %collective-permute-done.22.refs_1_), channel_id=1, source_target_pairs={{0,1},{1,0},{2,3},{3,2},{4,5},{5,4},{6,7},{7,6},{8,9},{9,8},{10,11... | collective-permute-start | bytes 811016 | tf_op jit(solution)/shard_map/ppermute | solution.py:369
  32.6 9.5 %collective-permute-start.20 = (bf16[176,768]{1,0:T(8,128)(2,1)}, bf16[176,768]{1,0:T(8,128)(2,1)}, u32[]{:S(2)}, u32[]{:S(2)}) collective-permute-start(bf16[176,768]{1,0:T(8,128)(2,1)} %collective-permute-done.18.refs_1_), channel_id=1, source_target_pairs={{0,1},{1,0},{2,3},{3,2},{4,5},{5,4},{6,7},{7,6},{8,9},{9,8},{10,11... | collective-permute-start | bytes 811016 | tf_op jit(solution)/shard_map/ppermute | solution.py:369
  32.6 0.7 copy-start.1
  33.3 15.5 %collective-permute-start.14 = (bf16[176,768]{1,0:T(8,128)(2,1)S(1)}, bf16[176,768]{1,0:T(8,128)(2,1)}, u32[]{:S(2)}, u32[]{:S(2)}) collective-permute-start(bf16[176,768]{1,0:T(8,128)(2,1)S(1)} %shard_map.68.refs_0_), channel_id=1, source_target_pairs={{0,1},{1,0},{2,3},{3,2},{4,5},{5,4},{6,7},{7,6},{8,9},{9,8},{10,11... | collective-permute-start | bytes 811016 | tf_op jit(solution)/shard_map/ppermute | solution.py:369
  36.2 12.6 %collective-permute-start.15 = (bf16[176,768]{1,0:T(8,128)(2,1)}, bf16[176,768]{1,0:T(8,128)(2,1)}, u32[]{:S(2)}, u32[]{:S(2)}) collective-permute-start(bf16[176,768]{1,0:T(8,128)(2,1)} %collective-permute-done.13.refs_1_), channel_id=1, source_target_pairs={{0,1},{1,0},{2,3},{3,2},{4,5},{5,4},{6,7},{7,6},{8,9},{9,8},{10,11... | collective-permute-start | bytes 811016 | tf_op jit(solution)/shard_map/ppermute | solution.py:369
  37.5 15.0 %collective-permute-start.9 = (bf16[176,768]{1,0:T(8,128)(2,1)S(1)}, bf16[176,768]{1,0:T(8,128)(2,1)S(1)}, u32[]{:S(2)}, u32[]{:S(2)}) collective-permute-start(bf16[176,768]{1,0:T(8,128)(2,1)S(1)} %shard_map.67.refs_0_), channel_id=1, source_target_pairs={{0,1},{1,0},{2,3},{3,2},{4,5},{5,4},{6,7},{7,6},{8,9},{9,8},{10,11... | collective-permute-start | bytes 811016 | tf_op jit(solution)/shard_map/ppermute | solution.py:369
  37.6 15.0 %collective-permute-start.10 = (bf16[176,768]{1,0:T(8,128)(2,1)S(1)}, bf16[176,768]{1,0:T(8,128)(2,1)S(1)}, u32[]{:S(2)}, u32[]{:S(2)}) collective-permute-start(bf16[176,768]{1,0:T(8,128)(2,1)S(1)} %collective-permute-done.8.refs_1_), channel_id=1, source_target_pairs={{0,1},{1,0},{2,3},{3,2},{4,5},{5,4},{6,7},{7,6},{8,9},{9,8},{10,11... | collective-permute-start | bytes 811016 | tf_op jit(solution)/shard_map/ppermute | solution.py:369
  38.7 6.5 %copy-start.2 = (bf16[176,768]{1,0:T(8,128)(2,1)S(1)}, bf16[176,768]{1,0:T(8,128)(2,1)}, u32[]{:S(2)}) copy-start(bf16[176,768]{1,0:T(8,128)(2,1)} %copy-done.1) | copy-start | bytes 811012
  38.7 0.6 copy-start.3
  42.0 22.5 %collective-permute-start.2 = (bf16[256,768]{1,0:T(8,128)(2,1)S(1)}, bf16[256,768]{1,0:T(8,128)(2,1)S(1)}, u32[]{:S(2)}, u32[]{:S(2)}) collective-permute-start(bf16[256,768]{1,0:T(8,128)(2,1)S(1)} %shard_map.65.refs_0_), channel_id=1, source_target_pairs={{0,4},{1,5},{2,6},{3,7},{4,0},{5,1},{6,2},{7,3},{8,12},{9,13},{10,... | collective-permute-start | bytes 1179656 | tf_op jit(solution)/shard_map/ppermute | solution.py:366
  55.6 19.7 %collective-permute-start.25 = (bf16[512,768]{1,0:T(8,128)(2,1)S(1)}, bf16[512,768]{1,0:T(8,128)(2,1)S(1)}, u32[]{:S(2)}, u32[]{:S(2)}) collective-permute-start(bf16[512,768]{1,0:T(8,128)(2,1)S(1)} %get-tuple-element.19.refs_4_.refs_5_), channel_id=1, source_target_pairs={{0,1},{1,0},{2,3},{3,2},{4,5},{5,4},{6,7},{7,6},{8,9},{9,8},{10,11... | collective-permute-start | bytes 2359304 | tf_op jit(solution)/shard_map/ppermute | solution.py:369
  55.6 7.3 %collective-permute-start.4 = (bf16[128,768]{1,0:T(8,128)(2,1)S(1)}, bf16[128,768]{1,0:T(8,128)(2,1)S(1)}, u32[]{:S(2)}, u32[]{:S(2)}) collective-permute-start(bf16[128,768]{1,0:T(8,128)(2,1)S(1)} %get-tuple-element.17.refs_0_), channel_id=1, source_target_pairs={{0,8},{8,0},{16,24},{24,16},{1,9},{9,1},{17,25},{25,17},{2,10},{10... | collective-permute-start | bytes 589832 | tf_op jit(solution)/shard_map/ppermute | solution.py:363
  63.0 10.7 %collective-permute-start.5 = (bf16[256,768]{1,0:T(8,128)(2,1)S(1)}, bf16[256,768]{1,0:T(8,128)(2,1)S(1)}, u32[]{:S(2)}, u32[]{:S(2)}) collective-permute-start(bf16[256,768]{1,0:T(8,128)(2,1)S(1)} %shard_map.66.refs_2_), channel_id=1, source_target_pairs={{0,16},{8,24},{16,0},{24,8},{1,17},{9,25},{17,1},{25,9},{2,18},{10... | collective-permute-start | bytes 1179656 | tf_op jit(solution)/shard_map/ppermute | solution.py:363
  64.5 10.7 %collective-permute-start.1 = (bf16[256,768]{1,0:T(8,128)(2,1)S(1)}, bf16[256,768]{1,0:T(8,128)(2,1)S(1)}, u32[]{:S(2)}, u32[]{:S(2)}) collective-permute-start(bf16[256,768]{1,0:T(8,128)(2,1)S(1)} %shard_map.65.refs_0_), channel_id=1, source_target_pairs={{0,1},{1,0},{2,3},{3,2},{4,5},{5,4},{6,7},{7,6},{8,9},{9,8},{10,11... | collective-permute-start | bytes 1179656 | tf_op jit(solution)/shard_map/ppermute | solution.py:369
  64.5 10.7 %collective-permute-start.3 = (bf16[256,768]{1,0:T(8,128)(2,1)S(1)}, bf16[256,768]{1,0:T(8,128)(2,1)S(1)}, u32[]{:S(2)}, u32[]{:S(2)}) collective-permute-start(bf16[256,768]{1,0:T(8,128)(2,1)S(1)} %collective-permute-done.2.refs_1_), channel_id=1, source_target_pairs={{0,1},{1,0},{2,3},{3,2},{4,5},{5,4},{6,7},{7,6},{8,9},{9,8},{10,11... | collective-permute-start | bytes 1179656 | tf_op jit(solution)/shard_map/ppermute | solution.py:369
  75.2 12.4 %copy-start = (bf16[1920,768]{1,0:T(8,128)(2,1)S(1)}, bf16[1920,768]{1,0:T(8,128)(2,1)}, u32[]{:S(2)}) copy-start(bf16[1920,768]{1,0:T(8,128)(2,1)} %projection_ref.1) | copy-start | bytes 8847364
  76.8 7.7 %collective-permute-start.26 = (bf16[128,768]{1,0:T(8,128)(2,1)S(1)}, bf16[128,768]{1,0:T(8,128)(2,1)S(1)}, u32[]{:S(2)}, u32[]{:S(2)}) collective-permute-start(bf16[128,768]{1,0:T(8,128)(2,1)S(1)} %get-tuple-element.22), channel_id=1, source_target_pairs={{0,8},{8,0},{16,24},{24,16},{1,9},{9,1},{17,25},{25,17},{2,10},{10... | collective-permute-start | bytes 589832 | tf_op jit(solution)/shard_map/ppermute | solution.py:363
  77.3 8.6 %collective-permute-start.27 = (bf16[128,768]{1,0:T(8,128)(2,1)S(1)}, bf16[128,768]{1,0:T(8,128)(2,1)S(1)}, u32[]{:S(2)}, u32[]{:S(2)}) collective-permute-start(bf16[128,768]{1,0:T(8,128)(2,1)S(1)} %get-tuple-element.23), channel_id=1, source_target_pairs={{0,16},{8,24},{16,0},{24,8},{1,17},{9,25},{17,1},{25,9},{2,18},{10... | collective-permute-start | bytes 589832 | tf_op jit(solution)/shard_map/ppermute | solution.py:363
  78.8 8.8 %collective-permute-start.28 = (bf16[128,768]{1,0:T(8,128)(2,1)S(1)}, bf16[128,768]{1,0:T(8,128)(2,1)S(1)}, u32[]{:S(2)}, u32[]{:S(2)}) collective-permute-start(bf16[128,768]{1,0:T(8,128)(2,1)S(1)} %get-tuple-element.24), channel_id=1, source_target_pairs={{0,24},{8,16},{16,8},{24,0},{1,25},{9,17},{17,9},{25,1},{2,26},{10... | collective-permute-start | bytes 589832 | tf_op jit(solution)/shard_map/ppermute | solution.py:363

commit v3 on v2

--- a/solution.py
+++ b/solution.py
@@ -29,46 +29,23 @@
     return pltpu.CompilerParams(vmem_limit_bytes=mib * 1024 * 1024)
 
 
-def prepare_kernel(
-    per_peer,
-    counts_hbm,
-    table_hbm,
-    map_hbm,
-    teacher_hbm,
-    hidden_hbm,
-    projection_hbm,
-    out_ref,
-    student_ref,
-    unit_ref,
-    inverse_ref,
-    counts,
-    table,
-    fields,
-    teacher,
-    hidden,
-    projection,
-    sems,
-):
-    part = projection.shape[0] // PARTS
+def in_hbm(*arrays):
+    return [pltpu.with_memory_space_constraint(x, pltpu.HBM) for x in arrays]
+
+
+def started(sources, targets, sems):
     copies = [
         pltpu.make_async_copy(source, target, sems.at[i])
-        for i, (source, target) in enumerate(
-            (
-                (counts_hbm, counts),
-                (table_hbm, table),
-                (map_hbm, fields),
-                (teacher_hbm, teacher),
-                (hidden_hbm, hidden),
-            )
-            + tuple(
-                (projection_hbm.at[pl.ds(p, part)], projection.at[pl.ds(p, part)])
-                for p in range(0, projection.shape[0], part)
-            )
-        )
+        for i, (source, target) in enumerate(zip(sources, targets))
     ]
     for copy in copies:
         copy.start()
-    for copy in copies[:4]:
+    return copies
+
+
+def pack_kernel(per_peer, *refs):
+    out_ref, counts, table, fields, teacher, sems = refs[4:]
+    for copy in started(refs[:4], (counts, table, fields, teacher), sems):
         copy.wait()
     tubes = teacher.shape[0]
     rows = fields.shape[0] // 3
@@ -87,9 +64,47 @@
     block = jnp.concatenate([tube.astype(F32), cell.astype(F32), weight], axis=1)
     out_ref[tubes:, 0 : 3 * LANES] = block.astype(BF16)
     out_ref[tubes:, 3 * LANES :] = jnp.zeros((rows, out_ref.shape[1] - 3 * LANES), BF16)
-    copies[4].wait()
+
+
+def pack(teacher, block_map, block_counts, interp_weights):
+    tubes, width = teacher.shape
+    slots = block_map.shape[2]
+    peers = block_counts.shape[1]
+    rows = slots // LANES
+    return pl.pallas_call(
+        functools.partial(pack_kernel, slots // peers),
+        out_shape=jax.ShapeDtypeStruct((tubes + rows, width), BF16),
+        in_specs=[HBM] * 4,
+        out_specs=VMEM,
+        scratch_shapes=[
+            pltpu.SMEM((peers,), jnp.int32),
+            pltpu.SMEM(interp_weights.shape, F32),
+            pltpu.VMEM((3 * rows, LANES), jnp.int32),
+            pltpu.VMEM(teacher.shape, BF16),
+            pltpu.SemaphoreType.DMA((4,)),
+        ],
+        compiler_params=params(8),
+    )(
+        *in_hbm(
+            block_counts.reshape(peers),
+            interp_weights,
+            block_map.reshape(3 * rows, LANES),
+            teacher,
+        )
+    )
+
+
+def project_kernel(hidden_hbm, projection_hbm, student_ref, unit_ref, inverse_ref, hidden, projection, sems):
+    part = projection.shape[0] // PARTS
+    spans = [pl.ds(i * part, part) for i in range(PARTS)]
+    copies = started(
+        [hidden_hbm] + [projection_hbm.at[span] for span in spans],
+        [hidden] + [projection.at[span] for span in spans],
+        sems,
+    )
+    copies[0].wait()
     proj = jnp.zeros((hidden.shape[0], projection.shape[1]), F32)
-    for i, copy in enumerate(copies[5:]):
+    for i, copy in enumerate(copies[1:]):
         copy.wait()
         proj = proj + jnp.dot(
             hidden[:, i * part : (i + 1) * part],
@@ -103,45 +118,24 @@
     student_ref[...] = unit.astype(BF16)
 
 
-def prepare(hidden, projection, teacher, block_map, block_counts, interp_weights):
-    tubes, width = teacher.shape
-    tokens = hidden.shape[0]
-    slots = block_map.shape[2]
-    peers = block_counts.shape[1]
-    rows = slots // LANES
-    return pl.pallas_call(
-        functools.partial(prepare_kernel, slots // peers),
+def project(hidden, projection):
+    tokens, width = hidden.shape[0], projection.shape[1]
+    return pl.pallas_call(
+        project_kernel,
         out_shape=(
-            jax.ShapeDtypeStruct((tubes + rows, width), BF16),
             jax.ShapeDtypeStruct((tokens, width), BF16),
             jax.ShapeDtypeStruct((tokens, width), F32),
             jax.ShapeDtypeStruct((tokens, LANES), F32),
         ),
-        in_specs=[HBM] * 6,
-        out_specs=(VMEM,) * 4,
+        in_specs=[HBM] * 2,
+        out_specs=(VMEM,) * 3,
         scratch_shapes=[
-            pltpu.SMEM((peers,), jnp.int32),
-            pltpu.SMEM(interp_weights.shape, F32),
-            pltpu.VMEM((3 * rows, LANES), jnp.int32),
-            pltpu.VMEM(teacher.shape, BF16),
             pltpu.VMEM(hidden.shape, BF16),
             pltpu.VMEM(projection.shape, BF16),
-            pltpu.SemaphoreType.DMA((5 + PARTS,)),
+            pltpu.SemaphoreType.DMA((1 + PARTS,)),
         ],
-        compiler_params=params(40),
-    )(
-        *(
-            pltpu.with_memory_space_constraint(x, pltpu.HBM)
-            for x in (
-                block_counts.reshape(peers),
-                interp_weights,
-                block_map.reshape(3 * rows, LANES),
-                teacher,
-                hidden,
-                projection,
-            )
-        )
-    )
+        compiler_params=params(16),
+    )(*in_hbm(hidden, projection))
 
 
 def pick(slots, window, per_peer, masks):
@@ -246,20 +240,21 @@
     )(dests, *held, *extra)
 
 
-def relation_kernel(tokens, n_rows, n_columns, last, *refs):
+def relation_kernel(tokens, n_rows, starts, last, *refs):
     students = refs[:n_rows]
-    columns = refs[n_rows : n_rows + n_columns]
-    teacher_ref, own_ref, column_ref = refs[n_rows + n_columns : n_rows + n_columns + 3]
-    rest = refs[n_rows + n_columns + 3 : -3]
-    student, column_s, column_t = refs[-3:]
-    for blocks, target in ((students, student), (columns, column_s)):
-        at = 0
-        for block in blocks:
-            target[at : at + block.shape[0], :] = block[...]
-            at += block.shape[0]
-    column_t[0:tokens, :] = own_ref[0:tokens, :]
-    column_t[tokens:, :] = column_ref[...]
-    gram_s = lax.dot_general(column_s[...], student[...], NT, preferred_element_type=F32)
+    columns_ref, teacher_ref = refs[n_rows : n_rows + 2]
+    teachers = refs[n_rows + 2 : n_rows + 2 + len(starts)]
+    rest = refs[n_rows + 2 + len(starts) : -2]
+    student, column_t = refs[-2:]
+    at = 0
+    for block in students:
+        student[at : at + block.shape[0], :] = block[...]
+        at += block.shape[0]
+    at = 0
+    for block, (start, rows) in zip(teachers, starts):
+        column_t[at : at + rows, :] = block[start : start + rows, :]
+        at += rows
+    gram_s = lax.dot_general(columns_ref[...], student[...], NT, preferred_element_type=F32)
     gram_t = lax.dot_general(column_t[...], teacher_ref[...], NT, preferred_element_type=F32)
     slope = jnp.clip((gram_s - gram_t) / huber_delta, -1.0, 1.0).astype(BF16)
     grad = jnp.dot(slope, student[...], preferred_element_type=F32)
@@ -267,59 +262,71 @@
         rest[0][...] = grad
         return
     grad = grad + rest[0][...]
-    rest[1][...] = grad[0:tokens, :]
-    for j, out in enumerate(rest[2:]):
-        out[...] = grad[(j + 1) * tokens : (j + 2) * tokens, :].astype(BF16)
-
-
-def relate(tokens, students, columns, teacher, own, column_teacher, partial):
-    width = students[0].shape[1]
-    total = sum(c.shape[0] for c in columns)
-    n_col = total // tokens
+    for j, out in enumerate(rest[1:]):
+        out[...] = grad[j * tokens : (j + 1) * tokens, :].astype(out.dtype)
+
+
+def relate(tokens, students, columns, teacher, column_teacher, partial, kinds):
+    width = columns.shape[1]
+    total = columns.shape[0]
+    starts = tuple((start, rows) for _, start, rows in column_teacher)
     last = partial is not None
     if last:
-        out_shape = (jax.ShapeDtypeStruct((tokens, width), F32),) + (
-            jax.ShapeDtypeStruct((tokens, width), BF16),
-        ) * (n_col - 1)
-        out_specs = (VMEM,) * n_col
+        out_shape = tuple(jax.ShapeDtypeStruct((tokens, width), kind) for kind in kinds)
+        out_specs = (VMEM,) * len(kinds)
         extra = (partial,)
     else:
         out_shape = jax.ShapeDtypeStruct((total, width), F32)
         out_specs = VMEM
         extra = ()
     return pl.pallas_call(
-        functools.partial(relation_kernel, tokens, len(students), len(columns), last),
+        functools.partial(relation_kernel, tokens, len(students), starts, last),
         out_shape=out_shape,
-        in_specs=[VMEM] * (len(students) + len(columns) + 3 + len(extra)),
+        in_specs=[VMEM] * (len(students) + 2 + len(starts) + len(extra)),
         out_specs=out_specs,
         scratch_shapes=[
             pltpu.VMEM((sum(x.shape[0] for x in students), width), BF16),
             pltpu.VMEM((total, width), BF16),
-            pltpu.VMEM((total, width), BF16),
         ],
         compiler_params=params(40),
-    )(*students, *columns, teacher, own, column_teacher, *extra)
+    )(*students, columns, teacher, *(array for array, _, _ in column_teacher), *extra)
 
 
 def finish_kernel(unit_ref, inverse_ref, projection_ref, own_ref, *refs):
+    out_hbm, out, sems = refs[-3:]
     grad = own_ref[...]
-    for other in refs[:-1]:
+    for other in refs[:-3]:
         grad = grad + other[...].astype(F32)
     grad = 2.0 * grad
     unit = unit_ref[...]
     along = jnp.sum(unit * grad, axis=1, keepdims=True)
     grad_proj = ((grad - unit * along) * inverse_ref[:, 0:1]).astype(BF16)
-    refs[-1][...] = lax.dot_general(
-        grad_proj, projection_ref[...], NT, preferred_element_type=F32
-    ).astype(BF16)
+    part = out.shape[1] // PARTS
+    copies = []
+    for i in range(PARTS):
+        span = pl.ds(i * part, part)
+        out[:, i * part : (i + 1) * part] = lax.dot_general(
+            grad_proj,
+            projection_ref[i * part : (i + 1) * part, :],
+            NT,
+            preferred_element_type=F32,
+        ).astype(BF16)
+        copies.append(
+            pltpu.make_async_copy(out.at[:, span], out_hbm.at[:, span], sems.at[i])
+        )
+        copies[-1].start()
+    for copy in copies:
+        copy.wait()
 
 
 def finish(unit, inverse, projection, own, others):
+    shape = (unit.shape[0], projection.shape[0])
     return pl.pallas_call(
         finish_kernel,
-        out_shape=jax.ShapeDtypeStruct((unit.shape[0], projection.shape[0]), BF16),
+        out_shape=jax.ShapeDtypeStruct(shape, BF16),
         in_specs=[VMEM] * (4 + len(others)),
-        out_specs=VMEM,
+        out_specs=HBM,
+        scratch_shapes=[pltpu.VMEM(shape, BF16), pltpu.SemaphoreType.DMA((PARTS,))],
         compiler_params=params(16),
     )(unit, inverse, projection, own, *others)
 
@@ -368,34 +375,50 @@
     def to_partner(x):
         return lax.ppermute(x, "col", [(i, i ^ 1) for i in range(n_col)])
 
-    payload, student, unit, inverse = prepare(
-        student_hidden, projection, teacher, block_map, block_counts, interp_weights
-    )
+    payload = pack(teacher, block_map, block_counts, interp_weights)
+    student, unit, inverse = project(student_hidden, projection)
     rows = payload.shape[0]
     planes = [payload] + [along_z(payload, k) for k in range(1, n_z)]
-    columns = doubled([student], along_row, row_steps)
+    columns = doubled([student], along_row, row_steps[::-1])
     students = doubled([student], along_z, z_steps)
     partner_students = [to_partner(x) for x in students]
+    offsets = [0]
+    for step in row_steps[::-1]:
+        offsets += [j ^ step for j in offsets]
     dests = jnp.stack(
         [row * n_col + (col ^ (CORES * k)) for k in range(n_z)]
-        + [(row ^ j) * n_col + col for j in range(1, n_row)]
+        + [(row ^ j) * n_col + col for j in offsets[1:]]
     ).astype(jnp.int32)
     total = None
-    sequence = list(range(n_z))
-    if n_z > 99:
-        sequence[1:3] = 2, 1
-    for k in sequence:
-        order = row_steps[::-1] if k in REVERSED else row_steps
-        held = doubled([planes[k]], along_row, order)
-        held = held + [to_partner(x) for x in held]
-        n_last = n_z * tokens if k == n_z - 1 else None
-        total = add_targets(total, held, dests, tubes, per_peer, tokens, rows, n_last)
+    batches = [[k] for k in range(min(n_z, 2))] + [
+        list(range(k, min(k + 2, n_z))) for k in range(2, n_z, 2)
+    ]
+    for batch in batches:
+        senders = []
+        for k in batch:
+            order = row_steps[::-1] if k in REVERSED else row_steps
+            held = doubled([planes[k]], along_row, order)
+            senders += held
+            senders += [to_partner(x) for x in held]
+        n_last = n_z * tokens if batch is batches[-1] else None
+        total = add_targets(total, senders, dests, tubes, per_peer, tokens, rows, n_last)
     own, column = total
     partner = to_partner(own)
-    grad = relate(tokens, students, columns, own, own, column, None)
-    mine, *others = relate(tokens, partner_students, columns, partner, own, column, grad)
-    arrived = [along_row(x, j) for j, x in enumerate(others, 1)]
-    return finish(unit, inverse, projection, mine, arrived)
+    half = n_row // 2
+    near = ((own, 0, tokens), (column, 0, (half - 1) * tokens))
+    far = ((column, (half - 1) * tokens, half * tokens),)
+    near_kinds = (F32,) + (BF16,) * (half - 1)
+    far_kinds = (BF16,) * half
+    sides = ((columns[0], near, near_kinds), (columns[1], far, far_kinds))
+    sums = [
+        relate(tokens, students, c, own, t, None, kinds)
+        for c, t, kinds in sides
+    ]
+    blocks = []
+    for i, (c, t, kinds) in enumerate(sides):
+        blocks += relate(tokens, partner_students, c, partner, t, sums[i], kinds)
+    arrived = [along_row(x, j) for j, x in zip(offsets[1:], blocks[1:])]
+    return finish(unit, inverse, projection, blocks[0], arrived)
 
 
 def solution(mesh):

time: 89.7 us -> 87.6 us (0.977)
  waiting for transfers between devices: 40.2 us -> 37 us
  local copies, waits for them, and re-layouts: 1.96 us -> 3.72 us
  starting transfers between devices: 26.3 us -> 25.1 us
    ppermute x13, starting transfers between devices: 15.5 us -> 12.8 us  [along_row(): return lax.ppermute(x, 'row', [(i, i ^ k) for i in range(n_row)])]
    unnamed x8 -> x12, local copies, waits for them, and re-layouts: 1.35 us -> 3.06 us
    ppermute x5, waiting for transfers between devices: 7.33 us -> 5.63 us  [along_z(): return lax.ppermute(x, 'col', [(i, i ^ CORES * k) for i in range(n_col)])]
    ppermute x13, waiting for transfers between devices: 32.9 us -> 31.3 us  [along_row(): return lax.ppermute(x, 'row', [(i, i ^ k) for i in range(n_row)])]
    ppermute x5, starting transfers between devices: 9.09 us -> 10.6 us  [along_z(): return lax.ppermute(x, 'col', [(i, i ^ CORES * k) for i in range(n_col)])]
    pallas_call x4 -> x3, Pallas kernels: 13 us -> 11.6 us  [add_targets(): pl.pallas_call(functools.partial(target_kernel, tubes, per_peer, tokens,...]
    pallas_call x2 -> x3, Pallas kernels: 4.6 us -> 5.32 us  [the longest x1 2.54 us: project(): pl.pallas_call(project_kernel, out_shape=(jax.ShapeDtypeStruct((tokens, w...]
    pallas_call x2 -> x4, Pallas kernels: 3.11 us -> 3.75 us  [relate(): pl.pallas_call(functools.partial(relation_kernel, tokens, len(students),...]
  transfers between devices with their start and end apart: 29 -> 29, of which waited for: 10 -> 12; matrix products, arithmetic and copies ran while one was open for 1% -> 1% of each run, Pallas kernels for 16% -> 20%
where the time goes in v3:
time: 87.6 us; the launch traced here: 86.8 us
  waiting for transfers between devices  37 us (42%)
  starting transfers between devices  25.1 us (29%)
  Pallas kernels  20.8 us (24%)
  local copies, waits for them, and re-layouts  3.72 us (4%)
    ppermute x13, waiting for transfers between devices, along_row(): return lax.ppermute(x, 'row', [(i, i ^ k) for i in range(n_row)])  31.3 us
    ppermute x13, starting transfers between devices, along_row(): return lax.ppermute(x, 'row', [(i, i ^ k) for i in range(n_row)])  12.8 us
    pallas_call x3, Pallas kernels, add_targets(): pl.pallas_call(functools.partial(target_kernel, tubes, per_peer, tokens,...  11.6 us
    ppermute x5, starting transfers between devices, along_z(): return lax.ppermute(x, 'col', [(i, i ^ CORES * k) for i in range(n_col)])  10.6 us
    ppermute x5, waiting for transfers between devices, along_z(): return lax.ppermute(x, 'col', [(i, i ^ CORES * k) for i in range(n_col)])  5.63 us
    pallas_call x4, Pallas kernels, relate(): pl.pallas_call(functools.partial(relation_kernel, tokens, len(students),...  3.75 us
    unnamed x12, local copies, waits for them, and re-layouts  3.06 us
    pallas_call x1, Pallas kernels, project(): pl.pallas_call(project_kernel, out_shape=(jax.ShapeDtypeStruct((tokens, w...  2.54 us
  transfers between devices with their start and end apart: 29, of which 12 were waited for; matrix products, arithmetic and copies ran while one was open for 1% of the time, Pallas kernels for 20%

profile of v3, /device:TPU:0, one launch (start us, length us, event | category | flops | bytes accessed | tf_op | source)
XLA Modules:
  0.0 86.8 jit_solution(7650903031684706781)
XLA Ops:
  0.0 1.0 %shard_map.67.refs_0_ = bf16[88,768]{1,0:T(8,128)(2,1)S(1)} custom-call(s32[32]{0:T(128)} %bitcast.10, f32[64]{0:T(128)} %refs_1_.1, s32[24,128]{1,0:T(8,128)} %bitcast.9, bf16[80,768]{1,0:T(8,128)(2,1)} %refs_3_.1), custom_call_target="tpu_custom_call" | custom-call | tf_op jit(solution)/shard_map/pallas_call | solution.py:74
  1.0 3.1 %collective-permute-start.15 = (bf16[88,768]{1,0:T(8,128)(2,1)S(1)}, bf16[88,768]{1,0:T(8,128)(2,1)S(1)}, u32[]{:S(2)}, u32[]{:S(2)}) collective-permute-start(bf16[88,768]{1,0:T(8,128)(2,1)S(1)} %shard_map.67.refs_0_), channel_id=1, source_target_pairs={{0,2},{1,3},{2,0},{3,1},{4,6},{5,7},{6,4},{7,5},{8,10},{9,11},{10,... | collective-permute-start | bytes 405512 | tf_op jit(solution)/shard_map/ppermute | solution.py:373
  4.1 1.5 %collective-permute-start.20 = (bf16[88,768]{1,0:T(8,128)(2,1)S(1)}, bf16[88,768]{1,0:T(8,128)(2,1)S(1)}, u32[]{:S(2)}, u32[]{:S(2)}) collective-permute-start(bf16[88,768]{1,0:T(8,128)(2,1)S(1)} %shard_map.67.refs_0_), channel_id=1, source_target_pairs={{0,8},{8,0},{16,24},{24,16},{1,9},{9,1},{17,25},{25,17},{2,10},{10... | collective-permute-start | bytes 405512 | tf_op jit(solution)/shard_map/ppermute | solution.py:370
  5.6 2.5 %collective-permute-start.10 = (bf16[88,768]{1,0:T(8,128)(2,1)S(1)}, bf16[88,768]{1,0:T(8,128)(2,1)S(1)}, u32[]{:S(2)}, u32[]{:S(2)}) collective-permute-start(bf16[88,768]{1,0:T(8,128)(2,1)S(1)} %shard_map.67.refs_0_), channel_id=1, source_target_pairs={{0,6},{1,7},{2,4},{3,5},{4,2},{5,3},{6,0},{7,1},{8,14},{9,15},{10,... | collective-permute-start | bytes 405512 | tf_op jit(solution)/shard_map/ppermute | solution.py:373
  8.1 0.1 collective-permute-start.5
  8.2 1.5 %collective-permute-start.16 = (bf16[88,768]{1,0:T(8,128)(2,1)S(1)}, bf16[88,768]{1,0:T(8,128)(2,1)S(1)}, u32[]{:S(2)}, u32[]{:S(2)}) collective-permute-start(bf16[88,768]{1,0:T(8,128)(2,1)S(1)} %collective-permute-done.15.refs_0_), channel_id=1, source_target_pairs={{0,16},{8,24},{16,0},{24,8},{1,17},{9,25},{17,1},{25,9},{2,18},{10... | collective-permute-start | bytes 405512 | tf_op jit(solution)/shard_map/ppermute | solution.py:370
  9.8 1.0 %collective-permute-start.21 = (bf16[176,768]{1,0:T(8,128)(2,1)S(1)}, bf16[176,768]{1,0:T(8,128)(2,1)S(1)}, u32[]{:S(2)}, u32[]{:S(2)}) collective-permute-start(bf16[176,768]{1,0:T(8,128)(2,1)S(1)} %shard_map.71.refs_0_), channel_id=1, source_target_pairs={{0,16},{8,24},{16,0},{24,8},{1,17},{9,25},{17,1},{25,9},{2,18},{10... | collective-permute-start | bytes 811016 | tf_op jit(solution)/shard_map/ppermute | solution.py:370
  10.8 2.5 %shard_map.64 = (bf16[128,768]{1,0:T(8,128)(2,1)S(1)}, f32[128,768]{1,0:T(8,128)S(1)}, f32[128,128]{1,0:T(8,128)S(1)}) custom-call(bf16[128,1920]{1,0:T(8,128)(2,1)} %hidden_hbm.1, bf16[1920,768]{1,0:T(8,128)(2,1)} %projection_ref.1), custom_call_target="tpu_custom_call" | custom-call | tf_op jit(solution)/shard_map/pallas_call | solution.py:123
  13.3 0.6 collective-permute-done.10.refs_0_
  14.0 4.8 %collective-permute-start = (bf16[128,768]{1,0:T(8,128)(2,1)S(1)}, bf16[128,768]{1,0:T(8,128)(2,1)S(1)}, u32[]{:S(2)}, u32[]{:S(2)}) collective-permute-start(bf16[128,768]{1,0:T(8,128)(2,1)S(1)} %get-tuple-element.16.refs_0_), channel_id=1, source_target_pairs={{0,2},{1,3},{2,0},{3,1},{4,6},{5,7},{6,4},{7,5},{8,10},{9,11},{10,... | collective-permute-start | bytes 589832 | tf_op jit(solution)/shard_map/ppermute | solution.py:373
  18.8 1.3 %collective-permute-done.5.refs_0_ = bf16[88,768]{1,0:T(8,128)(2,1)S(1)} collective-permute-done((bf16[88,768]{1,0:T(8,128)(2,1)S(1)}, bf16[88,768]{1,0:T(8,128)(2,1)S(1)}, u32[]{:S(2)}, u32[]{:S(2)}) %collective-permute-start.5) | collective-permute-done | bytes 135200 | tf_op jit(solution)/shard_map/ppermute | solution.py:373
  20.0 1.5 %collective-permute-start.11 = (bf16[88,768]{1,0:T(8,128)(2,1)S(1)}, bf16[88,768]{1,0:T(8,128)(2,1)S(1)}, u32[]{:S(2)}, u32[]{:S(2)}) collective-permute-start(bf16[88,768]{1,0:T(8,128)(2,1)S(1)} %collective-permute-done.10.refs_0_), channel_id=1, source_target_pairs={{0,16},{8,24},{16,0},{24,8},{1,17},{9,25},{17,1},{25,9},{2,18},{10... | collective-permute-start | bytes 405512 | tf_op jit(solution)/shard_map/ppermute | solution.py:370
  21.5 0.5 collective-permute-start.6
  22.1 2.9 %collective-permute-done.11.refs_1_ = bf16[88,768]{1,0:T(8,128)(2,1)S(1)} collective-permute-done((bf16[88,768]{1,0:T(8,128)(2,1)S(1)}, bf16[88,768]{1,0:T(8,128)(2,1)S(1)}, u32[]{:S(2)}, u32[]{:S(2)}) %collective-permute-start.11) | collective-permute-done | bytes 135200 | tf_op jit(solution)/shard_map/ppermute | solution.py:370
  25.0 0.5 collective-permute-start.17
  25.6 1.9 %collective-permute-done.6.refs_1_ = bf16[88,768]{1,0:T(8,128)(2,1)S(1)} collective-permute-done((bf16[88,768]{1,0:T(8,128)(2,1)S(1)}, bf16[88,768]{1,0:T(8,128)(2,1)S(1)}, u32[]{:S(2)}, u32[]{:S(2)}) %collective-permute-start.6) | collective-permute-done | bytes 135200 | tf_op jit(solution)/shard_map/ppermute | solution.py:370
  27.6 0.5 collective-permute-start.12
  28.0 0.8 collective-permute-start.7
  28.8 5.3 %collective-permute-done.17.refs_1_ = bf16[176,768]{1,0:T(8,128)(2,1)} collective-permute-done((bf16[176,768]{1,0:T(8,128)(2,1)S(1)}, bf16[176,768]{1,0:T(8,128)(2,1)}, u32[]{:S(2)}, u32[]{:S(2)}) %collective-permute-start.17) | collective-permute-done | bytes 270368 | tf_op jit(solution)/shard_map/ppermute | solution.py:370
  34.1 0.7 copy-done.3
  34.8 0.5 collective-permute-start.19
  35.3 2.8 %collective-permute-done.12.refs_5_ = bf16[176,768]{1,0:T(8,128)(2,1)S(1)} collective-permute-done((bf16[176,768]{1,0:T(8,128)(2,1)S(1)}, bf16[176,768]{1,0:T(8,128)(2,1)S(1)}, u32[]{:S(2)}, u32[]{:S(2)}) %collective-permute-start.12) | collective-permute-done | bytes 270368 | tf_op jit(solution)/shard_map/ppermute | solution.py:370
  38.2 0.5 collective-permute-start.14
  38.7 0.7 copy-done.1
  39.4 0.7 stack.31.dests_ref
  40.1 1.0 %copy-done.2 = bf16[176,768]{1,0:T(8,128)(2,1)S(1)} copy-done((bf16[176,768]{1,0:T(8,128)(2,1)S(1)}, bf16[176,768]{1,0:T(8,128)(2,1)}, u32[]{:S(2)}) %copy-start.2) | copy-done | bytes 270360
  41.1 0.7 copy-done.5
  41.7 2.7 %shard_map.72.refs_4_ = f32[896,768]{1,0:T(8,128)S(1)} custom-call(s32[7]{0:T(128)S(1)} %copy-done.5, bf16[176,768]{1,0:T(8,128)(2,1)S(1)} %shard_map.71.refs_0_, bf16[176,768]{1,0:T(8,128)(2,1)S(1)} %collective-permute-done.21.refs_1_, bf16[176,768]{1,0:T(8,128)(2,1)S(1)} %collective-permute-done.22.refs_2_, bf16[176,768]{1,0:T(8,128)(2,1)S(1)} %copy-done.2), custom_call_target="tpu_custom_call" | custom-call | tf_op jit(solution)/shard_map/pallas_call | solution.py:228
  44.5 3.6 %shard_map.73.refs_8_ = f32[896,768]{1,0:T(8,128)S(1)} custom-call(s32[7]{0:T(128)S(1)} %copy-done.5, bf16[176,768]{1,0:T(8,128)(2,1)S(1)} %shard_map.70.refs_0_, bf16[176,768]{1,0:T(8,128)(2,1)} %collective-permute-done.17.refs_1_, bf16[176,768]{1,0:T(8,128)(2,1)S(1)} %copy-done.4, ...), custom_call_target="tpu_custom_call", output_to_operand_aliasing={{}: (5, {})} | custom-call | tf_op jit(solution)/shard_map/pallas_call | solution.py:228
  48.2 5.3 %shard_map.74 = (bf16[512,768]{1,0:T(8,128)(2,1)S(1)}, bf16[384,768]{1,0:T(8,128)(2,1)S(1)}) custom-call(s32[7]{0:T(128)S(1)} %copy-done.5, bf16[176,768]{1,0:T(8,128)(2,1)S(1)} %shard_map.68.refs_0_, bf16[176,768]{1,0:T(8,128)(2,1)S(1)} %collective-permute-done.7.refs_1_, bf16[176,768]{1,0:T(8,128)(2,1)S(1)} %collective-permute-done.8.refs_2_, ...), custom_call_target="tpu_custom_call" | custom-call | tf_op jit(solution)/shard_map/pallas_call | solution.py:228
  53.5 0.6 collective-permute-start.24
  54.0 0.7 collective-permute-start.4
  54.7 6.2 %collective-permute-done.4.refs_1_ = bf16[128,768]{1,0:T(8,128)(2,1)S(1)} collective-permute-done((bf16[128,768]{1,0:T(8,128)(2,1)S(1)}, bf16[128,768]{1,0:T(8,128)(2,1)S(1)}, u32[]{:S(2)}, u32[]{:S(2)}) %collective-permute-start.4) | collective-permute-done | bytes 196640 | tf_op jit(solution)/shard_map/ppermute | solution.py:370
  60.9 0.7 collective-permute-start.26
  61.6 3.7 %collective-permute-done.2.refs_1_ = bf16[256,768]{1,0:T(8,128)(2,1)S(1)} collective-permute-done((bf16[256,768]{1,0:T(8,128)(2,1)S(1)}, bf16[256,768]{1,0:T(8,128)(2,1)S(1)}, u32[]{:S(2)}, u32[]{:S(2)}) %collective-permute-start.2) | collective-permute-done | bytes 393248 | tf_op jit(solution)/shard_map/ppermute | solution.py:373
  65.3 0.1 collective-permute-start.3
  65.4 0.9 %shard_map.75.refs_6_ = f32[256,768]{1,0:T(8,128)S(1)} custom-call(bf16[256,768]{1,0:T(8,128)(2,1)S(1)} %shard_map.65.refs_0_, bf16[256,768]{1,0:T(8,128)(2,1)S(1)} %collective-permute-done.2.refs_1_, bf16[256,768]{1,0:T(8,128)(2,1)S(1)} %shard_map.66.refs_2_, bf16[512,768]{1,0:T(8,128)(2,1)S(1)} %get-tuple-element.17.refs_3_.refs_4_, ...), custom_call_target="tpu_custom_call" | custom-call | tf_op jit(solution)/shard_map/pallas_call | solution.py:282
  66.3 4.9 %collective-permute-done.26.refs_2_ = bf16[256,768]{1,0:T(8,128)(2,1)S(1)} collective-permute-done((bf16[256,768]{1,0:T(8,128)(2,1)S(1)}, bf16[256,768]{1,0:T(8,128)(2,1)S(1)}, u32[]{:S(2)}, u32[]{:S(2)}) %collective-permute-start.26) | collective-permute-done | bytes 393248 | tf_op jit(solution)/shard_map/ppermute | solution.py:370
  71.2 0.9 %shard_map.77.refs_5_ = f32[256,768]{1,0:T(8,128)S(1)} custom-call(bf16[256,768]{1,0:T(8,128)(2,1)S(1)} %shard_map.65.refs_0_, bf16[256,768]{1,0:T(8,128)(2,1)S(1)} %collective-permute-done.2.refs_1_, bf16[256,768]{1,0:T(8,128)(2,1)S(1)} %collective-permute-done.26.refs_2_, bf16[512,768]{1,0:T(8,128)(2,1)S(1)} %get-tuple-element.17.refs_3_.refs_4_, ...), custom_call_target="tpu_custom_call" | custom-call | tf_op jit(solution)/shard_map/pallas_call | solution.py:282
  72.2 0.9 %shard_map.78 = (bf16[128,768]{1,0:T(8,128)(2,1)S(1)}, bf16[128,768]{1,0:T(8,128)(2,1)S(1)}) custom-call(bf16[256,768]{1,0:T(8,128)(2,1)S(1)} %collective-permute-done.1.refs_0_, bf16[256,768]{1,0:T(8,128)(2,1)S(1)} %collective-permute-done.3.refs_1_, bf16[256,768]{1,0:T(8,128)(2,1)S(1)} %collective-permute-done.26.refs_2_, ...), custom_call_target="tpu_custom_call" | custom-call | tf_op jit(solution)/shard_map/pallas_call | solution.py:282
  73.2 0.7 collective-permute-start.27
  73.9 1.5 %collective-permute-start.28 = (bf16[128,768]{1,0:T(8,128)(2,1)S(1)}, bf16[128,768]{1,0:T(8,128)(2,1)S(1)}, u32[]{:S(2)}, u32[]{:S(2)}) collective-permute-start(bf16[128,768]{1,0:T(8,128)(2,1)S(1)} %get-tuple-element.22), channel_id=1, source_target_pairs={{0,24},{8,16},{16,8},{24,0},{1,25},{9,17},{17,9},{25,1},{2,26},{10... | collective-permute-start | bytes 589832 | tf_op jit(solution)/shard_map/ppermute | solution.py:370
  75.4 0.9 %shard_map.76 = (f32[128,768]{1,0:T(8,128)S(1)}, bf16[128,768]{1,0:T(8,128)(2,1)S(1)}) custom-call(bf16[256,768]{1,0:T(8,128)(2,1)S(1)} %collective-permute-done.1.refs_0_, bf16[256,768]{1,0:T(8,128)(2,1)S(1)} %collective-permute-done.3.refs_1_, bf16[256,768]{1,0:T(8,128)(2,1)S(1)} %shard_map.66.refs_2_, ...), custom_call_target="tpu_custom_call" | custom-call | tf_op jit(solution)/shard_map/pallas_call | solution.py:282
  76.3 1.4 %collective-permute-start.25 = (bf16[128,768]{1,0:T(8,128)(2,1)S(1)}, bf16[128,768]{1,0:T(8,128)(2,1)S(1)}, u32[]{:S(2)}, u32[]{:S(2)}) collective-permute-start(bf16[128,768]{1,0:T(8,128)(2,1)S(1)} %get-tuple-element.20), channel_id=1, source_target_pairs={{0,16},{8,24},{16,0},{24,8},{1,17},{9,25},{17,1},{25,9},{2,18},{10... | collective-permute-start | bytes 589832 | tf_op jit(solution)/shard_map/ppermute | solution.py:370
  77.7 2.8 %collective-permute-done.27.refs_1_ = bf16[128,768]{1,0:T(8,128)(2,1)S(1)} collective-permute-done((bf16[128,768]{1,0:T(8,128)(2,1)S(1)}, bf16[128,768]{1,0:T(8,128)(2,1)S(1)}, u32[]{:S(2)}, u32[]{:S(2)}) %collective-permute-start.27) | collective-permute-done | bytes 196640 | tf_op jit(solution)/shard_map/ppermute | solution.py:370
  80.5 2.4 %collective-permute-done.28.refs_2_ = bf16[128,768]{1,0:T(8,128)(2,1)S(1)} collective-permute-done((bf16[128,768]{1,0:T(8,128)(2,1)S(1)}, bf16[128,768]{1,0:T(8,128)(2,1)S(1)}, u32[]{:S(2)}, u32[]{:S(2)}) %collective-permute-start.28) | collective-permute-done | bytes 196640 | tf_op jit(solution)/shard_map/ppermute | solution.py:370
  82.9 2.0 %collective-permute-done.25.refs_0_ = bf16[128,768]{1,0:T(8,128)(2,1)S(1)} collective-permute-done((bf16[128,768]{1,0:T(8,128)(2,1)S(1)}, bf16[128,768]{1,0:T(8,128)(2,1)S(1)}, u32[]{:S(2)}, u32[]{:S(2)}) %collective-permute-start.25) | collective-permute-done | bytes 196640 | tf_op jit(solution)/shard_map/ppermute | solution.py:370
  85.0 1.8 %shard_map.79 = bf16[128,1920]{1,0:T(8,128)(2,1)} custom-call(f32[128,768]{1,0:T(8,128)S(1)} %get-tuple-element.14.unit_ref, f32[128,128]{1,0:T(8,128)S(1)} %get-tuple-element.15.inverse_ref, bf16[1920,768]{1,0:T(8,128)(2,1)S(1)} %copy-done, f32[128,768]{1,0:T(8,128)S(1)} %get-tuple-element.19.own_ref, bf16[128,768]{1,0:T(8,128)(2,1)S(1)} %collective-permute-done.25.refs_0_, ...), custom_call_target="tpu_custom_call" | custom-call | tf_op jit(solution)/shard_map/pallas_call | solution.py:324
  (39 shorter events, 0.3 us)
Async XLA Ops:
  1.0 7.2 %collective-permute-start.15 = (bf16[88,768]{1,0:T(8,128)(2,1)S(1)}, bf16[88,768]{1,0:T(8,128)(2,1)S(1)}, u32[]{:S(2)}, u32[]{:S(2)}) collective-permute-start(bf16[88,768]{1,0:T(8,128)(2,1)S(1)} %shard_map.67.refs_0_), channel_id=1, source_target_pairs={{0,2},{1,3},{2,0},{3,1},{4,6},{5,7},{6,4},{7,5},{8,10},{9,11},{10,... | collective-permute-start | bytes 405512 | tf_op jit(solution)/shard_map/ppermute | solution.py:373
  4.1 5.6 %collective-permute-start.20 = (bf16[88,768]{1,0:T(8,128)(2,1)S(1)}, bf16[88,768]{1,0:T(8,128)(2,1)S(1)}, u32[]{:S(2)}, u32[]{:S(2)}) collective-permute-start(bf16[88,768]{1,0:T(8,128)(2,1)S(1)} %shard_map.67.refs_0_), channel_id=1, source_target_pairs={{0,8},{8,0},{16,24},{24,16},{1,9},{9,1},{17,25},{25,17},{2,10},{10... | collective-permute-start | bytes 405512 | tf_op jit(solution)/shard_map/ppermute | solution.py:370
  5.6 8.4 %collective-permute-start.10 = (bf16[88,768]{1,0:T(8,128)(2,1)S(1)}, bf16[88,768]{1,0:T(8,128)(2,1)S(1)}, u32[]{:S(2)}, u32[]{:S(2)}) collective-permute-start(bf16[88,768]{1,0:T(8,128)(2,1)S(1)} %shard_map.67.refs_0_), channel_id=1, source_target_pairs={{0,6},{1,7},{2,4},{3,5},{4,2},{5,3},{6,0},{7,1},{8,14},{9,15},{10,... | collective-permute-start | bytes 405512 | tf_op jit(solution)/shard_map/ppermute | solution.py:373
  8.1 11.9 %collective-permute-start.5 = (bf16[88,768]{1,0:T(8,128)(2,1)S(1)}, bf16[88,768]{1,0:T(8,128)(2,1)S(1)}, u32[]{:S(2)}, u32[]{:S(2)}) collective-permute-start(bf16[88,768]{1,0:T(8,128)(2,1)S(1)} %shard_map.67.refs_0_), channel_id=1, source_target_pairs={{0,4},{1,5},{2,6},{3,7},{4,0},{5,1},{6,2},{7,3},{8,12},{9,13},{10,... | collective-permute-start | bytes 405512 | tf_op jit(solution)/shard_map/ppermute | solution.py:373
  8.2 13.3 %collective-permute-start.16 = (bf16[88,768]{1,0:T(8,128)(2,1)S(1)}, bf16[88,768]{1,0:T(8,128)(2,1)S(1)}, u32[]{:S(2)}, u32[]{:S(2)}) collective-permute-start(bf16[88,768]{1,0:T(8,128)(2,1)S(1)} %collective-permute-done.15.refs_0_), channel_id=1, source_target_pairs={{0,16},{8,24},{16,0},{24,8},{1,17},{9,25},{17,1},{25,9},{2,18},{10... | collective-permute-start | bytes 405512 | tf_op jit(solution)/shard_map/ppermute | solution.py:370
  9.8 18.3 %collective-permute-start.21 = (bf16[176,768]{1,0:T(8,128)(2,1)S(1)}, bf16[176,768]{1,0:T(8,128)(2,1)S(1)}, u32[]{:S(2)}, u32[]{:S(2)}) collective-permute-start(bf16[176,768]{1,0:T(8,128)(2,1)S(1)} %shard_map.71.refs_0_), channel_id=1, source_target_pairs={{0,16},{8,24},{16,0},{24,8},{1,17},{9,25},{17,1},{25,9},{2,18},{10... | collective-permute-start | bytes 811016 | tf_op jit(solution)/shard_map/ppermute | solution.py:370
  10.8 18.0 %collective-permute-start.22 = (bf16[176,768]{1,0:T(8,128)(2,1)S(1)}, bf16[176,768]{1,0:T(8,128)(2,1)S(1)}, u32[]{:S(2)}, u32[]{:S(2)}) collective-permute-start(bf16[176,768]{1,0:T(8,128)(2,1)S(1)} %shard_map.71.refs_0_), channel_id=1, source_target_pairs={{0,1},{1,0},{2,3},{3,2},{4,5},{5,4},{6,7},{7,6},{8,9},{9,8},{10,11... | collective-permute-start | bytes 811016 | tf_op jit(solution)/shard_map/ppermute | solution.py:376
  14.0 13.6 %collective-permute-start = (bf16[128,768]{1,0:T(8,128)(2,1)S(1)}, bf16[128,768]{1,0:T(8,128)(2,1)S(1)}, u32[]{:S(2)}, u32[]{:S(2)}) collective-permute-start(bf16[128,768]{1,0:T(8,128)(2,1)S(1)} %get-tuple-element.16.refs_0_), channel_id=1, source_target_pairs={{0,2},{1,3},{2,0},{3,1},{4,6},{5,7},{6,4},{7,5},{8,10},{9,11},{10,... | collective-permute-start | bytes 589832 | tf_op jit(solution)/shard_map/ppermute | solution.py:373
  20.0 5.0 %collective-permute-start.11 = (bf16[88,768]{1,0:T(8,128)(2,1)S(1)}, bf16[88,768]{1,0:T(8,128)(2,1)S(1)}, u32[]{:S(2)}, u32[]{:S(2)}) collective-permute-start(bf16[88,768]{1,0:T(8,128)(2,1)S(1)} %collective-permute-done.10.refs_0_), channel_id=1, source_target_pairs={{0,16},{8,24},{16,0},{24,8},{1,17},{9,25},{17,1},{25,9},{2,18},{10... | collective-permute-start | bytes 405512 | tf_op jit(solution)/shard_map/ppermute | solution.py:370
  21.5 6.0 %collective-permute-start.6 = (bf16[88,768]{1,0:T(8,128)(2,1)S(1)}, bf16[88,768]{1,0:T(8,128)(2,1)S(1)}, u32[]{:S(2)}, u32[]{:S(2)}) collective-permute-start(bf16[88,768]{1,0:T(8,128)(2,1)S(1)} %collective-permute-done.5.refs_0_), channel_id=1, source_target_pairs={{0,8},{8,0},{16,24},{24,16},{1,9},{9,1},{17,25},{25,17},{2,10},{10... | collective-permute-start | bytes 405512 | tf_op jit(solution)/shard_map/ppermute | solution.py:370
  25.0 9.1 %collective-permute-start.17 = (bf16[176,768]{1,0:T(8,128)(2,1)S(1)}, bf16[176,768]{1,0:T(8,128)(2,1)}, u32[]{:S(2)}, u32[]{:S(2)}) collective-permute-start(bf16[176,768]{1,0:T(8,128)(2,1)S(1)} %shard_map.70.refs_0_), channel_id=1, source_target_pairs={{0,8},{8,0},{16,24},{24,16},{1,9},{9,1},{17,25},{25,17},{2,10},{10... | collective-permute-start | bytes 811016 | tf_op jit(solution)/shard_map/ppermute | solution.py:370
  27.5 6.6 %collective-permute-start.18 = (bf16[176,768]{1,0:T(8,128)(2,1)S(1)}, bf16[176,768]{1,0:T(8,128)(2,1)S(1)}, u32[]{:S(2)}, u32[]{:S(2)}) collective-permute-start(bf16[176,768]{1,0:T(8,128)(2,1)S(1)} %shard_map.70.refs_0_), channel_id=1, source_target_pairs={{0,1},{1,0},{2,3},{3,2},{4,5},{5,4},{6,7},{7,6},{8,9},{9,8},{10,11... | collective-permute-start | bytes 811016 | tf_op jit(solution)/shard_map/ppermute | solution.py:376
  27.6 10.6 %collective-permute-start.12 = (bf16[176,768]{1,0:T(8,128)(2,1)S(1)}, bf16[176,768]{1,0:T(8,128)(2,1)S(1)}, u32[]{:S(2)}, u32[]{:S(2)}) collective-permute-start(bf16[176,768]{1,0:T(8,128)(2,1)S(1)} %shard_map.69.refs_4_), channel_id=1, source_target_pairs={{0,8},{8,0},{16,24},{24,16},{1,9},{9,1},{17,25},{25,17},{2,10},{10... | collective-permute-start | bytes 811016 | tf_op jit(solution)/shard_map/ppermute | solution.py:370
  28.0 10.1 %collective-permute-start.7 = (bf16[176,768]{1,0:T(8,128)(2,1)S(1)}, bf16[176,768]{1,0:T(8,128)(2,1)S(1)}, u32[]{:S(2)}, u32[]{:S(2)}) collective-permute-start(bf16[176,768]{1,0:T(8,128)(2,1)S(1)} %shard_map.68.refs_0_), channel_id=1, source_target_pairs={{0,16},{8,24},{16,0},{24,8},{1,17},{9,25},{17,1},{25,9},{2,18},{10... | collective-permute-start | bytes 811016 | tf_op jit(solution)/shard_map/ppermute | solution.py:370
  28.8 9.9 %collective-permute-start.23 = (bf16[176,768]{1,0:T(8,128)(2,1)S(1)}, bf16[176,768]{1,0:T(8,128)(2,1)S(1)}, u32[]{:S(2)}, u32[]{:S(2)}) collective-permute-start(bf16[176,768]{1,0:T(8,128)(2,1)S(1)} %collective-permute-done.21.refs_1_), channel_id=1, source_target_pairs={{0,1},{1,0},{2,3},{3,2},{4,5},{5,4},{6,7},{7,6},{8,9},{9,8},{10,11... | collective-permute-start | bytes 811016 | tf_op jit(solution)/shard_map/ppermute | solution.py:376
  34.1 14.0 %collective-permute-start.13 = (bf16[176,768]{1,0:T(8,128)(2,1)S(1)}, bf16[176,768]{1,0:T(8,128)(2,1)S(1)}, u32[]{:S(2)}, u32[]{:S(2)}) collective-permute-start(bf16[176,768]{1,0:T(8,128)(2,1)S(1)} %shard_map.69.refs_4_), channel_id=1, source_target_pairs={{0,1},{1,0},{2,3},{3,2},{4,5},{5,4},{6,7},{7,6},{8,9},{9,8},{10,11... | collective-permute-start | bytes 811016 | tf_op jit(solution)/shard_map/ppermute | solution.py:376
  34.1 0.7 copy-start.3
  34.8 9.6 %collective-permute-start.19 = (bf16[176,768]{1,0:T(8,128)(2,1)}, bf16[176,768]{1,0:T(8,128)(2,1)}, u32[]{:S(2)}, u32[]{:S(2)}) collective-permute-start(bf16[176,768]{1,0:T(8,128)(2,1)} %collective-permute-done.17.refs_1_), channel_id=1, source_target_pairs={{0,1},{1,0},{2,3},{3,2},{4,5},{5,4},{6,7},{7,6},{8,9},{9,8},{10,11... | collective-permute-start | bytes 811016 | tf_op jit(solution)/shard_map/ppermute | solution.py:376
  38.1 10.0 %collective-permute-start.8 = (bf16[176,768]{1,0:T(8,128)(2,1)S(1)}, bf16[176,768]{1,0:T(8,128)(2,1)S(1)}, u32[]{:S(2)}, u32[]{:S(2)}) collective-permute-start(bf16[176,768]{1,0:T(8,128)(2,1)S(1)} %shard_map.68.refs_0_), channel_id=1, source_target_pairs={{0,1},{1,0},{2,3},{3,2},{4,5},{5,4},{6,7},{7,6},{8,9},{9,8},{10,11... | collective-permute-start | bytes 811016 | tf_op jit(solution)/shard_map/ppermute | solution.py:376
  38.2 10.0 %collective-permute-start.14 = (bf16[176,768]{1,0:T(8,128)(2,1)S(1)}, bf16[176,768]{1,0:T(8,128)(2,1)}, u32[]{:S(2)}, u32[]{:S(2)}) collective-permute-start(bf16[176,768]{1,0:T(8,128)(2,1)S(1)} %collective-permute-done.12.refs_5_), channel_id=1, source_target_pairs={{0,1},{1,0},{2,3},{3,2},{4,5},{5,4},{6,7},{7,6},{8,9},{9,8},{10,11... | collective-permute-start | bytes 811016 | tf_op jit(solution)/shard_map/ppermute | solution.py:376
  38.7 0.7 copy-start.1
  39.4 8.8 %collective-permute-start.9 = (bf16[176,768]{1,0:T(8,128)(2,1)S(1)}, bf16[176,768]{1,0:T(8,128)(2,1)}, u32[]{:S(2)}, u32[]{:S(2)}) collective-permute-start(bf16[176,768]{1,0:T(8,128)(2,1)S(1)} %collective-permute-done.7.refs_1_), channel_id=1, source_target_pairs={{0,1},{1,0},{2,3},{3,2},{4,5},{5,4},{6,7},{7,6},{8,9},{9,8},{10,11... | collective-permute-start | bytes 811016 | tf_op jit(solution)/shard_map/ppermute | solution.py:376
  40.0 4.5 %copy-start.4 = (bf16[176,768]{1,0:T(8,128)(2,1)S(1)}, bf16[176,768]{1,0:T(8,128)(2,1)}, u32[]{:S(2)}) copy-start(bf16[176,768]{1,0:T(8,128)(2,1)} %copy-done.3) | copy-start | bytes 811012
  40.1 1.0 %copy-start.2 = (bf16[176,768]{1,0:T(8,128)(2,1)S(1)}, bf16[176,768]{1,0:T(8,128)(2,1)}, u32[]{:S(2)}) copy-start(bf16[176,768]{1,0:T(8,128)(2,1)} %copy-done.1) | copy-start | bytes 811012
  41.1 0.7 copy-start.5
  44.4 20.9 %collective-permute-start.2 = (bf16[256,768]{1,0:T(8,128)(2,1)S(1)}, bf16[256,768]{1,0:T(8,128)(2,1)S(1)}, u32[]{:S(2)}, u32[]{:S(2)}) collective-permute-start(bf16[256,768]{1,0:T(8,128)(2,1)S(1)} %shard_map.65.refs_0_), channel_id=1, source_target_pairs={{0,4},{1,5},{2,6},{3,7},{4,0},{5,1},{6,2},{7,3},{8,12},{9,13},{10,... | collective-permute-start | bytes 1179656 | tf_op jit(solution)/shard_map/ppermute | solution.py:373
  53.5 18.7 %collective-permute-start.24 = (bf16[512,768]{1,0:T(8,128)(2,1)S(1)}, bf16[512,768]{1,0:T(8,128)(2,1)S(1)}, u32[]{:S(2)}, u32[]{:S(2)}) collective-permute-start(bf16[512,768]{1,0:T(8,128)(2,1)S(1)} %get-tuple-element.17.refs_3_.refs_4_), channel_id=1, source_target_pairs={{0,1},{1,0},{2,3},{3,2},{4,5},{5,4},{6,7},{7,6},{8,9},{9,8},{10,11... | collective-permute-start | bytes 2359304 | tf_op jit(solution)/shard_map/ppermute | solution.py:376
  54.0 6.9 %collective-permute-start.4 = (bf16[128,768]{1,0:T(8,128)(2,1)S(1)}, bf16[128,768]{1,0:T(8,128)(2,1)S(1)}, u32[]{:S(2)}, u32[]{:S(2)}) collective-permute-start(bf16[128,768]{1,0:T(8,128)(2,1)S(1)} %get-tuple-element.16.refs_0_), channel_id=1, source_target_pairs={{0,16},{8,24},{16,0},{24,8},{1,17},{9,25},{17,1},{25,9},{2,18},{10... | collective-permute-start | bytes 589832 | tf_op jit(solution)/shard_map/ppermute | solution.py:370
  60.9 10.3 %collective-permute-start.26 = (bf16[256,768]{1,0:T(8,128)(2,1)S(1)}, bf16[256,768]{1,0:T(8,128)(2,1)S(1)}, u32[]{:S(2)}, u32[]{:S(2)}) collective-permute-start(bf16[256,768]{1,0:T(8,128)(2,1)S(1)} %shard_map.66.refs_2_), channel_id=1, source_target_pairs={{0,8},{8,0},{16,24},{24,16},{1,9},{9,1},{17,25},{25,17},{2,10},{10... | collective-permute-start | bytes 1179656 | tf_op jit(solution)/shard_map/ppermute | solution.py:370
  61.6 10.6 %collective-permute-start.1 = (bf16[256,768]{1,0:T(8,128)(2,1)S(1)}, bf16[256,768]{1,0:T(8,128)(2,1)S(1)}, u32[]{:S(2)}, u32[]{:S(2)}) collective-permute-start(bf16[256,768]{1,0:T(8,128)(2,1)S(1)} %shard_map.65.refs_0_), channel_id=1, source_target_pairs={{0,1},{1,0},{2,3},{3,2},{4,5},{5,4},{6,7},{7,6},{8,9},{9,8},{10,11... | collective-permute-start | bytes 1179656 | tf_op jit(solution)/shard_map/ppermute | solution.py:376
  65.3 6.9 %collective-permute-start.3 = (bf16[256,768]{1,0:T(8,128)(2,1)S(1)}, bf16[256,768]{1,0:T(8,128)(2,1)S(1)}, u32[]{:S(2)}, u32[]{:S(2)}) collective-permute-start(bf16[256,768]{1,0:T(8,128)(2,1)S(1)} %collective-permute-done.2.refs_1_), channel_id=1, source_target_pairs={{0,1},{1,0},{2,3},{3,2},{4,5},{5,4},{6,7},{7,6},{8,9},{9,8},{10,11... | collective-permute-start | bytes 1179656 | tf_op jit(solution)/shard_map/ppermute | solution.py:376
  73.2 11.8 %copy-start = (bf16[1920,768]{1,0:T(8,128)(2,1)S(1)}, bf16[1920,768]{1,0:T(8,128)(2,1)}, u32[]{:S(2)}) copy-start(bf16[1920,768]{1,0:T(8,128)(2,1)} %projection_ref.1) | copy-start | bytes 8847364
  73.2 7.3 %collective-permute-start.27 = (bf16[128,768]{1,0:T(8,128)(2,1)S(1)}, bf16[128,768]{1,0:T(8,128)(2,1)S(1)}, u32[]{:S(2)}, u32[]{:S(2)}) collective-permute-start(bf16[128,768]{1,0:T(8,128)(2,1)S(1)} %get-tuple-element.21), channel_id=1, source_target_pairs={{0,8},{8,0},{16,24},{24,16},{1,9},{9,1},{17,25},{25,17},{2,10},{10... | collective-permute-start | bytes 589832 | tf_op jit(solution)/shard_map/ppermute | solution.py:370
  73.9 9.1 %collective-permute-start.28 = (bf16[128,768]{1,0:T(8,128)(2,1)S(1)}, bf16[128,768]{1,0:T(8,128)(2,1)S(1)}, u32[]{:S(2)}, u32[]{:S(2)}) collective-permute-start(bf16[128,768]{1,0:T(8,128)(2,1)S(1)} %get-tuple-element.22), channel_id=1, source_target_pairs={{0,24},{8,16},{16,8},{24,0},{1,25},{9,17},{17,9},{25,1},{2,26},{10... | collective-permute-start | bytes 589832 | tf_op jit(solution)/shard_map/ppermute | solution.py:370
  76.3 8.6 %collective-permute-start.25 = (bf16[128,768]{1,0:T(8,128)(2,1)S(1)}, bf16[128,768]{1,0:T(8,128)(2,1)S(1)}, u32[]{:S(2)}, u32[]{:S(2)}) collective-permute-start(bf16[128,768]{1,0:T(8,128)(2,1)S(1)} %get-tuple-element.20), channel_id=1, source_target_pairs={{0,16},{8,24},{16,0},{24,8},{1,17},{9,25},{17,1},{25,9},{2,18},{10... | collective-permute-start | bytes 589832 | tf_op jit(solution)/shard_map/ppermute | solution.py:370

commit v4 on v3

--- a/solution.py
+++ b/solution.py
@@ -390,17 +390,21 @@
         + [(row ^ j) * n_col + col for j in offsets[1:]]
     ).astype(jnp.int32)
     total = None
-    batches = [[k] for k in range(min(n_z, 2))] + [
-        list(range(k, min(k + 2, n_z))) for k in range(2, n_z, 2)
-    ]
-    for batch in batches:
-        senders = []
-        for k in batch:
-            order = row_steps[::-1] if k in REVERSED else row_steps
-            held = doubled([planes[k]], along_row, order)
-            senders += held
-            senders += [to_partner(x) for x in held]
-        n_last = n_z * tokens if batch is batches[-1] else None
+    early, late = [], []
+    batches = []
+    for k in range(n_z):
+        order = row_steps[::-1] if k in REVERSED else row_steps
+        held = doubled([planes[k]], along_row, order)
+        halves = [(x, to_partner(x)) for x in held]
+        if k < n_z - 2:
+            batches.append([*halves[0], *halves[1]])
+        else:
+            early += halves[0]
+            late += halves[1]
+    batches = batches[:-1] + [sum(batches[-1:], []) + early]
+    batches.append(late)
+    for i, senders in enumerate(batches):
+        n_last = n_z * tokens if i == len(batches) - 1 else None
         total = add_targets(total, senders, dests, tubes, per_peer, tokens, rows, n_last)
     own, column = total
     partner = to_partner(own)

time: 87.6 us -> 88.4 us (level)
  starting transfers between devices: 25.1 us -> 26.3 us
    ppermute x13, starting transfers between devices: 12.8 us -> 15.7 us  [along_row(): return lax.ppermute(x, 'row', [(i, i ^ k) for i in range(n_row)])]
    ppermute x5, starting transfers between devices: 10.6 us -> 9.07 us  [along_z(): return lax.ppermute(x, 'col', [(i, i ^ CORES * k) for i in range(n_col)])]
    ppermute x5, waiting for transfers between devices: 5.63 us -> 6.56 us  [along_z(): return lax.ppermute(x, 'col', [(i, i ^ CORES * k) for i in range(n_col)])]
  transfers between devices with their start and end apart: 29 -> 29, of which waited for: 12 -> 10; matrix products, arithmetic and copies ran while one was open for 1% -> 1% of each run, Pallas kernels for 20% -> 19%
where the time goes in v4:
time: 88.4 us; the launch traced here: 88.2 us
  waiting for transfers between devices  37.6 us (43%)
  starting transfers between devices  26.3 us (30%)
  Pallas kernels  20.3 us (23%)
  local copies, waits for them, and re-layouts  3.73 us (4%)
    ppermute x13, waiting for transfers between devices, along_row(): return lax.ppermute(x, 'row', [(i, i ^ k) for i in range(n_row)])  31 us
    ppermute x13, starting transfers between devices, along_row(): return lax.ppermute(x, 'row', [(i, i ^ k) for i in range(n_row)])  15.7 us
    pallas_call x3, Pallas kernels, add_targets(): pl.pallas_call(functools.partial(target_kernel, tubes, per_peer, tokens,...  11.2 us
    ppermute x5, starting transfers between devices, along_z(): return lax.ppermute(x, 'col', [(i, i ^ CORES * k) for i in range(n_col)])  9.07 us
    ppermute x5, waiting for transfers between devices, along_z(): return lax.ppermute(x, 'col', [(i, i ^ CORES * k) for i in range(n_col)])  6.56 us
    pallas_call x4, Pallas kernels, relate(): pl.pallas_call(functools.partial(relation_kernel, tokens, len(students),...  3.75 us
    unnamed x12, local copies, waits for them, and re-layouts  3.07 us
    pallas_call x1, Pallas kernels, project(): pl.pallas_call(project_kernel, out_shape=(jax.ShapeDtypeStruct((tokens, w...  2.54 us
  transfers between devices with their start and end apart: 29, of which 10 were waited for; matrix products, arithmetic and copies ran while one was open for 1% of the time, Pallas kernels for 19%

profile of v4, /device:TPU:0, one launch (start us, length us, event | category | flops | bytes accessed | tf_op | source)
XLA Modules:
  0.0 88.2 jit_solution(13945970561747886142)
XLA Ops:
  0.0 1.0 %shard_map.67.refs_0_ = bf16[88,768]{1,0:T(8,128)(2,1)S(1)} custom-call(s32[32]{0:T(128)} %bitcast.10, f32[64]{0:T(128)} %refs_1_.1, s32[24,128]{1,0:T(8,128)} %bitcast.9, bf16[80,768]{1,0:T(8,128)(2,1)} %refs_3_.1), custom_call_target="tpu_custom_call" | custom-call | tf_op jit(solution)/shard_map/pallas_call | solution.py:74
  1.0 3.1 %collective-permute-start.13 = (bf16[88,768]{1,0:T(8,128)(2,1)S(1)}, bf16[88,768]{1,0:T(8,128)(2,1)S(1)}, u32[]{:S(2)}, u32[]{:S(2)}) collective-permute-start(bf16[88,768]{1,0:T(8,128)(2,1)S(1)} %shard_map.67.refs_0_), channel_id=1, source_target_pairs={{0,2},{1,3},{2,0},{3,1},{4,6},{5,7},{6,4},{7,5},{8,10},{9,11},{10,... | collective-permute-start | bytes 405512 | tf_op jit(solution)/shard_map/ppermute | solution.py:373
  4.1 1.5 %collective-permute-start.20 = (bf16[88,768]{1,0:T(8,128)(2,1)S(1)}, bf16[88,768]{1,0:T(8,128)(2,1)S(1)}, u32[]{:S(2)}, u32[]{:S(2)}) collective-permute-start(bf16[88,768]{1,0:T(8,128)(2,1)S(1)} %shard_map.67.refs_0_), channel_id=1, source_target_pairs={{0,8},{8,0},{16,24},{24,16},{1,9},{9,1},{17,25},{25,17},{2,10},{10... | collective-permute-start | bytes 405512 | tf_op jit(solution)/shard_map/ppermute | solution.py:370
  5.6 2.6 %collective-permute-start.5 = (bf16[88,768]{1,0:T(8,128)(2,1)S(1)}, bf16[88,768]{1,0:T(8,128)(2,1)S(1)}, u32[]{:S(2)}, u32[]{:S(2)}) collective-permute-start(bf16[88,768]{1,0:T(8,128)(2,1)S(1)} %shard_map.67.refs_0_), channel_id=1, source_target_pairs={{0,4},{1,5},{2,6},{3,7},{4,0},{5,1},{6,2},{7,3},{8,12},{9,13},{10,... | collective-permute-start | bytes 405512 | tf_op jit(solution)/shard_map/ppermute | solution.py:373
  8.2 0.2 collective-permute-start.9
  8.4 1.5 %collective-permute-start.14 = (bf16[88,768]{1,0:T(8,128)(2,1)S(1)}, bf16[88,768]{1,0:T(8,128)(2,1)S(1)}, u32[]{:S(2)}, u32[]{:S(2)}) collective-permute-start(bf16[88,768]{1,0:T(8,128)(2,1)S(1)} %collective-permute-done.13.refs_0_), channel_id=1, source_target_pairs={{0,16},{8,24},{16,0},{24,8},{1,17},{9,25},{17,1},{25,9},{2,18},{10... | collective-permute-start | bytes 405512 | tf_op jit(solution)/shard_map/ppermute | solution.py:370
  10.0 0.8 collective-permute-start.22
  10.8 2.5 %shard_map.64 = (bf16[128,768]{1,0:T(8,128)(2,1)S(1)}, f32[128,768]{1,0:T(8,128)S(1)}, f32[128,128]{1,0:T(8,128)S(1)}) custom-call(bf16[128,1920]{1,0:T(8,128)(2,1)} %hidden_hbm.1, bf16[1920,768]{1,0:T(8,128)(2,1)} %projection_ref.1), custom_call_target="tpu_custom_call" | custom-call | tf_op jit(solution)/shard_map/pallas_call | solution.py:123
  13.3 4.8 %collective-permute-done.5.refs_0_ = bf16[88,768]{1,0:T(8,128)(2,1)S(1)} collective-permute-done((bf16[88,768]{1,0:T(8,128)(2,1)S(1)}, bf16[88,768]{1,0:T(8,128)(2,1)S(1)}, u32[]{:S(2)}, u32[]{:S(2)}) %collective-permute-start.5) | collective-permute-done | bytes 135200 | tf_op jit(solution)/shard_map/ppermute | solution.py:373
  18.1 1.1 %collective-permute-start.6 = (bf16[88,768]{1,0:T(8,128)(2,1)S(1)}, bf16[88,768]{1,0:T(8,128)(2,1)S(1)}, u32[]{:S(2)}, u32[]{:S(2)}) collective-permute-start(bf16[88,768]{1,0:T(8,128)(2,1)S(1)} %collective-permute-done.5.refs_0_), channel_id=1, source_target_pairs={{0,8},{8,0},{16,24},{24,16},{1,9},{9,1},{17,25},{25,17},{2,10},{10... | collective-permute-start | bytes 405512 | tf_op jit(solution)/shard_map/ppermute | solution.py:370
  19.2 1.5 %collective-permute-start.10 = (bf16[88,768]{1,0:T(8,128)(2,1)S(1)}, bf16[88,768]{1,0:T(8,128)(2,1)S(1)}, u32[]{:S(2)}, u32[]{:S(2)}) collective-permute-start(bf16[88,768]{1,0:T(8,128)(2,1)S(1)} %collective-permute-done.9.refs_0_), channel_id=1, source_target_pairs={{0,16},{8,24},{16,0},{24,8},{1,17},{9,25},{17,1},{25,9},{2,18},{10... | collective-permute-start | bytes 405512 | tf_op jit(solution)/shard_map/ppermute | solution.py:370
  20.8 2.9 %collective-permute-done.6.refs_1_ = bf16[88,768]{1,0:T(8,128)(2,1)S(1)} collective-permute-done((bf16[88,768]{1,0:T(8,128)(2,1)S(1)}, bf16[88,768]{1,0:T(8,128)(2,1)S(1)}, u32[]{:S(2)}, u32[]{:S(2)}) %collective-permute-start.6) | collective-permute-done | bytes 135200 | tf_op jit(solution)/shard_map/ppermute | solution.py:370
  23.6 1.9 %collective-permute-start.16 = (bf16[176,768]{1,0:T(8,128)(2,1)S(1)}, bf16[176,768]{1,0:T(8,128)(2,1)}, u32[]{:S(2)}, u32[]{:S(2)}) collective-permute-start(bf16[176,768]{1,0:T(8,128)(2,1)S(1)} %shard_map.70.refs_0_), channel_id=1, source_target_pairs={{0,8},{8,0},{16,24},{24,16},{1,9},{9,1},{17,25},{25,17},{2,10},{10... | collective-permute-start | bytes 811016 | tf_op jit(solution)/shard_map/ppermute | solution.py:370
  25.6 0.1 collective-permute-start.15
  25.7 0.2 collective-permute-start.11
  25.9 1.5 %collective-permute-start.7 = (bf16[176,768]{1,0:T(8,128)(2,1)S(1)}, bf16[176,768]{1,0:T(8,128)(2,1)S(1)}, u32[]{:S(2)}, u32[]{:S(2)}) collective-permute-start(bf16[176,768]{1,0:T(8,128)(2,1)S(1)} %shard_map.68.refs_4_), channel_id=1, source_target_pairs={{0,16},{8,24},{16,0},{24,8},{1,17},{9,25},{17,1},{25,9},{2,18},{10... | collective-permute-start | bytes 811016 | tf_op jit(solution)/shard_map/ppermute | solution.py:370
  27.4 0.2 collective-permute-start.23
  27.6 4.8 %collective-permute-done.16.refs_2_ = bf16[176,768]{1,0:T(8,128)(2,1)} collective-permute-done((bf16[176,768]{1,0:T(8,128)(2,1)S(1)}, bf16[176,768]{1,0:T(8,128)(2,1)}, u32[]{:S(2)}, u32[]{:S(2)}) %collective-permute-start.16) | collective-permute-done | bytes 270368 | tf_op jit(solution)/shard_map/ppermute | solution.py:370
  32.4 0.7 copy-done.3
  33.1 0.5 collective-permute-start.19
  33.6 2.3 %collective-permute-done.11.refs_2_ = bf16[176,768]{1,0:T(8,128)(2,1)S(1)} collective-permute-done((bf16[176,768]{1,0:T(8,128)(2,1)S(1)}, bf16[176,768]{1,0:T(8,128)(2,1)S(1)}, u32[]{:S(2)}, u32[]{:S(2)}) %collective-permute-start.11) | collective-permute-done | bytes 270368 | tf_op jit(solution)/shard_map/ppermute | solution.py:370
  35.9 0.5 collective-permute-start.12
  36.4 0.7 copy-done.1
  37.1 0.0 collective-permute-start.8
  37.1 0.7 stack.31.dests_ref
  37.8 1.0 %copy-done.2 = bf16[176,768]{1,0:T(8,128)(2,1)S(1)} copy-done((bf16[176,768]{1,0:T(8,128)(2,1)S(1)}, bf16[176,768]{1,0:T(8,128)(2,1)}, u32[]{:S(2)}) %copy-start.2) | copy-done | bytes 270360
  38.8 0.7 copy-done.5
  39.5 2.7 %shard_map.72.refs_8_ = f32[896,768]{1,0:T(8,128)S(1)} custom-call(s32[7]{0:T(128)S(1)} %copy-done.5, bf16[176,768]{1,0:T(8,128)(2,1)S(1)} %shard_map.71.refs_0_, bf16[176,768]{1,0:T(8,128)(2,1)S(1)} %collective-permute-done.21.refs_1_, bf16[176,768]{1,0:T(8,128)(2,1)S(1)} %collective-permute-done.22.refs_2_, bf16[176,768]{1,0:T(8,128)(2,1)S(1)} %copy-done.2), custom_call_target="tpu_custom_call" | custom-call | tf_op jit(solution)/shard_map/pallas_call | solution.py:228
  42.2 3.1 %collective-permute-start.2 = (bf16[256,768]{1,0:T(8,128)(2,1)S(1)}, bf16[256,768]{1,0:T(8,128)(2,1)S(1)}, u32[]{:S(2)}, u32[]{:S(2)}) collective-permute-start(bf16[256,768]{1,0:T(8,128)(2,1)S(1)} %shard_map.65.refs_0_), channel_id=1, source_target_pairs={{0,4},{1,5},{2,6},{3,7},{4,0},{5,1},{6,2},{7,3},{8,12},{9,13},{10,... | collective-permute-start | bytes 1179656 | tf_op jit(solution)/shard_map/ppermute | solution.py:373
  45.3 5.5 %shard_map.73.refs_4_ = f32[896,768]{1,0:T(8,128)S(1)} custom-call(s32[7]{0:T(128)S(1)} %copy-done.5, bf16[176,768]{1,0:T(8,128)(2,1)S(1)} %shard_map.70.refs_0_, bf16[176,768]{1,0:T(8,128)(2,1)S(1)} %copy-done.4, bf16[176,768]{1,0:T(8,128)(2,1)} %collective-permute-done.16.refs_2_, ...), custom_call_target="tpu_custom_call", output_to_operand_aliasing={{}: (9, {})} | custom-call | tf_op jit(solution)/shard_map/pallas_call | solution.py:228
  50.8 3.0 %shard_map.74 = (bf16[512,768]{1,0:T(8,128)(2,1)S(1)}, bf16[384,768]{1,0:T(8,128)(2,1)S(1)}) custom-call(s32[7]{0:T(128)S(1)} %copy-done.5, bf16[176,768]{1,0:T(8,128)(2,1)S(1)} %collective-permute-done.7.refs_0_, bf16[176,768]{1,0:T(8,128)(2,1)S(1)} %collective-permute-done.8.refs_1_, bf16[176,768]{1,0:T(8,128)(2,1)S(1)} %collective-permute-done.11.refs_2_, ...), custom_call_target="tpu_custom_call" | custom-call | tf_op jit(solution)/shard_map/pallas_call | solution.py:228
  53.8 0.3 collective-permute-start.24
  54.1 1.5 %collective-permute-start.4 = (bf16[128,768]{1,0:T(8,128)(2,1)S(1)}, bf16[128,768]{1,0:T(8,128)(2,1)S(1)}, u32[]{:S(2)}, u32[]{:S(2)}) collective-permute-start(bf16[128,768]{1,0:T(8,128)(2,1)S(1)} %get-tuple-element.16.refs_0_), channel_id=1, source_target_pairs={{0,16},{8,24},{16,0},{24,8},{1,17},{9,25},{17,1},{25,9},{2,18},{10... | collective-permute-start | bytes 589832 | tf_op jit(solution)/shard_map/ppermute | solution.py:370
  55.7 5.6 %collective-permute-done.4.refs_1_ = bf16[128,768]{1,0:T(8,128)(2,1)S(1)} collective-permute-done((bf16[128,768]{1,0:T(8,128)(2,1)S(1)}, bf16[128,768]{1,0:T(8,128)(2,1)S(1)}, u32[]{:S(2)}, u32[]{:S(2)}) %collective-permute-start.4) | collective-permute-done | bytes 196640 | tf_op jit(solution)/shard_map/ppermute | solution.py:370
  61.3 0.5 collective-permute-start.26
  61.8 1.8 %collective-permute-done.2.refs_1_ = bf16[256,768]{1,0:T(8,128)(2,1)S(1)} collective-permute-done((bf16[256,768]{1,0:T(8,128)(2,1)S(1)}, bf16[256,768]{1,0:T(8,128)(2,1)S(1)}, u32[]{:S(2)}, u32[]{:S(2)}) %collective-permute-start.2) | collective-permute-done | bytes 393248 | tf_op jit(solution)/shard_map/ppermute | solution.py:373
  63.5 0.9 %shard_map.75.refs_6_ = f32[256,768]{1,0:T(8,128)S(1)} custom-call(bf16[256,768]{1,0:T(8,128)(2,1)S(1)} %shard_map.65.refs_0_, bf16[256,768]{1,0:T(8,128)(2,1)S(1)} %collective-permute-done.2.refs_1_, bf16[256,768]{1,0:T(8,128)(2,1)S(1)} %shard_map.66.refs_2_, bf16[512,768]{1,0:T(8,128)(2,1)S(1)} %get-tuple-element.17.refs_3_.refs_4_, ...), custom_call_target="tpu_custom_call" | custom-call | tf_op jit(solution)/shard_map/pallas_call | solution.py:282
  64.5 7.3 %collective-permute-done.26.refs_2_ = bf16[256,768]{1,0:T(8,128)(2,1)S(1)} collective-permute-done((bf16[256,768]{1,0:T(8,128)(2,1)S(1)}, bf16[256,768]{1,0:T(8,128)(2,1)S(1)}, u32[]{:S(2)}, u32[]{:S(2)}) %collective-permute-start.26) | collective-permute-done | bytes 393248 | tf_op jit(solution)/shard_map/ppermute | solution.py:370
  71.8 0.9 %shard_map.77.refs_5_ = f32[256,768]{1,0:T(8,128)S(1)} custom-call(bf16[256,768]{1,0:T(8,128)(2,1)S(1)} %shard_map.65.refs_0_, bf16[256,768]{1,0:T(8,128)(2,1)S(1)} %collective-permute-done.2.refs_1_, bf16[256,768]{1,0:T(8,128)(2,1)S(1)} %collective-permute-done.26.refs_2_, bf16[512,768]{1,0:T(8,128)(2,1)S(1)} %get-tuple-element.17.refs_3_.refs_4_, ...), custom_call_target="tpu_custom_call" | custom-call | tf_op jit(solution)/shard_map/pallas_call | solution.py:282
  72.7 0.9 %shard_map.78 = (bf16[128,768]{1,0:T(8,128)(2,1)S(1)}, bf16[128,768]{1,0:T(8,128)(2,1)S(1)}) custom-call(bf16[256,768]{1,0:T(8,128)(2,1)S(1)} %collective-permute-done.1.refs_0_, bf16[256,768]{1,0:T(8,128)(2,1)S(1)} %collective-permute-done.3.refs_1_, bf16[256,768]{1,0:T(8,128)(2,1)S(1)} %collective-permute-done.26.refs_2_, ...), custom_call_target="tpu_custom_call" | custom-call | tf_op jit(solution)/shard_map/pallas_call | solution.py:282
  73.7 0.5 collective-permute-start.27
  74.2 2.6 %collective-permute-start.28 = (bf16[128,768]{1,0:T(8,128)(2,1)S(1)}, bf16[128,768]{1,0:T(8,128)(2,1)S(1)}, u32[]{:S(2)}, u32[]{:S(2)}) collective-permute-start(bf16[128,768]{1,0:T(8,128)(2,1)S(1)} %get-tuple-element.22), channel_id=1, source_target_pairs={{0,24},{8,16},{16,8},{24,0},{1,25},{9,17},{17,9},{25,1},{2,26},{10... | collective-permute-start | bytes 589832 | tf_op jit(solution)/shard_map/ppermute | solution.py:370
  76.7 0.9 %shard_map.76 = (f32[128,768]{1,0:T(8,128)S(1)}, bf16[128,768]{1,0:T(8,128)(2,1)S(1)}) custom-call(bf16[256,768]{1,0:T(8,128)(2,1)S(1)} %collective-permute-done.1.refs_0_, bf16[256,768]{1,0:T(8,128)(2,1)S(1)} %collective-permute-done.3.refs_1_, bf16[256,768]{1,0:T(8,128)(2,1)S(1)} %shard_map.66.refs_2_, ...), custom_call_target="tpu_custom_call" | custom-call | tf_op jit(solution)/shard_map/pallas_call | solution.py:282
  77.7 0.6 collective-permute-start.25
  78.3 3.0 %collective-permute-done.27.refs_1_ = bf16[128,768]{1,0:T(8,128)(2,1)S(1)} collective-permute-done((bf16[128,768]{1,0:T(8,128)(2,1)S(1)}, bf16[128,768]{1,0:T(8,128)(2,1)S(1)}, u32[]{:S(2)}, u32[]{:S(2)}) %collective-permute-start.27) | collective-permute-done | bytes 196640 | tf_op jit(solution)/shard_map/ppermute | solution.py:370
  81.2 3.2 %collective-permute-done.28.refs_2_ = bf16[128,768]{1,0:T(8,128)(2,1)S(1)} collective-permute-done((bf16[128,768]{1,0:T(8,128)(2,1)S(1)}, bf16[128,768]{1,0:T(8,128)(2,1)S(1)}, u32[]{:S(2)}, u32[]{:S(2)}) %collective-permute-start.28) | collective-permute-done | bytes 196640 | tf_op jit(solution)/shard_map/ppermute | solution.py:370
  84.4 2.0 %collective-permute-done.25.refs_0_ = bf16[128,768]{1,0:T(8,128)(2,1)S(1)} collective-permute-done((bf16[128,768]{1,0:T(8,128)(2,1)S(1)}, bf16[128,768]{1,0:T(8,128)(2,1)S(1)}, u32[]{:S(2)}, u32[]{:S(2)}) %collective-permute-start.25) | collective-permute-done | bytes 196640 | tf_op jit(solution)/shard_map/ppermute | solution.py:370
  86.5 1.8 %shard_map.79 = bf16[128,1920]{1,0:T(8,128)(2,1)} custom-call(f32[128,768]{1,0:T(8,128)S(1)} %get-tuple-element.14.unit_ref, f32[128,128]{1,0:T(8,128)S(1)} %get-tuple-element.15.inverse_ref, bf16[1920,768]{1,0:T(8,128)(2,1)S(1)} %copy-done, f32[128,768]{1,0:T(8,128)S(1)} %get-tuple-element.19.own_ref, bf16[128,768]{1,0:T(8,128)(2,1)S(1)} %collective-permute-done.25.refs_0_, ...), custom_call_target="tpu_custom_call" | custom-call | tf_op jit(solution)/shard_map/pallas_call | solution.py:324
  (39 shorter events, 0.2 us)
Async XLA Ops:
  1.0 7.4 %collective-permute-start.13 = (bf16[88,768]{1,0:T(8,128)(2,1)S(1)}, bf16[88,768]{1,0:T(8,128)(2,1)S(1)}, u32[]{:S(2)}, u32[]{:S(2)}) collective-permute-start(bf16[88,768]{1,0:T(8,128)(2,1)S(1)} %shard_map.67.refs_0_), channel_id=1, source_target_pairs={{0,2},{1,3},{2,0},{3,1},{4,6},{5,7},{6,4},{7,5},{8,10},{9,11},{10,... | collective-permute-start | bytes 405512 | tf_op jit(solution)/shard_map/ppermute | solution.py:373
  4.1 5.8 %collective-permute-start.20 = (bf16[88,768]{1,0:T(8,128)(2,1)S(1)}, bf16[88,768]{1,0:T(8,128)(2,1)S(1)}, u32[]{:S(2)}, u32[]{:S(2)}) collective-permute-start(bf16[88,768]{1,0:T(8,128)(2,1)S(1)} %shard_map.67.refs_0_), channel_id=1, source_target_pairs={{0,8},{8,0},{16,24},{24,16},{1,9},{9,1},{17,25},{25,17},{2,10},{10... | collective-permute-start | bytes 405512 | tf_op jit(solution)/shard_map/ppermute | solution.py:370
  5.6 12.5 %collective-permute-start.5 = (bf16[88,768]{1,0:T(8,128)(2,1)S(1)}, bf16[88,768]{1,0:T(8,128)(2,1)S(1)}, u32[]{:S(2)}, u32[]{:S(2)}) collective-permute-start(bf16[88,768]{1,0:T(8,128)(2,1)S(1)} %shard_map.67.refs_0_), channel_id=1, source_target_pairs={{0,4},{1,5},{2,6},{3,7},{4,0},{5,1},{6,2},{7,3},{8,12},{9,13},{10,... | collective-permute-start | bytes 405512 | tf_op jit(solution)/shard_map/ppermute | solution.py:373
  8.2 9.9 %collective-permute-start.9 = (bf16[88,768]{1,0:T(8,128)(2,1)S(1)}, bf16[88,768]{1,0:T(8,128)(2,1)S(1)}, u32[]{:S(2)}, u32[]{:S(2)}) collective-permute-start(bf16[88,768]{1,0:T(8,128)(2,1)S(1)} %shard_map.67.refs_0_), channel_id=1, source_target_pairs={{0,6},{1,7},{2,4},{3,5},{4,2},{5,3},{6,0},{7,1},{8,14},{9,15},{10,... | collective-permute-start | bytes 405512 | tf_op jit(solution)/shard_map/ppermute | solution.py:373
  8.4 10.8 %collective-permute-start.14 = (bf16[88,768]{1,0:T(8,128)(2,1)S(1)}, bf16[88,768]{1,0:T(8,128)(2,1)S(1)}, u32[]{:S(2)}, u32[]{:S(2)}) collective-permute-start(bf16[88,768]{1,0:T(8,128)(2,1)S(1)} %collective-permute-done.13.refs_0_), channel_id=1, source_target_pairs={{0,16},{8,24},{16,0},{24,8},{1,17},{9,25},{17,1},{25,9},{2,18},{10... | collective-permute-start | bytes 405512 | tf_op jit(solution)/shard_map/ppermute | solution.py:370
  10.0 15.9 %collective-permute-start.22 = (bf16[176,768]{1,0:T(8,128)(2,1)S(1)}, bf16[176,768]{1,0:T(8,128)(2,1)S(1)}, u32[]{:S(2)}, u32[]{:S(2)}) collective-permute-start(bf16[176,768]{1,0:T(8,128)(2,1)S(1)} %shard_map.71.refs_0_), channel_id=1, source_target_pairs={{0,16},{8,24},{16,0},{24,8},{1,17},{9,25},{17,1},{25,9},{2,18},{10... | collective-permute-start | bytes 811016 | tf_op jit(solution)/shard_map/ppermute | solution.py:370
  10.8 16.6 %collective-permute-start.21 = (bf16[176,768]{1,0:T(8,128)(2,1)S(1)}, bf16[176,768]{1,0:T(8,128)(2,1)S(1)}, u32[]{:S(2)}, u32[]{:S(2)}) collective-permute-start(bf16[176,768]{1,0:T(8,128)(2,1)S(1)} %shard_map.71.refs_0_), channel_id=1, source_target_pairs={{0,1},{1,0},{2,3},{3,2},{4,5},{5,4},{6,7},{7,6},{8,9},{9,8},{10,11... | collective-permute-start | bytes 811016 | tf_op jit(solution)/shard_map/ppermute | solution.py:376
  18.1 7.6 %collective-permute-start = (bf16[128,768]{1,0:T(8,128)(2,1)S(1)}, bf16[128,768]{1,0:T(8,128)(2,1)S(1)}, u32[]{:S(2)}, u32[]{:S(2)}) collective-permute-start(bf16[128,768]{1,0:T(8,128)(2,1)S(1)} %get-tuple-element.16.refs_0_), channel_id=1, source_target_pairs={{0,2},{1,3},{2,0},{3,1},{4,6},{5,7},{6,4},{7,5},{8,10},{9,11},{10,... | collective-permute-start | bytes 589832 | tf_op jit(solution)/shard_map/ppermute | solution.py:373
  18.1 5.5 %collective-permute-start.6 = (bf16[88,768]{1,0:T(8,128)(2,1)S(1)}, bf16[88,768]{1,0:T(8,128)(2,1)S(1)}, u32[]{:S(2)}, u32[]{:S(2)}) collective-permute-start(bf16[88,768]{1,0:T(8,128)(2,1)S(1)} %collective-permute-done.5.refs_0_), channel_id=1, source_target_pairs={{0,8},{8,0},{16,24},{24,16},{1,9},{9,1},{17,25},{25,17},{2,10},{10... | collective-permute-start | bytes 405512 | tf_op jit(solution)/shard_map/ppermute | solution.py:370
  19.2 6.4 %collective-permute-start.10 = (bf16[88,768]{1,0:T(8,128)(2,1)S(1)}, bf16[88,768]{1,0:T(8,128)(2,1)S(1)}, u32[]{:S(2)}, u32[]{:S(2)}) collective-permute-start(bf16[88,768]{1,0:T(8,128)(2,1)S(1)} %collective-permute-done.9.refs_0_), channel_id=1, source_target_pairs={{0,16},{8,24},{16,0},{24,8},{1,17},{9,25},{17,1},{25,9},{2,18},{10... | collective-permute-start | bytes 405512 | tf_op jit(solution)/shard_map/ppermute | solution.py:370
  23.6 8.8 %collective-permute-start.16 = (bf16[176,768]{1,0:T(8,128)(2,1)S(1)}, bf16[176,768]{1,0:T(8,128)(2,1)}, u32[]{:S(2)}, u32[]{:S(2)}) collective-permute-start(bf16[176,768]{1,0:T(8,128)(2,1)S(1)} %shard_map.70.refs_0_), channel_id=1, source_target_pairs={{0,8},{8,0},{16,24},{24,16},{1,9},{9,1},{17,25},{25,17},{2,10},{10... | collective-permute-start | bytes 811016 | tf_op jit(solution)/shard_map/ppermute | solution.py:370
  25.6 6.8 %collective-permute-start.15 = (bf16[176,768]{1,0:T(8,128)(2,1)S(1)}, bf16[176,768]{1,0:T(8,128)(2,1)S(1)}, u32[]{:S(2)}, u32[]{:S(2)}) collective-permute-start(bf16[176,768]{1,0:T(8,128)(2,1)S(1)} %shard_map.70.refs_0_), channel_id=1, source_target_pairs={{0,1},{1,0},{2,3},{3,2},{4,5},{5,4},{6,7},{7,6},{8,9},{9,8},{10,11... | collective-permute-start | bytes 811016 | tf_op jit(solution)/shard_map/ppermute | solution.py:376
  25.7 10.2 %collective-permute-start.11 = (bf16[176,768]{1,0:T(8,128)(2,1)S(1)}, bf16[176,768]{1,0:T(8,128)(2,1)S(1)}, u32[]{:S(2)}, u32[]{:S(2)}) collective-permute-start(bf16[176,768]{1,0:T(8,128)(2,1)S(1)} %shard_map.69.refs_6_), channel_id=1, source_target_pairs={{0,8},{8,0},{16,24},{24,16},{1,9},{9,1},{17,25},{25,17},{2,10},{10... | collective-permute-start | bytes 811016 | tf_op jit(solution)/shard_map/ppermute | solution.py:370
  25.9 10.0 %collective-permute-start.7 = (bf16[176,768]{1,0:T(8,128)(2,1)S(1)}, bf16[176,768]{1,0:T(8,128)(2,1)S(1)}, u32[]{:S(2)}, u32[]{:S(2)}) collective-permute-start(bf16[176,768]{1,0:T(8,128)(2,1)S(1)} %shard_map.68.refs_4_), channel_id=1, source_target_pairs={{0,16},{8,24},{16,0},{24,8},{1,17},{9,25},{17,1},{25,9},{2,18},{10... | collective-permute-start | bytes 811016 | tf_op jit(solution)/shard_map/ppermute | solution.py:370
  27.4 9.0 %collective-permute-start.23 = (bf16[176,768]{1,0:T(8,128)(2,1)S(1)}, bf16[176,768]{1,0:T(8,128)(2,1)S(1)}, u32[]{:S(2)}, u32[]{:S(2)}) collective-permute-start(bf16[176,768]{1,0:T(8,128)(2,1)S(1)} %collective-permute-done.22.refs_2_), channel_id=1, source_target_pairs={{0,1},{1,0},{2,3},{3,2},{4,5},{5,4},{6,7},{7,6},{8,9},{9,8},{10,11... | collective-permute-start | bytes 811016 | tf_op jit(solution)/shard_map/ppermute | solution.py:376
  32.4 9.8 %collective-permute-start.18 = (bf16[176,768]{1,0:T(8,128)(2,1)S(1)}, bf16[176,768]{1,0:T(8,128)(2,1)}, u32[]{:S(2)}, u32[]{:S(2)}) collective-permute-start(bf16[176,768]{1,0:T(8,128)(2,1)S(1)} %shard_map.68.refs_4_), channel_id=1, source_target_pairs={{0,1},{1,0},{2,3},{3,2},{4,5},{5,4},{6,7},{7,6},{8,9},{9,8},{10,11... | collective-permute-start | bytes 811016 | tf_op jit(solution)/shard_map/ppermute | solution.py:376
  32.4 0.7 copy-start.3
  33.1 12.2 %collective-permute-start.19 = (bf16[176,768]{1,0:T(8,128)(2,1)S(1)}, bf16[176,768]{1,0:T(8,128)(2,1)}, u32[]{:S(2)}, u32[]{:S(2)}) collective-permute-start(bf16[176,768]{1,0:T(8,128)(2,1)S(1)} %shard_map.69.refs_6_), channel_id=1, source_target_pairs={{0,1},{1,0},{2,3},{3,2},{4,5},{5,4},{6,7},{7,6},{8,9},{9,8},{10,11... | collective-permute-start | bytes 811016 | tf_op jit(solution)/shard_map/ppermute | solution.py:376
  35.9 9.4 %collective-permute-start.17 = (bf16[176,768]{1,0:T(8,128)(2,1)}, bf16[176,768]{1,0:T(8,128)(2,1)}, u32[]{:S(2)}, u32[]{:S(2)}) collective-permute-start(bf16[176,768]{1,0:T(8,128)(2,1)} %collective-permute-done.16.refs_2_), channel_id=1, source_target_pairs={{0,1},{1,0},{2,3},{3,2},{4,5},{5,4},{6,7},{7,6},{8,9},{9,8},{10,11... | collective-permute-start | bytes 811016 | tf_op jit(solution)/shard_map/ppermute | solution.py:376
  35.9 14.9 %collective-permute-start.12 = (bf16[176,768]{1,0:T(8,128)(2,1)S(1)}, bf16[176,768]{1,0:T(8,128)(2,1)S(1)}, u32[]{:S(2)}, u32[]{:S(2)}) collective-permute-start(bf16[176,768]{1,0:T(8,128)(2,1)S(1)} %collective-permute-done.11.refs_2_), channel_id=1, source_target_pairs={{0,1},{1,0},{2,3},{3,2},{4,5},{5,4},{6,7},{7,6},{8,9},{9,8},{10,11... | collective-permute-start | bytes 811016 | tf_op jit(solution)/shard_map/ppermute | solution.py:376
  36.4 0.7 copy-start.1
  37.1 13.7 %collective-permute-start.8 = (bf16[176,768]{1,0:T(8,128)(2,1)S(1)}, bf16[176,768]{1,0:T(8,128)(2,1)S(1)}, u32[]{:S(2)}, u32[]{:S(2)}) collective-permute-start(bf16[176,768]{1,0:T(8,128)(2,1)S(1)} %collective-permute-done.7.refs_0_), channel_id=1, source_target_pairs={{0,1},{1,0},{2,3},{3,2},{4,5},{5,4},{6,7},{7,6},{8,9},{9,8},{10,11... | collective-permute-start | bytes 811016 | tf_op jit(solution)/shard_map/ppermute | solution.py:376
  37.8 7.5 %copy-start.4 = (bf16[176,768]{1,0:T(8,128)(2,1)S(1)}, bf16[176,768]{1,0:T(8,128)(2,1)}, u32[]{:S(2)}) copy-start(bf16[176,768]{1,0:T(8,128)(2,1)} %copy-done.3) | copy-start | bytes 811012
  37.8 1.0 %copy-start.2 = (bf16[176,768]{1,0:T(8,128)(2,1)S(1)}, bf16[176,768]{1,0:T(8,128)(2,1)}, u32[]{:S(2)}) copy-start(bf16[176,768]{1,0:T(8,128)(2,1)} %copy-done.1) | copy-start | bytes 811012
  38.8 0.7 copy-start.5
  42.2 21.4 %collective-permute-start.2 = (bf16[256,768]{1,0:T(8,128)(2,1)S(1)}, bf16[256,768]{1,0:T(8,128)(2,1)S(1)}, u32[]{:S(2)}, u32[]{:S(2)}) collective-permute-start(bf16[256,768]{1,0:T(8,128)(2,1)S(1)} %shard_map.65.refs_0_), channel_id=1, source_target_pairs={{0,4},{1,5},{2,6},{3,7},{4,0},{5,1},{6,2},{7,3},{8,12},{9,13},{10,... | collective-permute-start | bytes 1179656 | tf_op jit(solution)/shard_map/ppermute | solution.py:373
  53.8 18.9 %collective-permute-start.24 = (bf16[512,768]{1,0:T(8,128)(2,1)S(1)}, bf16[512,768]{1,0:T(8,128)(2,1)S(1)}, u32[]{:S(2)}, u32[]{:S(2)}) collective-permute-start(bf16[512,768]{1,0:T(8,128)(2,1)S(1)} %get-tuple-element.17.refs_3_.refs_4_), channel_id=1, source_target_pairs={{0,1},{1,0},{2,3},{3,2},{4,5},{5,4},{6,7},{7,6},{8,9},{9,8},{10,11... | collective-permute-start | bytes 2359304 | tf_op jit(solution)/shard_map/ppermute | solution.py:376
  54.1 7.1 %collective-permute-start.4 = (bf16[128,768]{1,0:T(8,128)(2,1)S(1)}, bf16[128,768]{1,0:T(8,128)(2,1)S(1)}, u32[]{:S(2)}, u32[]{:S(2)}) collective-permute-start(bf16[128,768]{1,0:T(8,128)(2,1)S(1)} %get-tuple-element.16.refs_0_), channel_id=1, source_target_pairs={{0,16},{8,24},{16,0},{24,8},{1,17},{9,25},{17,1},{25,9},{2,18},{10... | collective-permute-start | bytes 589832 | tf_op jit(solution)/shard_map/ppermute | solution.py:370
  61.3 10.5 %collective-permute-start.26 = (bf16[256,768]{1,0:T(8,128)(2,1)S(1)}, bf16[256,768]{1,0:T(8,128)(2,1)S(1)}, u32[]{:S(2)}, u32[]{:S(2)}) collective-permute-start(bf16[256,768]{1,0:T(8,128)(2,1)S(1)} %shard_map.66.refs_2_), channel_id=1, source_target_pairs={{0,8},{8,0},{16,24},{24,16},{1,9},{9,1},{17,25},{25,17},{2,10},{10... | collective-permute-start | bytes 1179656 | tf_op jit(solution)/shard_map/ppermute | solution.py:370
  61.8 11.0 %collective-permute-start.1 = (bf16[256,768]{1,0:T(8,128)(2,1)S(1)}, bf16[256,768]{1,0:T(8,128)(2,1)S(1)}, u32[]{:S(2)}, u32[]{:S(2)}) collective-permute-start(bf16[256,768]{1,0:T(8,128)(2,1)S(1)} %shard_map.65.refs_0_), channel_id=1, source_target_pairs={{0,1},{1,0},{2,3},{3,2},{4,5},{5,4},{6,7},{7,6},{8,9},{9,8},{10,11... | collective-permute-start | bytes 1179656 | tf_op jit(solution)/shard_map/ppermute | solution.py:376
  63.5 9.2 %collective-permute-start.3 = (bf16[256,768]{1,0:T(8,128)(2,1)S(1)}, bf16[256,768]{1,0:T(8,128)(2,1)S(1)}, u32[]{:S(2)}, u32[]{:S(2)}) collective-permute-start(bf16[256,768]{1,0:T(8,128)(2,1)S(1)} %collective-permute-done.2.refs_1_), channel_id=1, source_target_pairs={{0,1},{1,0},{2,3},{3,2},{4,5},{5,4},{6,7},{7,6},{8,9},{9,8},{10,11... | collective-permute-start | bytes 1179656 | tf_op jit(solution)/shard_map/ppermute | solution.py:376
  73.7 12.8 %copy-start = (bf16[1920,768]{1,0:T(8,128)(2,1)S(1)}, bf16[1920,768]{1,0:T(8,128)(2,1)}, u32[]{:S(2)}) copy-start(bf16[1920,768]{1,0:T(8,128)(2,1)} %projection_ref.1) | copy-start | bytes 8847364
  73.7 7.5 %collective-permute-start.27 = (bf16[128,768]{1,0:T(8,128)(2,1)S(1)}, bf16[128,768]{1,0:T(8,128)(2,1)S(1)}, u32[]{:S(2)}, u32[]{:S(2)}) collective-permute-start(bf16[128,768]{1,0:T(8,128)(2,1)S(1)} %get-tuple-element.21), channel_id=1, source_target_pairs={{0,8},{8,0},{16,24},{24,16},{1,9},{9,1},{17,25},{25,17},{2,10},{10... | collective-permute-start | bytes 589832 | tf_op jit(solution)/shard_map/ppermute | solution.py:370
  74.2 10.2 %collective-permute-start.28 = (bf16[128,768]{1,0:T(8,128)(2,1)S(1)}, bf16[128,768]{1,0:T(8,128)(2,1)S(1)}, u32[]{:S(2)}, u32[]{:S(2)}) collective-permute-start(bf16[128,768]{1,0:T(8,128)(2,1)S(1)} %get-tuple-element.22), channel_id=1, source_target_pairs={{0,24},{8,16},{16,8},{24,0},{1,25},{9,17},{17,9},{25,1},{2,26},{10... | collective-permute-start | bytes 589832 | tf_op jit(solution)/shard_map/ppermute | solution.py:370
  77.7 8.8 %collective-permute-start.25 = (bf16[128,768]{1,0:T(8,128)(2,1)S(1)}, bf16[128,768]{1,0:T(8,128)(2,1)S(1)}, u32[]{:S(2)}, u32[]{:S(2)}) collective-permute-start(bf16[128,768]{1,0:T(8,128)(2,1)S(1)} %get-tuple-element.20), channel_id=1, source_target_pairs={{0,16},{8,24},{16,0},{24,8},{1,17},{9,25},{17,1},{25,9},{2,18},{10... | collective-permute-start | bytes 589832 | tf_op jit(solution)/shard_map/ppermute | solution.py:370

commit v5 on v4

--- a/solution.py
+++ b/solution.py
@@ -11,7 +11,7 @@
 norm_eps = 1e-06
 CORES = 2
 LANES = 128
-PARTS = 3
+PARTS = 5
 REVERSED = (1, 3)
 F32 = jnp.float32
 BF16 = jnp.bfloat16
@@ -305,10 +305,9 @@
     copies = []
     for i in range(PARTS):
         span = pl.ds(i * part, part)
-        out[:, i * part : (i + 1) * part] = lax.dot_general(
+        out[:, i * part : (i + 1) * part] = jnp.dot(
             grad_proj,
-            projection_ref[i * part : (i + 1) * part, :],
-            NT,
+            projection_ref[:, i * part : (i + 1) * part],
             preferred_element_type=F32,
         ).astype(BF16)
         copies.append(
@@ -320,7 +319,7 @@
 
 
 def finish(unit, inverse, projection, own, others):
-    shape = (unit.shape[0], projection.shape[0])
+    shape = (unit.shape[0], projection.shape[1])
     return pl.pallas_call(
         finish_kernel,
         out_shape=jax.ShapeDtypeStruct(shape, BF16),
@@ -329,6 +328,20 @@
         scratch_shapes=[pltpu.VMEM(shape, BF16), pltpu.SemaphoreType.DMA((PARTS,))],
         compiler_params=params(16),
     )(unit, inverse, projection, own, *others)
+
+
+def turn_kernel(in_ref, out_ref):
+    out_ref[...] = in_ref[...].T
+
+
+def turn(x):
+    return pl.pallas_call(
+        turn_kernel,
+        out_shape=jax.ShapeDtypeStruct(x.shape[::-1], x.dtype),
+        in_specs=[VMEM],
+        out_specs=VMEM,
+        compiler_params=params(16),
+    )(x)
 
 
 def join_kernel(*refs):
@@ -422,7 +435,8 @@
     for i, (c, t, kinds) in enumerate(sides):
         blocks += relate(tokens, partner_students, c, partner, t, sums[i], kinds)
     arrived = [along_row(x, j) for j, x in zip(offsets[1:], blocks[1:])]
-    return finish(unit, inverse, projection, blocks[0], arrived)
+    turned = turn(projection)
+    return finish(unit, inverse, turned, blocks[0], arrived)
 
 
 def solution(mesh):

time: 88.4 us -> 88.2 us (level)
  transfers between devices with their start and end apart: 29 -> 29, of which waited for: 10 -> 10; matrix products, arithmetic and copies ran while one was open for 1% -> 1% of each run, Pallas kernels for 19% -> 20%
where the time goes in v5:
time: 88.2 us; the launch traced here: 88 us
  waiting for transfers between devices  36.8 us (42%)
  starting transfers between devices  26.3 us (30%)
  Pallas kernels  20.9 us (24%)
  local copies, waits for them, and re-layouts  3.73 us (4%)
    ppermute x13, waiting for transfers between devices, along_row(): return lax.ppermute(x, 'row', [(i, i ^ k) for i in range(n_row)])  30.2 us
    ppermute x13, starting transfers between devices, along_row(): return lax.ppermute(x, 'row', [(i, i ^ k) for i in range(n_row)])  15.7 us
    pallas_call x3, Pallas kernels, add_targets(): pl.pallas_call(functools.partial(target_kernel, tubes, per_peer, tokens,...  11.2 us
    ppermute x5, starting transfers between devices, along_z(): return lax.ppermute(x, 'col', [(i, i ^ CORES * k) for i in range(n_col)])  9.07 us
    ppermute x5, waiting for transfers between devices, along_z(): return lax.ppermute(x, 'col', [(i, i ^ CORES * k) for i in range(n_col)])  6.58 us
    pallas_call x4, Pallas kernels, relate(): pl.pallas_call(functools.partial(relation_kernel, tokens, len(students),...  3.75 us
    unnamed x12, local copies, waits for them, and re-layouts  3.07 us
    pallas_call x1, Pallas kernels, project(): pl.pallas_call(project_kernel, out_shape=(jax.ShapeDtypeStruct((tokens, w...  2.52 us
  transfers between devices with their start and end apart: 29, of which 10 were waited for; matrix products, arithmetic and copies ran while one was open for 1% of the time, Pallas kernels for 20%

profile of v5, /device:TPU:0, one launch (start us, length us, event | category | flops | bytes accessed | tf_op | source)
XLA Modules:
  0.0 88.0 jit_solution(15371811142458226769)
XLA Ops:
  0.0 1.0 %shard_map.68.refs_0_ = bf16[88,768]{1,0:T(8,128)(2,1)S(1)} custom-call(s32[32]{0:T(128)} %bitcast.10, f32[64]{0:T(128)} %refs_1_.1, s32[24,128]{1,0:T(8,128)} %bitcast.9, bf16[80,768]{1,0:T(8,128)(2,1)} %refs_3_.1), custom_call_target="tpu_custom_call" | custom-call | tf_op jit(solution)/shard_map/pallas_call | solution.py:74
  1.0 3.1 %collective-permute-start.13 = (bf16[88,768]{1,0:T(8,128)(2,1)S(1)}, bf16[88,768]{1,0:T(8,128)(2,1)S(1)}, u32[]{:S(2)}, u32[]{:S(2)}) collective-permute-start(bf16[88,768]{1,0:T(8,128)(2,1)S(1)} %shard_map.68.refs_0_), channel_id=1, source_target_pairs={{0,2},{1,3},{2,0},{3,1},{4,6},{5,7},{6,4},{7,5},{8,10},{9,11},{10,... | collective-permute-start | bytes 405512 | tf_op jit(solution)/shard_map/ppermute | solution.py:386
  4.1 1.5 %collective-permute-start.20 = (bf16[88,768]{1,0:T(8,128)(2,1)S(1)}, bf16[88,768]{1,0:T(8,128)(2,1)S(1)}, u32[]{:S(2)}, u32[]{:S(2)}) collective-permute-start(bf16[88,768]{1,0:T(8,128)(2,1)S(1)} %shard_map.68.refs_0_), channel_id=1, source_target_pairs={{0,8},{8,0},{16,24},{24,16},{1,9},{9,1},{17,25},{25,17},{2,10},{10... | collective-permute-start | bytes 405512 | tf_op jit(solution)/shard_map/ppermute | solution.py:383
  5.6 2.6 %collective-permute-start.5 = (bf16[88,768]{1,0:T(8,128)(2,1)S(1)}, bf16[88,768]{1,0:T(8,128)(2,1)S(1)}, u32[]{:S(2)}, u32[]{:S(2)}) collective-permute-start(bf16[88,768]{1,0:T(8,128)(2,1)S(1)} %shard_map.68.refs_0_), channel_id=1, source_target_pairs={{0,4},{1,5},{2,6},{3,7},{4,0},{5,1},{6,2},{7,3},{8,12},{9,13},{10,... | collective-permute-start | bytes 405512 | tf_op jit(solution)/shard_map/ppermute | solution.py:386
  8.2 0.2 collective-permute-start.9
  8.4 1.5 %collective-permute-start.14 = (bf16[88,768]{1,0:T(8,128)(2,1)S(1)}, bf16[88,768]{1,0:T(8,128)(2,1)S(1)}, u32[]{:S(2)}, u32[]{:S(2)}) collective-permute-start(bf16[88,768]{1,0:T(8,128)(2,1)S(1)} %collective-permute-done.13.refs_0_), channel_id=1, source_target_pairs={{0,16},{8,24},{16,0},{24,8},{1,17},{9,25},{17,1},{25,9},{2,18},{10... | collective-permute-start | bytes 405512 | tf_op jit(solution)/shard_map/ppermute | solution.py:383
  10.0 0.8 collective-permute-start.22
  10.8 2.5 %shard_map.64 = (bf16[128,768]{1,0:T(8,128)(2,1)S(1)}, f32[128,768]{1,0:T(8,128)S(1)}, f32[128,128]{1,0:T(8,128)S(1)}) custom-call(bf16[128,1920]{1,0:T(8,128)(2,1)} %hidden_hbm.1, bf16[1920,768]{1,0:T(8,128)(2,1)} %in_ref.1), custom_call_target="tpu_custom_call" | custom-call | tf_op jit(solution)/shard_map/pallas_call | solution.py:123
  13.3 4.8 %collective-permute-done.5.refs_0_ = bf16[88,768]{1,0:T(8,128)(2,1)S(1)} collective-permute-done((bf16[88,768]{1,0:T(8,128)(2,1)S(1)}, bf16[88,768]{1,0:T(8,128)(2,1)S(1)}, u32[]{:S(2)}, u32[]{:S(2)}) %collective-permute-start.5) | collective-permute-done | bytes 135200 | tf_op jit(solution)/shard_map/ppermute | solution.py:386
  18.1 1.1 %collective-permute-start.6 = (bf16[88,768]{1,0:T(8,128)(2,1)S(1)}, bf16[88,768]{1,0:T(8,128)(2,1)S(1)}, u32[]{:S(2)}, u32[]{:S(2)}) collective-permute-start(bf16[88,768]{1,0:T(8,128)(2,1)S(1)} %collective-permute-done.5.refs_0_), channel_id=1, source_target_pairs={{0,8},{8,0},{16,24},{24,16},{1,9},{9,1},{17,25},{25,17},{2,10},{10... | collective-permute-start | bytes 405512 | tf_op jit(solution)/shard_map/ppermute | solution.py:383
  19.2 1.5 %collective-permute-start.10 = (bf16[88,768]{1,0:T(8,128)(2,1)S(1)}, bf16[88,768]{1,0:T(8,128)(2,1)S(1)}, u32[]{:S(2)}, u32[]{:S(2)}) collective-permute-start(bf16[88,768]{1,0:T(8,128)(2,1)S(1)} %collective-permute-done.9.refs_0_), channel_id=1, source_target_pairs={{0,16},{8,24},{16,0},{24,8},{1,17},{9,25},{17,1},{25,9},{2,18},{10... | collective-permute-start | bytes 405512 | tf_op jit(solution)/shard_map/ppermute | solution.py:383
  20.8 2.9 %collective-permute-done.6.refs_1_ = bf16[88,768]{1,0:T(8,128)(2,1)S(1)} collective-permute-done((bf16[88,768]{1,0:T(8,128)(2,1)S(1)}, bf16[88,768]{1,0:T(8,128)(2,1)S(1)}, u32[]{:S(2)}, u32[]{:S(2)}) %collective-permute-start.6) | collective-permute-done | bytes 135200 | tf_op jit(solution)/shard_map/ppermute | solution.py:383
  23.6 1.9 %collective-permute-start.16 = (bf16[176,768]{1,0:T(8,128)(2,1)S(1)}, bf16[176,768]{1,0:T(8,128)(2,1)}, u32[]{:S(2)}, u32[]{:S(2)}) collective-permute-start(bf16[176,768]{1,0:T(8,128)(2,1)S(1)} %shard_map.71.refs_0_), channel_id=1, source_target_pairs={{0,8},{8,0},{16,24},{24,16},{1,9},{9,1},{17,25},{25,17},{2,10},{10... | collective-permute-start | bytes 811016 | tf_op jit(solution)/shard_map/ppermute | solution.py:383
  25.6 0.1 collective-permute-start.15
  25.7 0.2 collective-permute-start.11
  25.9 1.5 %collective-permute-start.7 = (bf16[176,768]{1,0:T(8,128)(2,1)S(1)}, bf16[176,768]{1,0:T(8,128)(2,1)S(1)}, u32[]{:S(2)}, u32[]{:S(2)}) collective-permute-start(bf16[176,768]{1,0:T(8,128)(2,1)S(1)} %shard_map.69.refs_4_), channel_id=1, source_target_pairs={{0,16},{8,24},{16,0},{24,8},{1,17},{9,25},{17,1},{25,9},{2,18},{10... | collective-permute-start | bytes 811016 | tf_op jit(solution)/shard_map/ppermute | solution.py:383
  27.4 0.2 collective-permute-start.23
  27.6 4.8 %collective-permute-done.16.refs_2_ = bf16[176,768]{1,0:T(8,128)(2,1)} collective-permute-done((bf16[176,768]{1,0:T(8,128)(2,1)S(1)}, bf16[176,768]{1,0:T(8,128)(2,1)}, u32[]{:S(2)}, u32[]{:S(2)}) %collective-permute-start.16) | collective-permute-done | bytes 270368 | tf_op jit(solution)/shard_map/ppermute | solution.py:383
  32.4 0.7 copy-done.3
  33.1 0.5 collective-permute-start.19
  33.6 2.3 %collective-permute-done.11.refs_2_ = bf16[176,768]{1,0:T(8,128)(2,1)S(1)} collective-permute-done((bf16[176,768]{1,0:T(8,128)(2,1)S(1)}, bf16[176,768]{1,0:T(8,128)(2,1)S(1)}, u32[]{:S(2)}, u32[]{:S(2)}) %collective-permute-start.11) | collective-permute-done | bytes 270368 | tf_op jit(solution)/shard_map/ppermute | solution.py:383
  35.9 0.5 collective-permute-start.12
  36.4 0.7 copy-done.1
  37.1 0.7 stack.31.dests_ref
  37.8 1.0 %copy-done.2 = bf16[176,768]{1,0:T(8,128)(2,1)S(1)} copy-done((bf16[176,768]{1,0:T(8,128)(2,1)S(1)}, bf16[176,768]{1,0:T(8,128)(2,1)}, u32[]{:S(2)}) %copy-start.2) | copy-done | bytes 270360
  38.8 0.7 copy-done.5
  39.5 2.7 %shard_map.73.refs_8_ = f32[896,768]{1,0:T(8,128)S(1)} custom-call(s32[7]{0:T(128)S(1)} %copy-done.5, bf16[176,768]{1,0:T(8,128)(2,1)S(1)} %shard_map.72.refs_0_, bf16[176,768]{1,0:T(8,128)(2,1)S(1)} %collective-permute-done.21.refs_1_, bf16[176,768]{1,0:T(8,128)(2,1)S(1)} %collective-permute-done.22.refs_2_, bf16[176,768]{1,0:T(8,128)(2,1)S(1)} %copy-done.2), custom_call_target="tpu_custom_call" | custom-call | tf_op jit(solution)/shard_map/pallas_call | solution.py:228
  42.2 3.1 %collective-permute-start.2 = (bf16[256,768]{1,0:T(8,128)(2,1)S(1)}, bf16[256,768]{1,0:T(8,128)(2,1)S(1)}, u32[]{:S(2)}, u32[]{:S(2)}) collective-permute-start(bf16[256,768]{1,0:T(8,128)(2,1)S(1)} %shard_map.66.refs_0_), channel_id=1, source_target_pairs={{0,4},{1,5},{2,6},{3,7},{4,0},{5,1},{6,2},{7,3},{8,12},{9,13},{10,... | collective-permute-start | bytes 1179656 | tf_op jit(solution)/shard_map/ppermute | solution.py:386
  45.3 5.5 %shard_map.74.refs_4_ = f32[896,768]{1,0:T(8,128)S(1)} custom-call(s32[7]{0:T(128)S(1)} %copy-done.5, bf16[176,768]{1,0:T(8,128)(2,1)S(1)} %shard_map.71.refs_0_, bf16[176,768]{1,0:T(8,128)(2,1)S(1)} %copy-done.4, bf16[176,768]{1,0:T(8,128)(2,1)} %collective-permute-done.16.refs_2_, ...), custom_call_target="tpu_custom_call", output_to_operand_aliasing={{}: (9, {})} | custom-call | tf_op jit(solution)/shard_map/pallas_call | solution.py:228
  50.8 3.0 %shard_map.75 = (bf16[512,768]{1,0:T(8,128)(2,1)S(1)}, bf16[384,768]{1,0:T(8,128)(2,1)S(1)}) custom-call(s32[7]{0:T(128)S(1)} %copy-done.5, bf16[176,768]{1,0:T(8,128)(2,1)S(1)} %collective-permute-done.7.refs_0_, bf16[176,768]{1,0:T(8,128)(2,1)S(1)} %collective-permute-done.8.refs_1_, bf16[176,768]{1,0:T(8,128)(2,1)S(1)} %collective-permute-done.11.refs_2_, ...), custom_call_target="tpu_custom_call" | custom-call | tf_op jit(solution)/shard_map/pallas_call | solution.py:228
  53.8 0.3 collective-permute-start.24
  54.1 1.5 %collective-permute-start.4 = (bf16[128,768]{1,0:T(8,128)(2,1)S(1)}, bf16[128,768]{1,0:T(8,128)(2,1)S(1)}, u32[]{:S(2)}, u32[]{:S(2)}) collective-permute-start(bf16[128,768]{1,0:T(8,128)(2,1)S(1)} %get-tuple-element.16.refs_0_), channel_id=1, source_target_pairs={{0,16},{8,24},{16,0},{24,8},{1,17},{9,25},{17,1},{25,9},{2,18},{10... | collective-permute-start | bytes 589832 | tf_op jit(solution)/shard_map/ppermute | solution.py:383
  55.7 5.6 %collective-permute-done.4.refs_1_ = bf16[128,768]{1,0:T(8,128)(2,1)S(1)} collective-permute-done((bf16[128,768]{1,0:T(8,128)(2,1)S(1)}, bf16[128,768]{1,0:T(8,128)(2,1)S(1)}, u32[]{:S(2)}, u32[]{:S(2)}) %collective-permute-start.4) | collective-permute-done | bytes 196640 | tf_op jit(solution)/shard_map/ppermute | solution.py:383
  61.3 0.5 collective-permute-start.26
  61.8 1.8 %collective-permute-done.2.refs_1_ = bf16[256,768]{1,0:T(8,128)(2,1)S(1)} collective-permute-done((bf16[256,768]{1,0:T(8,128)(2,1)S(1)}, bf16[256,768]{1,0:T(8,128)(2,1)S(1)}, u32[]{:S(2)}, u32[]{:S(2)}) %collective-permute-start.2) | collective-permute-done | bytes 393248 | tf_op jit(solution)/shard_map/ppermute | solution.py:386
  63.5 0.9 %shard_map.76.refs_6_ = f32[256,768]{1,0:T(8,128)S(1)} custom-call(bf16[256,768]{1,0:T(8,128)(2,1)S(1)} %shard_map.66.refs_0_, bf16[256,768]{1,0:T(8,128)(2,1)S(1)} %collective-permute-done.2.refs_1_, bf16[256,768]{1,0:T(8,128)(2,1)S(1)} %shard_map.67.refs_2_, bf16[512,768]{1,0:T(8,128)(2,1)S(1)} %get-tuple-element.17.refs_3_.refs_4_, ...), custom_call_target="tpu_custom_call" | custom-call | tf_op jit(solution)/shard_map/pallas_call | solution.py:282
  64.5 7.3 %collective-permute-done.26.refs_2_ = bf16[256,768]{1,0:T(8,128)(2,1)S(1)} collective-permute-done((bf16[256,768]{1,0:T(8,128)(2,1)S(1)}, bf16[256,768]{1,0:T(8,128)(2,1)S(1)}, u32[]{:S(2)}, u32[]{:S(2)}) %collective-permute-start.26) | collective-permute-done | bytes 393248 | tf_op jit(solution)/shard_map/ppermute | solution.py:383
  71.8 0.9 %shard_map.78.refs_5_ = f32[256,768]{1,0:T(8,128)S(1)} custom-call(bf16[256,768]{1,0:T(8,128)(2,1)S(1)} %shard_map.66.refs_0_, bf16[256,768]{1,0:T(8,128)(2,1)S(1)} %collective-permute-done.2.refs_1_, bf16[256,768]{1,0:T(8,128)(2,1)S(1)} %collective-permute-done.26.refs_2_, bf16[512,768]{1,0:T(8,128)(2,1)S(1)} %get-tuple-element.17.refs_3_.refs_4_, ...), custom_call_target="tpu_custom_call" | custom-call | tf_op jit(solution)/shard_map/pallas_call | solution.py:282
  72.8 0.9 %shard_map.79 = (bf16[128,768]{1,0:T(8,128)(2,1)S(1)}, bf16[128,768]{1,0:T(8,128)(2,1)S(1)}) custom-call(bf16[256,768]{1,0:T(8,128)(2,1)S(1)} %collective-permute-done.1.refs_0_, bf16[256,768]{1,0:T(8,128)(2,1)S(1)} %collective-permute-done.3.refs_1_, bf16[256,768]{1,0:T(8,128)(2,1)S(1)} %collective-permute-done.26.refs_2_, ...), custom_call_target="tpu_custom_call" | custom-call | tf_op jit(solution)/shard_map/pallas_call | solution.py:282
  73.7 0.5 collective-permute-start.27
  74.2 2.6 %collective-permute-start.28 = (bf16[128,768]{1,0:T(8,128)(2,1)S(1)}, bf16[128,768]{1,0:T(8,128)(2,1)S(1)}, u32[]{:S(2)}, u32[]{:S(2)}) collective-permute-start(bf16[128,768]{1,0:T(8,128)(2,1)S(1)} %get-tuple-element.22), channel_id=1, source_target_pairs={{0,24},{8,16},{16,8},{24,0},{1,25},{9,17},{17,9},{25,1},{2,26},{10... | collective-permute-start | bytes 589832 | tf_op jit(solution)/shard_map/ppermute | solution.py:383
  76.7 0.9 %shard_map.77 = (f32[128,768]{1,0:T(8,128)S(1)}, bf16[128,768]{1,0:T(8,128)(2,1)S(1)}) custom-call(bf16[256,768]{1,0:T(8,128)(2,1)S(1)} %collective-permute-done.1.refs_0_, bf16[256,768]{1,0:T(8,128)(2,1)S(1)} %collective-permute-done.3.refs_1_, bf16[256,768]{1,0:T(8,128)(2,1)S(1)} %shard_map.67.refs_2_, ...), custom_call_target="tpu_custom_call" | custom-call | tf_op jit(solution)/shard_map/pallas_call | solution.py:282
  77.7 0.6 collective-permute-start.25
  78.3 0.8 shard_map.65.projection_ref
  79.1 2.2 %collective-permute-done.27.refs_1_ = bf16[128,768]{1,0:T(8,128)(2,1)S(1)} collective-permute-done((bf16[128,768]{1,0:T(8,128)(2,1)S(1)}, bf16[128,768]{1,0:T(8,128)(2,1)S(1)}, u32[]{:S(2)}, u32[]{:S(2)}) %collective-permute-start.27) | collective-permute-done | bytes 196640 | tf_op jit(solution)/shard_map/ppermute | solution.py:383
  81.2 3.2 %collective-permute-done.28.refs_2_ = bf16[128,768]{1,0:T(8,128)(2,1)S(1)} collective-permute-done((bf16[128,768]{1,0:T(8,128)(2,1)S(1)}, bf16[128,768]{1,0:T(8,128)(2,1)S(1)}, u32[]{:S(2)}, u32[]{:S(2)}) %collective-permute-start.28) | collective-permute-done | bytes 196640 | tf_op jit(solution)/shard_map/ppermute | solution.py:383
  84.4 2.0 %collective-permute-done.25.refs_0_ = bf16[128,768]{1,0:T(8,128)(2,1)S(1)} collective-permute-done((bf16[128,768]{1,0:T(8,128)(2,1)S(1)}, bf16[128,768]{1,0:T(8,128)(2,1)S(1)}, u32[]{:S(2)}, u32[]{:S(2)}) %collective-permute-start.25) | collective-permute-done | bytes 196640 | tf_op jit(solution)/shard_map/ppermute | solution.py:383
  86.4 1.6 %shard_map.80 = bf16[128,1920]{1,0:T(8,128)(2,1)} custom-call(f32[128,768]{1,0:T(8,128)S(1)} %get-tuple-element.14.unit_ref, f32[128,128]{1,0:T(8,128)S(1)} %get-tuple-element.15.inverse_ref, bf16[768,1920]{1,0:T(8,128)(2,1)S(1)} %shard_map.65.projection_ref, f32[128,768]{1,0:T(8,128)S(1)} %get-tuple-element.19.own_ref, ...), custom_call_target="tpu_custom_call" | custom-call | tf_op jit(solution)/shard_map/pallas_call | solution.py:323
  (40 shorter events, 0.2 us)
Async XLA Ops:
  1.0 7.4 %collective-permute-start.13 = (bf16[88,768]{1,0:T(8,128)(2,1)S(1)}, bf16[88,768]{1,0:T(8,128)(2,1)S(1)}, u32[]{:S(2)}, u32[]{:S(2)}) collective-permute-start(bf16[88,768]{1,0:T(8,128)(2,1)S(1)} %shard_map.68.refs_0_), channel_id=1, source_target_pairs={{0,2},{1,3},{2,0},{3,1},{4,6},{5,7},{6,4},{7,5},{8,10},{9,11},{10,... | collective-permute-start | bytes 405512 | tf_op jit(solution)/shard_map/ppermute | solution.py:386
  4.1 5.8 %collective-permute-start.20 = (bf16[88,768]{1,0:T(8,128)(2,1)S(1)}, bf16[88,768]{1,0:T(8,128)(2,1)S(1)}, u32[]{:S(2)}, u32[]{:S(2)}) collective-permute-start(bf16[88,768]{1,0:T(8,128)(2,1)S(1)} %shard_map.68.refs_0_), channel_id=1, source_target_pairs={{0,8},{8,0},{16,24},{24,16},{1,9},{9,1},{17,25},{25,17},{2,10},{10... | collective-permute-start | bytes 405512 | tf_op jit(solution)/shard_map/ppermute | solution.py:383
  5.6 12.5 %collective-permute-start.5 = (bf16[88,768]{1,0:T(8,128)(2,1)S(1)}, bf16[88,768]{1,0:T(8,128)(2,1)S(1)}, u32[]{:S(2)}, u32[]{:S(2)}) collective-permute-start(bf16[88,768]{1,0:T(8,128)(2,1)S(1)} %shard_map.68.refs_0_), channel_id=1, source_target_pairs={{0,4},{1,5},{2,6},{3,7},{4,0},{5,1},{6,2},{7,3},{8,12},{9,13},{10,... | collective-permute-start | bytes 405512 | tf_op jit(solution)/shard_map/ppermute | solution.py:386
  8.2 9.9 %collective-permute-start.9 = (bf16[88,768]{1,0:T(8,128)(2,1)S(1)}, bf16[88,768]{1,0:T(8,128)(2,1)S(1)}, u32[]{:S(2)}, u32[]{:S(2)}) collective-permute-start(bf16[88,768]{1,0:T(8,128)(2,1)S(1)} %shard_map.68.refs_0_), channel_id=1, source_target_pairs={{0,6},{1,7},{2,4},{3,5},{4,2},{5,3},{6,0},{7,1},{8,14},{9,15},{10,... | collective-permute-start | bytes 405512 | tf_op jit(solution)/shard_map/ppermute | solution.py:386
  8.4 10.8 %collective-permute-start.14 = (bf16[88,768]{1,0:T(8,128)(2,1)S(1)}, bf16[88,768]{1,0:T(8,128)(2,1)S(1)}, u32[]{:S(2)}, u32[]{:S(2)}) collective-permute-start(bf16[88,768]{1,0:T(8,128)(2,1)S(1)} %collective-permute-done.13.refs_0_), channel_id=1, source_target_pairs={{0,16},{8,24},{16,0},{24,8},{1,17},{9,25},{17,1},{25,9},{2,18},{10... | collective-permute-start | bytes 405512 | tf_op jit(solution)/shard_map/ppermute | solution.py:383
  10.0 15.9 %collective-permute-start.22 = (bf16[176,768]{1,0:T(8,128)(2,1)S(1)}, bf16[176,768]{1,0:T(8,128)(2,1)S(1)}, u32[]{:S(2)}, u32[]{:S(2)}) collective-permute-start(bf16[176,768]{1,0:T(8,128)(2,1)S(1)} %shard_map.72.refs_0_), channel_id=1, source_target_pairs={{0,16},{8,24},{16,0},{24,8},{1,17},{9,25},{17,1},{25,9},{2,18},{10... | collective-permute-start | bytes 811016 | tf_op jit(solution)/shard_map/ppermute | solution.py:383
  10.8 16.6 %collective-permute-start.21 = (bf16[176,768]{1,0:T(8,128)(2,1)S(1)}, bf16[176,768]{1,0:T(8,128)(2,1)S(1)}, u32[]{:S(2)}, u32[]{:S(2)}) collective-permute-start(bf16[176,768]{1,0:T(8,128)(2,1)S(1)} %shard_map.72.refs_0_), channel_id=1, source_target_pairs={{0,1},{1,0},{2,3},{3,2},{4,5},{5,4},{6,7},{7,6},{8,9},{9,8},{10,11... | collective-permute-start | bytes 811016 | tf_op jit(solution)/shard_map/ppermute | solution.py:389
  18.1 7.6 %collective-permute-start = (bf16[128,768]{1,0:T(8,128)(2,1)S(1)}, bf16[128,768]{1,0:T(8,128)(2,1)S(1)}, u32[]{:S(2)}, u32[]{:S(2)}) collective-permute-start(bf16[128,768]{1,0:T(8,128)(2,1)S(1)} %get-tuple-element.16.refs_0_), channel_id=1, source_target_pairs={{0,2},{1,3},{2,0},{3,1},{4,6},{5,7},{6,4},{7,5},{8,10},{9,11},{10,... | collective-permute-start | bytes 589832 | tf_op jit(solution)/shard_map/ppermute | solution.py:386
  18.1 5.5 %collective-permute-start.6 = (bf16[88,768]{1,0:T(8,128)(2,1)S(1)}, bf16[88,768]{1,0:T(8,128)(2,1)S(1)}, u32[]{:S(2)}, u32[]{:S(2)}) collective-permute-start(bf16[88,768]{1,0:T(8,128)(2,1)S(1)} %collective-permute-done.5.refs_0_), channel_id=1, source_target_pairs={{0,8},{8,0},{16,24},{24,16},{1,9},{9,1},{17,25},{25,17},{2,10},{10... | collective-permute-start | bytes 405512 | tf_op jit(solution)/shard_map/ppermute | solution.py:383
  19.2 6.4 %collective-permute-start.10 = (bf16[88,768]{1,0:T(8,128)(2,1)S(1)}, bf16[88,768]{1,0:T(8,128)(2,1)S(1)}, u32[]{:S(2)}, u32[]{:S(2)}) collective-permute-start(bf16[88,768]{1,0:T(8,128)(2,1)S(1)} %collective-permute-done.9.refs_0_), channel_id=1, source_target_pairs={{0,16},{8,24},{16,0},{24,8},{1,17},{9,25},{17,1},{25,9},{2,18},{10... | collective-permute-start | bytes 405512 | tf_op jit(solution)/shard_map/ppermute | solution.py:383
  23.6 8.7 %collective-permute-start.16 = (bf16[176,768]{1,0:T(8,128)(2,1)S(1)}, bf16[176,768]{1,0:T(8,128)(2,1)}, u32[]{:S(2)}, u32[]{:S(2)}) collective-permute-start(bf16[176,768]{1,0:T(8,128)(2,1)S(1)} %shard_map.71.refs_0_), channel_id=1, source_target_pairs={{0,8},{8,0},{16,24},{24,16},{1,9},{9,1},{17,25},{25,17},{2,10},{10... | collective-permute-start | bytes 811016 | tf_op jit(solution)/shard_map/ppermute | solution.py:383
  25.6 6.8 %collective-permute-start.15 = (bf16[176,768]{1,0:T(8,128)(2,1)S(1)}, bf16[176,768]{1,0:T(8,128)(2,1)S(1)}, u32[]{:S(2)}, u32[]{:S(2)}) collective-permute-start(bf16[176,768]{1,0:T(8,128)(2,1)S(1)} %shard_map.71.refs_0_), channel_id=1, source_target_pairs={{0,1},{1,0},{2,3},{3,2},{4,5},{5,4},{6,7},{7,6},{8,9},{9,8},{10,11... | collective-permute-start | bytes 811016 | tf_op jit(solution)/shard_map/ppermute | solution.py:389
  25.7 10.2 %collective-permute-start.11 = (bf16[176,768]{1,0:T(8,128)(2,1)S(1)}, bf16[176,768]{1,0:T(8,128)(2,1)S(1)}, u32[]{:S(2)}, u32[]{:S(2)}) collective-permute-start(bf16[176,768]{1,0:T(8,128)(2,1)S(1)} %shard_map.70.refs_6_), channel_id=1, source_target_pairs={{0,8},{8,0},{16,24},{24,16},{1,9},{9,1},{17,25},{25,17},{2,10},{10... | collective-permute-start | bytes 811016 | tf_op jit(solution)/shard_map/ppermute | solution.py:383
  25.9 10.0 %collective-permute-start.7 = (bf16[176,768]{1,0:T(8,128)(2,1)S(1)}, bf16[176,768]{1,0:T(8,128)(2,1)S(1)}, u32[]{:S(2)}, u32[]{:S(2)}) collective-permute-start(bf16[176,768]{1,0:T(8,128)(2,1)S(1)} %shard_map.69.refs_4_), channel_id=1, source_target_pairs={{0,16},{8,24},{16,0},{24,8},{1,17},{9,25},{17,1},{25,9},{2,18},{10... | collective-permute-start | bytes 811016 | tf_op jit(solution)/shard_map/ppermute | solution.py:383
  27.4 9.0 %collective-permute-start.23 = (bf16[176,768]{1,0:T(8,128)(2,1)S(1)}, bf16[176,768]{1,0:T(8,128)(2,1)S(1)}, u32[]{:S(2)}, u32[]{:S(2)}) collective-permute-start(bf16[176,768]{1,0:T(8,128)(2,1)S(1)} %collective-permute-done.22.refs_2_), channel_id=1, source_target_pairs={{0,1},{1,0},{2,3},{3,2},{4,5},{5,4},{6,7},{7,6},{8,9},{9,8},{10,11... | collective-permute-start | bytes 811016 | tf_op jit(solution)/shard_map/ppermute | solution.py:389
  32.4 9.8 %collective-permute-start.18 = (bf16[176,768]{1,0:T(8,128)(2,1)S(1)}, bf16[176,768]{1,0:T(8,128)(2,1)}, u32[]{:S(2)}, u32[]{:S(2)}) collective-permute-start(bf16[176,768]{1,0:T(8,128)(2,1)S(1)} %shard_map.69.refs_4_), channel_id=1, source_target_pairs={{0,1},{1,0},{2,3},{3,2},{4,5},{5,4},{6,7},{7,6},{8,9},{9,8},{10,11... | collective-permute-start | bytes 811016 | tf_op jit(solution)/shard_map/ppermute | solution.py:389
  32.4 0.7 copy-start.3
  33.1 12.2 %collective-permute-start.19 = (bf16[176,768]{1,0:T(8,128)(2,1)S(1)}, bf16[176,768]{1,0:T(8,128)(2,1)}, u32[]{:S(2)}, u32[]{:S(2)}) collective-permute-start(bf16[176,768]{1,0:T(8,128)(2,1)S(1)} %shard_map.70.refs_6_), channel_id=1, source_target_pairs={{0,1},{1,0},{2,3},{3,2},{4,5},{5,4},{6,7},{7,6},{8,9},{9,8},{10,11... | collective-permute-start | bytes 811016 | tf_op jit(solution)/shard_map/ppermute | solution.py:389
  35.9 9.4 %collective-permute-start.17 = (bf16[176,768]{1,0:T(8,128)(2,1)}, bf16[176,768]{1,0:T(8,128)(2,1)}, u32[]{:S(2)}, u32[]{:S(2)}) collective-permute-start(bf16[176,768]{1,0:T(8,128)(2,1)} %collective-permute-done.16.refs_2_), channel_id=1, source_target_pairs={{0,1},{1,0},{2,3},{3,2},{4,5},{5,4},{6,7},{7,6},{8,9},{9,8},{10,11... | collective-permute-start | bytes 811016 | tf_op jit(solution)/shard_map/ppermute | solution.py:389
  35.9 14.9 %collective-permute-start.12 = (bf16[176,768]{1,0:T(8,128)(2,1)S(1)}, bf16[176,768]{1,0:T(8,128)(2,1)S(1)}, u32[]{:S(2)}, u32[]{:S(2)}) collective-permute-start(bf16[176,768]{1,0:T(8,128)(2,1)S(1)} %collective-permute-done.11.refs_2_), channel_id=1, source_target_pairs={{0,1},{1,0},{2,3},{3,2},{4,5},{5,4},{6,7},{7,6},{8,9},{9,8},{10,11... | collective-permute-start | bytes 811016 | tf_op jit(solution)/shard_map/ppermute | solution.py:389
  36.4 0.7 copy-start.1
  37.1 13.7 %collective-permute-start.8 = (bf16[176,768]{1,0:T(8,128)(2,1)S(1)}, bf16[176,768]{1,0:T(8,128)(2,1)S(1)}, u32[]{:S(2)}, u32[]{:S(2)}) collective-permute-start(bf16[176,768]{1,0:T(8,128)(2,1)S(1)} %collective-permute-done.7.refs_0_), channel_id=1, source_target_pairs={{0,1},{1,0},{2,3},{3,2},{4,5},{5,4},{6,7},{7,6},{8,9},{9,8},{10,11... | collective-permute-start | bytes 811016 | tf_op jit(solution)/shard_map/ppermute | solution.py:389
  37.8 7.5 %copy-start.4 = (bf16[176,768]{1,0:T(8,128)(2,1)S(1)}, bf16[176,768]{1,0:T(8,128)(2,1)}, u32[]{:S(2)}) copy-start(bf16[176,768]{1,0:T(8,128)(2,1)} %copy-done.3) | copy-start | bytes 811012
  37.8 1.0 %copy-start.2 = (bf16[176,768]{1,0:T(8,128)(2,1)S(1)}, bf16[176,768]{1,0:T(8,128)(2,1)}, u32[]{:S(2)}) copy-start(bf16[176,768]{1,0:T(8,128)(2,1)} %copy-done.1) | copy-start | bytes 811012
  38.8 0.7 copy-start.5
  42.2 21.4 %collective-permute-start.2 = (bf16[256,768]{1,0:T(8,128)(2,1)S(1)}, bf16[256,768]{1,0:T(8,128)(2,1)S(1)}, u32[]{:S(2)}, u32[]{:S(2)}) collective-permute-start(bf16[256,768]{1,0:T(8,128)(2,1)S(1)} %shard_map.66.refs_0_), channel_id=1, source_target_pairs={{0,4},{1,5},{2,6},{3,7},{4,0},{5,1},{6,2},{7,3},{8,12},{9,13},{10,... | collective-permute-start | bytes 1179656 | tf_op jit(solution)/shard_map/ppermute | solution.py:386
  53.8 18.9 %collective-permute-start.24 = (bf16[512,768]{1,0:T(8,128)(2,1)S(1)}, bf16[512,768]{1,0:T(8,128)(2,1)S(1)}, u32[]{:S(2)}, u32[]{:S(2)}) collective-permute-start(bf16[512,768]{1,0:T(8,128)(2,1)S(1)} %get-tuple-element.17.refs_3_.refs_4_), channel_id=1, source_target_pairs={{0,1},{1,0},{2,3},{3,2},{4,5},{5,4},{6,7},{7,6},{8,9},{9,8},{10,11... | collective-permute-start | bytes 2359304 | tf_op jit(solution)/shard_map/ppermute | solution.py:389
  54.1 7.1 %collective-permute-start.4 = (bf16[128,768]{1,0:T(8,128)(2,1)S(1)}, bf16[128,768]{1,0:T(8,128)(2,1)S(1)}, u32[]{:S(2)}, u32[]{:S(2)}) collective-permute-start(bf16[128,768]{1,0:T(8,128)(2,1)S(1)} %get-tuple-element.16.refs_0_), channel_id=1, source_target_pairs={{0,16},{8,24},{16,0},{24,8},{1,17},{9,25},{17,1},{25,9},{2,18},{10... | collective-permute-start | bytes 589832 | tf_op jit(solution)/shard_map/ppermute | solution.py:383
  61.3 10.5 %collective-permute-start.26 = (bf16[256,768]{1,0:T(8,128)(2,1)S(1)}, bf16[256,768]{1,0:T(8,128)(2,1)S(1)}, u32[]{:S(2)}, u32[]{:S(2)}) collective-permute-start(bf16[256,768]{1,0:T(8,128)(2,1)S(1)} %shard_map.67.refs_2_), channel_id=1, source_target_pairs={{0,8},{8,0},{16,24},{24,16},{1,9},{9,1},{17,25},{25,17},{2,10},{10... | collective-permute-start | bytes 1179656 | tf_op jit(solution)/shard_map/ppermute | solution.py:383
  61.8 11.0 %collective-permute-start.1 = (bf16[256,768]{1,0:T(8,128)(2,1)S(1)}, bf16[256,768]{1,0:T(8,128)(2,1)S(1)}, u32[]{:S(2)}, u32[]{:S(2)}) collective-permute-start(bf16[256,768]{1,0:T(8,128)(2,1)S(1)} %shard_map.66.refs_0_), channel_id=1, source_target_pairs={{0,1},{1,0},{2,3},{3,2},{4,5},{5,4},{6,7},{7,6},{8,9},{9,8},{10,11... | collective-permute-start | bytes 1179656 | tf_op jit(solution)/shard_map/ppermute | solution.py:389
  63.5 9.2 %collective-permute-start.3 = (bf16[256,768]{1,0:T(8,128)(2,1)S(1)}, bf16[256,768]{1,0:T(8,128)(2,1)S(1)}, u32[]{:S(2)}, u32[]{:S(2)}) collective-permute-start(bf16[256,768]{1,0:T(8,128)(2,1)S(1)} %collective-permute-done.2.refs_1_), channel_id=1, source_target_pairs={{0,1},{1,0},{2,3},{3,2},{4,5},{5,4},{6,7},{7,6},{8,9},{9,8},{10,11... | collective-permute-start | bytes 1179656 | tf_op jit(solution)/shard_map/ppermute | solution.py:389
  72.7 5.6 %copy-start = (bf16[1920,768]{1,0:T(8,128)(2,1)S(1)}, bf16[1920,768]{1,0:T(8,128)(2,1)}, u32[]{:S(2)}) copy-start(bf16[1920,768]{1,0:T(8,128)(2,1)} %in_ref.1) | copy-start | bytes 8847364
  73.7 7.5 %collective-permute-start.27 = (bf16[128,768]{1,0:T(8,128)(2,1)S(1)}, bf16[128,768]{1,0:T(8,128)(2,1)S(1)}, u32[]{:S(2)}, u32[]{:S(2)}) collective-permute-start(bf16[128,768]{1,0:T(8,128)(2,1)S(1)} %get-tuple-element.21), channel_id=1, source_target_pairs={{0,8},{8,0},{16,24},{24,16},{1,9},{9,1},{17,25},{25,17},{2,10},{10... | collective-permute-start | bytes 589832 | tf_op jit(solution)/shard_map/ppermute | solution.py:383
  74.2 10.2 %collective-permute-start.28 = (bf16[128,768]{1,0:T(8,128)(2,1)S(1)}, bf16[128,768]{1,0:T(8,128)(2,1)S(1)}, u32[]{:S(2)}, u32[]{:S(2)}) collective-permute-start(bf16[128,768]{1,0:T(8,128)(2,1)S(1)} %get-tuple-element.22), channel_id=1, source_target_pairs={{0,24},{8,16},{16,8},{24,0},{1,25},{9,17},{17,9},{25,1},{2,26},{10... | collective-permute-start | bytes 589832 | tf_op jit(solution)/shard_map/ppermute | solution.py:383
  77.7 8.8 %collective-permute-start.25 = (bf16[128,768]{1,0:T(8,128)(2,1)S(1)}, bf16[128,768]{1,0:T(8,128)(2,1)S(1)}, u32[]{:S(2)}, u32[]{:S(2)}) collective-permute-start(bf16[128,768]{1,0:T(8,128)(2,1)S(1)} %get-tuple-element.20), channel_id=1, source_target_pairs={{0,16},{8,24},{16,0},{24,8},{1,17},{9,25},{17,1},{25,9},{2,18},{10... | collective-permute-start | bytes 589832 | tf_op jit(solution)/shard_map/ppermute | solution.py:383
